TPU v7x, 32 devices: a whole 2x2x4 slice. The times are simulated.
32 devices in a mesh: rows: 8 (over z, y), grp: 4 (over x, core).
Axes of the slice: x: 2, y: 2, z: 4, core: 2. Of those that a mesh axis runs over, the one named last changes fastest.
Arguments:
- a_vals: bfloat16 [2048, 16384], P(('rows', 'grp')), may hold values from -0.75 to 0.75
- a_cols: int32 [2048, 4], P(('rows', 'grp')), may hold values from 0 to 2047, as said below
- p_vals: bfloat16 [2048, 16384], P(('rows', 'grp')), may hold values from -0.25 to 0.25
- new_rows: int32 [2048], P(('rows', 'grp')), may hold values from 0 to 7, as said below
Outputs:
- a_moved: bfloat16 [2048, 16384], P(('rows', 'grp'))
- coarse: bfloat16 [2048, 768], P(('rows', 'grp'))
Inputs may be any that keep to these rules, and one draw needn't show every extreme that they name: `a_cols`: the first entry of row i is i itself; every entry names a block row whose slab is slab(i) - 1, slab(i) or slab(i) + 1, with any grp index. `new_rows`: the rows of one device go to each rows index either none or exactly 16 at a time, and for each grp index every rows index receives exactly 64 rows.
All inputs are finite; a program needn't handle non-finite values.
Results may differ from a plain program's by a relative error of at most 0.005.
Values may be sent and summed in bfloat16 or wider, within the bound.
No kernel may reach another device: no remote copies, remote signals or barrier semaphores. Data moves between devices by JAX's collectives and lax.ppermute only.
A program may use at most 192 MiB of HBM per device.

v0:
```python
import jax
import jax.numpy as jnp
from jax import lax
from jax.sharding import PartitionSpec as P

B = 64


def extended(block, sides, width):
    for axis, dim in sides:
        count = lax.axis_size(axis)
        forward = [(i, i + 1) for i in range(count - 1)]
        backward = [(target, source) for source, target in forward]
        low = lax.ppermute(
            lax.slice_in_dim(block, block.shape[dim] - width, None, axis=dim), axis, forward
        )
        high = lax.ppermute(lax.slice_in_dim(block, 0, width, axis=dim), axis, backward)
        block = jnp.concatenate([low, block, high], axis=dim)
    return block


def select_rows(picker, source):
    return jnp.dot(picker, source, preferred_element_type=jnp.float32).astype(jnp.bfloat16)


def migrate(a_vals, new_rows):
    row_count, row_width = a_vals.shape
    rows_total = lax.axis_size("rows")
    capacity = max(2, 2 * row_count // rows_total)
    slot_total = rows_total * capacity
    dest_hot = (new_rows[:, None] == jnp.arange(rows_total, dtype=jnp.int32)[None, :]).astype(
        jnp.int32
    )
    ranking = jnp.sum((jnp.cumsum(dest_hot, axis=0) - 1) * dest_hot, axis=1)
    slot_of = new_rows * capacity + ranking
    slot_ids = jnp.arange(slot_total, dtype=jnp.int32)
    sender = (slot_ids[:, None] == slot_of[None, :]).astype(jnp.bfloat16)
    outgoing = select_rows(sender, a_vals)
    filled = jnp.sum(sender, axis=1)
    incoming, flags = (
        lax.all_to_all(
            outgoing.reshape(rows_total, capacity, row_width),
            "rows",
            split_axis=0,
            concat_axis=0,
            tiled=True,
        ),
        lax.all_to_all(
            filled.reshape(rows_total, capacity), "rows", split_axis=0, concat_axis=0, tiled=True
        ),
    )
    flat_flags = flags.reshape(slot_total).astype(jnp.float32)
    position = jnp.cumsum(flat_flags) - 1.0
    flat_rows = incoming.reshape(slot_total, row_width)
    wanted = jnp.arange(row_count, dtype=jnp.float32)
    receiver = ((position[None, :] == wanted[:, None]) & (flat_flags[None, :] > 0.0)).astype(
        jnp.bfloat16
    )
    return select_rows(receiver, flat_rows)


def galerkin(a_vals, a_cols, p_vals):
    row_count, band = a_cols.shape
    slab_width = p_vals.shape[1] // B
    rows_pos = lax.axis_index("rows")
    slab_rows = row_count * lax.axis_size("grp")
    slab_all = lax.all_gather(p_vals, "grp", axis=0, tiled=True)
    padded = extended(slab_all, (("rows", 0),), slab_rows)
    owner_slab = a_cols // slab_rows
    window_slot = owner_slab - rows_pos + 1
    local_row = window_slot * slab_rows + (a_cols - owner_slab * slab_rows)
    gathered = padded[local_row].reshape(row_count, band, B, slab_width)
    blocks = a_vals.reshape(row_count, B, band, B)
    pieces = []
    for offset in range(3):
        kept_mask = (window_slot == offset).astype(jnp.bfloat16)
        masked = blocks * kept_mask[:, None, :, None]
        pieces.append(
            jnp.einsum("jake,jkef->jaf", masked, gathered, preferred_element_type=jnp.float32)
        )
    products = jnp.stack(pieces, axis=2).reshape(row_count * B, 3 * slab_width).astype(jnp.bfloat16)
    own_rows = p_vals.reshape(row_count * B, slab_width)
    partial_sum = lax.dot_general(
        own_rows, products, (((0,), (0,)), ((), ())), preferred_element_type=jnp.float32
    )
    return lax.psum_scatter(partial_sum, "grp", scatter_dimension=0, tiled=True).astype(
        jnp.bfloat16
    )


def local(a_vals, a_cols, p_vals, new_rows):
    coarse = galerkin(a_vals, a_cols, p_vals)
    a_moved = migrate(a_vals, new_rows)
    return (a_moved, coarse)


def solution(mesh):
    in_specs = (
        P(("rows", "grp"), None),
        P(("rows", "grp"), None),
        P(("rows", "grp"), None),
        P(("rows", "grp")),
    )
    out_specs = (P(("rows", "grp"), None), P(("rows", "grp"), None))
    return jax.shard_map(local, mesh=mesh, in_specs=in_specs, out_specs=out_specs, check_vma=False)
```

profile of v0, /device:TPU:0, one launch (start us, length us, event | category | flops | bytes accessed | tf_op | source)
XLA Modules:
  0.0 567.7 jit_solution(2155070878512227861)
XLA Ops:
  7.9 62.6 %all-gather.2.cloned.1.call-done = bf16[256,16384]{1,0:T(8,128)(2,1)} async-done(((bf16[64,16384]{1,0:T(8,128)(2,1)}), bf16[256,16384]{1,0:T(8,128)(2,1)}) %all-gather.2.cloned.1.call-update) | async-done | bytes 8388624 | tf_op jit(solution)/shard_map/all_gather | solution.py:67
  70.5 6.6 %collective-permute-start = (bf16[256,16384]{1,0:T(8,128)(2,1)}, bf16[256,16384]{1,0:T(8,128)(2,1)}, u32[]{:S(2)}, u32[]{:S(2)}) collective-permute-start(bf16[256,16384]{1,0:T(8,128)(2,1)} %all-gather.2.cloned.1.call-done), channel_id=1, source_target_pairs={{0,4},{4,8},{8,12},{12,16},{16,20},{20,24},{24,28},{1,5},{5,9},{9,... | collective-permute-start | bytes 25165832 | tf_op jit(solution)/shard_map/ppermute | solution.py:14
  77.1 1.3 collective-permute-start.1
  81.5 6.7 %all-to-all-start = ((bf16[8,1,16]{2,1,0:T(2,128)(2,1)}), bf16[8,1,16]{2,1,0:T(2,128)(2,1)S(1)}, u32[]{:S(2)}, u32[]{:S(2)}) async-start(bf16[8,1,16]{2,1,0:T(2,128)(2,1)} %all_to_all.12), calls=%async_computation | async-start | bytes 8192 | tf_op jit(solution)/shard_map/all_to_all | solution.py:48
  89.6 4.9 convolution_convert_fusion
  94.7 339.4 %all-to-all-done = bf16[8,1,16]{2,1,0:T(2,128)(2,1)S(1)} async-done(((bf16[8,1,16]{2,1,0:T(2,128)(2,1)}), bf16[8,1,16]{2,1,0:T(2,128)(2,1)S(1)}, u32[]{:S(2)}, u32[]{:S(2)}) %all-to-all-start) | async-done | bytes 288 | tf_op jit(solution)/shard_map/all_to_all | solution.py:48
  434.2 6.6 %all-to-all-start.1 = ((bf16[8,16,16384]{2,1,0:T(8,128)(2,1)}), bf16[8,16,16384]{2,1,0:T(8,128)(2,1)}, u32[]{:S(2)}, u32[]{:S(2)}) async-start(bf16[8,16,16384]{2,1,0:T(8,128)(2,1)} %bitcast.42), calls=%async_computation.1 | async-start | bytes 8388608 | tf_op jit(solution)/shard_map/all_to_all | solution.py:41
  440.9 5.5 reshape.86
  446.4 2.9 reshape.88
  449.6 17.6 %pad_maximum_fusion = bf16[768,16384]{1,0:T(8,128)(2,1)} fusion(bf16[256,16384]{1,0:T(8,128)(2,1)} %collective-permute-done.1, bf16[256,16384]{1,0:T(8,128)(2,1)} %all-gather.2.cloned.1.call-done, bf16[256,16384]{1,0:T(8,128)(2,1)} %collective-permute-done), kind=kLoop, calls=%fused_computation.1 | loop fusion | flops 75497472 | bytes 50331648 | tf_op jit(solution)/shard_map/concatenate | solution.py:18
  467.3 22.3 %gather_fusion = bf16[256,16384]{1,0:T(8,128)(2,1)} fusion(bf16[768,16384]{1,0:T(8,128)(2,1)} %pad_maximum_fusion, s32[1024]{0:T(1024)S(1)} %pad_clamp_fusion), kind=kCustom, calls=%fused_computation | custom fusion | bytes 16778240 | tf_op jit(solution)/shard_map/gather | solution.py:72
  489.6 9.4 %copy.62 = bf16[32,8,64,256]{3,2,1,0:T(8,128)(2,1)} copy(bf16[32,8,64,256]{3,1,2,0:T(8,128)(2,1)} %bitcast.39) | data formatting | bytes 16777216
  499.0 6.7 %fusion.10 = bf16[64,64,1,256]{3,1,0,2:T(8,128)(2,1)S(1)} fusion(bf16[64,4,64,256]{3,2,1,0:T(8,128)(2,1)} %bitcast.43, bf16[64,64,4,64]{3,2,1,0:T(4,128)(2,1)} %reshape.86, bf16[64,4]{1,0:T(8,128)(2,1)S(1)} %copy.51), kind=kOutput, calls=%fused_computation.18 | convolution fusion | flops 538968064 | bytes 12583424 | tf_op jit(solution)/shard_map/jake,jkef->jaf/dot_general | solution.py:79
  506.0 1.2 copy-done.2
  507.2 2.2 fusion.11
  509.4 2.2 fusion.9
  511.6 3.1 pad_maximum_fusion.1
  514.8 12.3 %copy.55 = bf16[64,64,3,256]{3,2,1,0:T(4,128)(2,1)} copy(bf16[64,64,3,256]{3,1,0,2:T(8,128)(2,1)} %pad_maximum_fusion.1) | data formatting | bytes 12582912 | tf_op jit(solution)/shard_map/stack | solution.py:81
  527.1 5.2 copy.63
  532.3 1.8 convolution_bitcast_fusion
  534.2 1.1 copy.60
  535.9 4.2 convolution_convert_fusion.1
  540.1 18.9 %reduce-scatter.4.cloned.1.call-done = f32[64,768]{1,0:T(8,128)} async-done(((f32[256,768]{1,0:T(8,128)}), f32[64,768]{1,0:T(8,128)}) %reduce-scatter.4.cloned.1.call-update) | async-done | bytes 196624
  559.0 1.1 copy.61
  (34 shorter events, 7.4 us)
Async XLA Ops:
  7.2 63.4 %all-gather.2.cloned.1.call-start = ((), (), s32[]{:S(2)}) async-start(), calls=%async_computation.3 | async-start | bytes 10485760 | tf_op jit(solution)/shard_map/all_gather | solution.py:67
  70.5 379.1 %collective-permute-start = (bf16[256,16384]{1,0:T(8,128)(2,1)}, bf16[256,16384]{1,0:T(8,128)(2,1)}, u32[]{:S(2)}, u32[]{:S(2)}) collective-permute-start(bf16[256,16384]{1,0:T(8,128)(2,1)} %all-gather.2.cloned.1.call-done), channel_id=1, source_target_pairs={{0,4},{4,8},{8,12},{12,16},{16,20},{20,24},{24,28},{1,5},{5,9},{9,... | collective-permute-start | bytes 25165832 | tf_op jit(solution)/shard_map/ppermute | solution.py:14
  77.1 372.5 %collective-permute-start.1 = (bf16[256,16384]{1,0:T(8,128)(2,1)}, bf16[256,16384]{1,0:T(8,128)(2,1)}, u32[]{:S(2)}, u32[]{:S(2)}) collective-permute-start(bf16[256,16384]{1,0:T(8,128)(2,1)} %all-gather.2.cloned.1.call-done), channel_id=1, source_target_pairs={{4,0},{8,4},{12,8},{16,12},{20,16},{24,20},{28,24},{5,1},{9,5},{13... | collective-permute-start | bytes 25165832 | tf_op jit(solution)/shard_map/ppermute | solution.py:17
  81.5 352.6 %all-to-all-start = ((bf16[8,1,16]{2,1,0:T(2,128)(2,1)}), bf16[8,1,16]{2,1,0:T(2,128)(2,1)S(1)}, u32[]{:S(2)}, u32[]{:S(2)}) async-start(bf16[8,1,16]{2,1,0:T(2,128)(2,1)} %all_to_all.12), calls=%async_computation | async-start | bytes 8192 | tf_op jit(solution)/shard_map/all_to_all | solution.py:48
  434.2 6.7 %copy-start = (bf16[64,16384]{1,0:T(8,128)(2,1)S(1)}, bf16[64,16384]{1,0:T(8,128)(2,1)}, u32[]{:S(2)}) copy-start(bf16[64,16384]{1,0:T(8,128)(2,1)} %param.4) | copy-start | bytes 6291460
  434.2 101.7 %all-to-all-start.1 = ((bf16[8,16,16384]{2,1,0:T(8,128)(2,1)}), bf16[8,16,16384]{2,1,0:T(8,128)(2,1)}, u32[]{:S(2)}, u32[]{:S(2)}) async-start(bf16[8,16,16384]{2,1,0:T(8,128)(2,1)} %bitcast.42), calls=%async_computation.1 | async-start | bytes 8388608 | tf_op jit(solution)/shard_map/all_to_all | solution.py:41
  440.8 118.2 %reduce-scatter.4.cloned.1.call-start = ((), (), s32[]{:S(2)}) async-start(), calls=%async_computation.4 | async-start | bytes 983040
  498.9 7.0 %copy-start.1 = (bf16[32,8,64,256]{3,2,1,0:T(8,128)(2,1)S(1)}, bf16[32,8,64,256]{3,2,1,0:T(8,128)(2,1)}, u32[]{:S(2)}) copy-start(bf16[32,8,64,256]{3,2,1,0:T(8,128)(2,1)} %copy.62) | copy-start | bytes 25165828
  499.0 8.2 %copy-start.2 = (bf16[64,64,4,64]{3,2,1,0:T(4,128)(2,1)S(1)}, bf16[64,64,4,64]{3,2,1,0:T(4,128)(2,1)}, u32[]{:S(2)}) copy-start(bf16[64,64,4,64]{3,2,1,0:T(4,128)(2,1)} %reshape.86) | copy-start | bytes 6291460
Sparse Core Ops, SparseCore 0:
  9.5 60.9 all-gather.1
  535.5 23.4 reduce-scatter.3
where the time goes:
time: 568 us
  waiting for transfers between devices  422 us (74%)
  local copies, waits for them, and re-layouts  63.5 us (11%)
  other arithmetic  24.9 us (4%)
  matrix products  22.1 us (4%)
  starting transfers between devices  21.3 us (4%)
  between operations  14.2 us (2%)
    all_to_all x1, waiting for transfers between devices, migrate(): lax.all_to_all(filled.reshape(rows_total, capacity), 'rows', split_axis=0...  339 us
    all_gather x1, waiting for transfers between devices, galerkin(): slab_all = lax.all_gather(p_vals, 'grp', axis=0, tiled=True)  62.6 us
    gather x1, local copies, waits for them, and re-layouts, galerkin(): gathered = padded[local_row].reshape(row_count, band, B, slab_width)  22.3 us
    unnamed x3, waiting for transfers between devices  19.6 us
    unnamed x11, local copies, waits for them, and re-layouts  19.1 us
    concatenate x1, other arithmetic, extended(): block = jnp.concatenate([low, block, high], axis=dim)  17.6 us
    another operation x1, local copies, waits for them, and re-layouts, galerkin(): jnp.stack(pieces, axis=2).reshape(row_count * B, 3 * slab_width)  12.3 us
  transfers between devices with their start and end apart: 6, of which 3 were waited for; matrix products, arithmetic and copies ran while one was open for 19% of the time, Pallas kernels for 0%

commit v1 on v0

v1 whole, which is shorter than its diff:
```python
import functools

import jax
import jax.numpy as jnp
from jax import lax
from jax.experimental import pallas as pl
from jax.experimental.pallas import tpu as pltpu
from jax.sharding import PartitionSpec as P


B = 64
UNROLL = 8
SLOTS = 3


def xor_permute(value, axis, bit):
    count = lax.axis_size(axis)
    return lax.ppermute(value, axis, [(i, i ^ bit) for i in range(count)])


def entry_codes(cols, rows_pos, grp_pos, groups):
    row_count, band = cols.shape
    device = cols // row_count
    near = device // groups - rows_pos
    side = jnp.where(rows_pos % 2 == 1, -near, near)
    slot = jnp.where(near == 0, 0, jnp.where(side == 1, 1, 2))
    target = slot * row_count + cols % row_count
    entry = jnp.arange(row_count, dtype=jnp.int32)[:, None] * band + jnp.arange(
        band, dtype=jnp.int32
    )
    code = entry * target_span(row_count) + target
    return jnp.where(device % groups == grp_pos, code, -1).reshape(-1)


def target_span(row_count):
    return pl.next_power_of_2(SLOTS * row_count + 1)


def clear(sums):
    rows = 2 * B

    def step(i, _):
        sums[pl.ds(pl.multiple_of(i * rows, rows), rows), :] = jnp.zeros(
            (rows, sums.shape[1]), sums.dtype
        )
        return 0

    lax.fori_loop(0, sums.shape[0] // rows, step, 0)


def scatter_part(band, row_count, offset, code_ref, a_ref, p_ref, sums, order):
    entries = row_count * band
    span = target_span(row_count)
    dummy = SLOTS * row_count

    def collect(step, found):
        code = code_ref[offset + step]
        order[found] = code
        return found + jnp.where(code >= 0, 1, 0)

    count = lax.fori_loop(0, entries, collect, 0, unroll=16)
    for pad in range(UNROLL):
        order[count + pad] = dummy

    def batch(step, _):
        terms = []
        for lane in range(UNROLL):
            code = order[step * UNROLL + lane]
            target = jnp.bitwise_and(code, span - 1)
            entry = lax.div(code, span)
            row = lax.div(entry, band)
            k = lax.rem(entry, band)
            start = pl.multiple_of(row * B, B)
            half = pl.multiple_of(lax.div(k, 2) * (2 * B), 2 * B)
            block = a_ref[pl.ds(start, B), pl.ds(half, 2 * B)]
            block = jnp.where(lax.rem(k, 2) == 1, block[:, B:], block[:, :B])
            left = p_ref[pl.ds(start, B), :]
            terms.append((contract(block, left), target))
        for term, target in terms:
            at = pl.ds(pl.multiple_of(target * B, B), B)
            sums[at, :] = sums[at, :] + term
        return 0

    lax.fori_loop(0, lax.div(count + UNROLL - 1, UNROLL), batch, 0)


def contract(left, right):
    return lax.dot_general(
        left, right, (((0,), (0,)), ((), ())), preferred_element_type=jnp.float32
    )


def early_kernel(band, row_count, parts, codes, *refs):
    sources, refs = refs[: 2 * parts], refs[2 * parts :]
    partial, (kept_1, kept_2) = refs[0], refs[1:3]
    buffers, refs = refs[3 : 3 + 2 * parts], refs[3 + 2 * parts :]
    sums, order, sems = refs
    copies = [
        pltpu.make_async_copy(src, dst, sems.at[i])
        for i, (src, dst) in enumerate(zip(sources, buffers))
    ]
    for copy in copies:
        copy.start()
    clear(sums)
    for part in range(parts):
        copies[2 * part].wait()
        copies[2 * part + 1].wait()
        a_ref, p_ref = buffers[2 * part : 2 * part + 2]
        scatter_part(
            band, row_count, part * row_count * band, codes, a_ref, p_ref, sums, order
        )
    size = row_count * B
    partial[...] = contract(sums[:size].astype(jnp.bfloat16), buffers[1][...])
    kept_1[...] = sums[size : 2 * size].astype(jnp.bfloat16)
    kept_2[...] = sums[2 * size : 3 * size].astype(jnp.bfloat16)


def late_kernel(band, row_count, parts, codes, *refs):
    count = 2 * parts + SLOTS + 3
    sources, refs = refs[:count], refs[count:]
    (keep, send), refs = refs[:2], refs[2:]
    buffers, refs = refs[:count], refs[count:]
    sums, order, sems = refs
    grp_pos = codes[parts * row_count * band]
    groups = 4
    share = keep.shape[0] // 2
    copies = [
        pltpu.make_async_copy(src, dst, sems.at[i])
        for i, (src, dst) in enumerate(zip(sources, buffers))
    ]
    for copy in copies:
        copy.start()
    clear(sums)
    for part in range(parts):
        copies[2 * part].wait()
        copies[2 * part + 1].wait()
        a_ref, p_ref = buffers[2 * part : 2 * part + 2]
        scatter_part(
            band, row_count, part * row_count * band, codes, a_ref, p_ref, sums, order
        )
    size = row_count * B
    rest = buffers[2 * parts :]
    rights, earlier, kept = rest[:SLOTS], rest[SLOTS], rest[SLOTS + 1 :]
    for copy in copies[2 * parts :]:
        copy.wait()
    width = rights[0].shape[1]
    for slot in range(SLOTS):
        right = rights[slot][...]
        here = contract(sums[slot * size : (slot + 1) * size].astype(jnp.bfloat16), right)
        if slot == 0:
            here = here + earlier[...]
        else:
            here = here + contract(kept[slot - 1][...], right)
        for block in range(groups):
            piece = here[block * share : (block + 1) * share]
            place = jnp.bitwise_xor(block, grp_pos)
            at = pl.ds(pl.multiple_of(lax.div(place, 2) * share, share), share)
            columns = slice(slot * width, (slot + 1) * width)

            @pl.when(lax.rem(place, 2) == 0)
            def _():
                keep[at, columns] = piece

            @pl.when(lax.rem(place, 2) == 1)
            def _():
                send[at, columns] = piece


def run_products(body, codes, arrays, outs, band, row_count, parts, flops):
    width = arrays[1].shape[1]
    return pl.pallas_call(
        functools.partial(body, band, row_count, parts),
        out_shape=outs,
        in_specs=[pl.BlockSpec(memory_space=pltpu.SMEM)]
        + [pl.BlockSpec(memory_space=pl.ANY)] * len(arrays),
        out_specs=jax.tree.map(lambda _: pl.BlockSpec(memory_space=pltpu.VMEM), outs),
        scratch_shapes=[pltpu.VMEM(x.shape, x.dtype) for x in arrays]
        + [
            pltpu.VMEM(((SLOTS * row_count + 2) * B, width), jnp.float32),
            pltpu.SMEM((row_count * band + UNROLL,), jnp.int32),
            pltpu.SemaphoreType.DMA((len(arrays),)),
        ],
        compiler_params=pltpu.CompilerParams(vmem_limit_bytes=56 << 20),
        cost_estimate=pl.CostEstimate(
            flops=flops,
            bytes_accessed=sum(x.size * x.dtype.itemsize for x in arrays),
            transcendentals=0,
        ),
    )(codes, *arrays)


def galerkin(a_vals, a_cols, p_vals):
    row_count, band = a_cols.shape
    width = p_vals.shape[1] // B
    rows_total, groups = lax.axis_size("rows"), lax.axis_size("grp")
    rows_pos, grp_pos = lax.axis_index("rows"), lax.axis_index("grp")
    assert groups == 4 and rows_total % 2 == 0
    p_own = p_vals.reshape(row_count * B, width)
    a_own = a_vals.reshape(row_count * B, band * B)

    partner = xor_permute(p_own, "rows", 1)
    both = ("rows", "grp")
    ahead = [
        (i * groups + g, j * groups + g)
        for g in range(1, groups, 2)
        for i in range(rows_total)
        for j in [i + 2 if i % 2 else i - 2]
        if 0 <= j < rows_total
    ]
    last = [
        (i * groups + g, j * groups + g)
        for g in range(0, groups, 2)
        for i in range(rows_total)
        for j in [i - 2 if i % 2 else i + 2]
        if 0 <= j < rows_total
    ]
    last += [(i * groups + g, (i ^ 1) * groups + g) for g in range(1, groups, 2) for i in range(rows_total)]
    moved = lax.ppermute(p_own, both, ahead)
    relay = jnp.where(grp_pos % 2 == 0, partner, moved)
    beyond = lax.ppermute(relay, both, last)

    c_far = xor_permute(a_cols, "grp", 2)
    c_near = xor_permute(a_cols, "grp", 1)
    c_last = xor_permute(c_far, "grp", 1)
    p_far = xor_permute(p_own, "grp", 2)
    a_far = xor_permute(a_own, "grp", 2)
    p_near = xor_permute(p_own, "grp", 1)
    a_near = xor_permute(a_own, "grp", 1)
    p_last = xor_permute(p_far, "grp", 1)
    a_last = xor_permute(a_far, "grp", 1)

    def codes(*cols):
        return jnp.concatenate([entry_codes(c, rows_pos, grp_pos, groups) for c in cols])

    flops = 4 * row_count * band * B * B * width // 2
    kept = jax.ShapeDtypeStruct((row_count * B, width), jnp.bfloat16)
    square = jax.ShapeDtypeStruct((width, width), jnp.float32)
    partial, kept_1, kept_2 = run_products(
        early_kernel,
        codes(a_cols, c_near),
        (a_own, p_own, a_near, p_near),
        (square, kept, kept),
        band,
        row_count,
        2,
        flops,
    )
    half = jax.ShapeDtypeStruct((width // 2, SLOTS * width), jnp.float32)
    keep, send = run_products(
        late_kernel,
        jnp.concatenate([codes(c_far, c_last), grp_pos.reshape(1)]),
        (a_far, p_far, a_last, p_last, p_own, partner, beyond, partial, kept_1, kept_2),
        (half, half),
        band,
        row_count,
        2,
        flops,
    )
    share = width // groups
    pair = keep + xor_permute(send, "grp", 1)
    total = pair[:share] + xor_permute(pair[share:], "grp", 2)
    total = total.astype(jnp.bfloat16)
    own, direct, diagonal = (total[:, i * width : (i + 1) * width] for i in range(SLOTS))
    even = rows_pos % 2 == 0
    return jnp.concatenate(
        [jnp.where(even, diagonal, direct), own, jnp.where(even, direct, diagonal)], axis=1
    )


def gather_kernel(chunks, capacity, source, target, probe, buffer, sems_probe, sems_in, sems_out):
    probes = [
        pltpu.make_async_copy(
            source.at[pl.ds(c * capacity, capacity), pl.ds(0, probe.shape[2])],
            probe.at[c],
            sems_probe.at[c],
        )
        for c in range(chunks)
    ]
    for copy in probes:
        copy.start()
    full, place, at = [], [], jnp.int32(0)
    limit = target.shape[0] // capacity - 1
    for c in range(chunks):
        probes[c].wait()
        here = jnp.max(probe[c].astype(jnp.float32)) < jnp.inf
        full.append(here)
        place.append(pl.multiple_of(jnp.minimum(at, limit) * capacity, capacity))
        at = at + jnp.where(here, 1, 0)

    def loads(c):
        return pltpu.make_async_copy(
            source.at[pl.ds(c * capacity, capacity), :],
            buffer.at[pl.ds(place[c], capacity), :],
            sems_in.at[c],
        )

    def stores(c):
        return pltpu.make_async_copy(
            buffer.at[pl.ds(place[c], capacity), :],
            target.at[pl.ds(place[c], capacity), :],
            sems_out.at[c],
        )

    for c in range(chunks):
        @pl.when(full[c])
        def _():
            loads(c).start()

    for c in range(chunks):
        @pl.when(full[c])
        def _():
            loads(c).wait()
            stores(c).start()

    for c in range(chunks):
        @pl.when(full[c])
        def _():
            stores(c).wait()


def gather_chunks(incoming, row_count, chunks, capacity):
    row_width = incoming.shape[1]
    return pl.pallas_call(
        functools.partial(gather_kernel, chunks, capacity),
        out_shape=jax.ShapeDtypeStruct((row_count, row_width), incoming.dtype),
        in_specs=[pl.BlockSpec(memory_space=pl.ANY)],
        out_specs=pl.BlockSpec(memory_space=pl.ANY),
        scratch_shapes=[
            pltpu.VMEM((chunks, capacity, 128), incoming.dtype),
            pltpu.VMEM((row_count, row_width), incoming.dtype),
            pltpu.SemaphoreType.DMA((chunks,)),
            pltpu.SemaphoreType.DMA((chunks,)),
            pltpu.SemaphoreType.DMA((chunks,)),
        ],
        name="gather_chunks",
    )(incoming)


def migrate(a_vals, new_rows):
    row_count, row_width = a_vals.shape
    rows_total = lax.axis_size("rows")
    capacity = max(2, 2 * row_count // rows_total)
    slot_total = rows_total * capacity
    earlier = jnp.arange(row_count)[None, :] < jnp.arange(row_count)[:, None]
    same = new_rows[:, None] == new_rows[None, :]
    ranking = jnp.sum((earlier & same).astype(jnp.int32), axis=1)
    slot_of = new_rows * capacity + ranking
    slot_ids = jnp.arange(slot_total, dtype=jnp.int32)
    sender = slot_ids[:, None] == slot_of[None, :]
    picked = jnp.dot(sender.astype(jnp.bfloat16), a_vals, preferred_element_type=jnp.float32)
    filled = jnp.any(sender, axis=1)
    chunked = capacity % 16 == 0
    if chunked:
        picked = jnp.where(filled[:, None], picked, jnp.inf)
    incoming = lax.all_to_all(
        picked.astype(a_vals.dtype).reshape(rows_total, capacity, row_width),
        "rows",
        split_axis=0,
        concat_axis=0,
        tiled=True,
    ).reshape(slot_total, row_width)
    if chunked:
        return gather_chunks(incoming, row_count, rows_total, capacity)
    flags = lax.all_to_all(
        filled.astype(jnp.bfloat16).reshape(rows_total, capacity),
        "rows",
        split_axis=0,
        concat_axis=0,
        tiled=True,
    )
    flat_flags = flags.reshape(slot_total).astype(jnp.float32)
    position = jnp.cumsum(flat_flags) - 1.0
    wanted = jnp.arange(row_count, dtype=jnp.float32)
    receiver = (position[None, :] == wanted[:, None]) & (flat_flags[None, :] > 0.0)
    return jnp.dot(
        receiver.astype(jnp.bfloat16), incoming, preferred_element_type=jnp.float32
    ).astype(a_vals.dtype)


def local(a_vals, a_cols, p_vals, new_rows):
    a_moved = migrate(a_vals, new_rows)
    coarse = galerkin(a_vals, a_cols, p_vals)
    return (a_moved, coarse)


def solution(mesh):
    in_specs = (
        P(("rows", "grp"), None),
        P(("rows", "grp"), None),
        P(("rows", "grp"), None),
        P(("rows", "grp")),
    )
    out_specs = (P(("rows", "grp"), None), P(("rows", "grp"), None))
    return jax.shard_map(local, mesh=mesh, in_specs=in_specs, out_specs=out_specs, check_vma=False)
```

time: 568 us -> 190 us (0.33)
  waiting for transfers between devices: 422 us -> 100 us
  local copies, waits for them, and re-layouts: 63.5 us -> 7.9 us
  Pallas kernels: 0 us -> 34.7 us
  matrix products: 22.1 us -> 4.93 us
  other arithmetic: 24.9 us -> 7.78 us
  between operations: 14.2 us -> 0.74 us
  starting transfers between devices: 21.3 us -> 33.4 us
    all_to_all x2 -> x1, waiting for transfers between devices: 339 us -> 0.01 us  [migrate(): lax.all_to_all(picked.astype(a_vals.dtype).reshape(rows_total, capacity,...]
    ppermute x2 -> x14, waiting for transfers between devices: 0.01 us -> 100 us  [the longest x12 95.7 us: xor_permute(): return lax.ppermute(value, axis, [(i, i ^ bit) for i in range(count)])]
    all_gather x1 -> x0, waiting for transfers between devices: 62.6 us -> none  [galerkin(): slab_all = lax.all_gather(p_vals, 'grp', axis=0, tiled=True)]
    pallas_call x0 -> x3, Pallas kernels: none -> 34.7 us  [the longest x2 30.6 us: run_products(): pl.pallas_call(functools.partial(body, band, row_count, parts), out_shape...]
    gather x1 -> x0, local copies, waits for them, and re-layouts: 22.3 us -> none  [galerkin(): gathered = padded[local_row].reshape(row_count, band, B, slab_width)]
    unnamed x3 -> x0, waiting for transfers between devices: 19.6 us -> none
    unnamed x11 -> x4, local copies, waits for them, and re-layouts: 19.1 us -> 0.01 us
    ppermute x2 -> x14, starting transfers between devices: 7.85 us -> 26.1 us  [the longest x1 16.1 us: galerkin(): beyond = lax.ppermute(relay, both, last)]
  transfers between devices with their start and end apart: 6 -> 15, of which waited for: 3 -> 6; matrix products, arithmetic and copies ran while one was open for 19% -> 7% of each run, Pallas kernels for 0% -> 16%
where the time goes in v1:
time: 190 us
  waiting for transfers between devices  100 us (53%)
  Pallas kernels  34.7 us (18%)
  starting transfers between devices  33.4 us (18%)
  local copies, waits for them, and re-layouts  7.9 us (4%)
  other arithmetic  7.78 us (4%)
  matrix products  4.93 us (3%)
    ppermute x12, waiting for transfers between devices, xor_permute(): return lax.ppermute(value, axis, [(i, i ^ bit) for i in range(count)])  95.7 us
    pallas_call x2, Pallas kernels, run_products(): pl.pallas_call(functools.partial(body, band, row_count, parts), out_shape...  30.6 us
    ppermute x1, starting transfers between devices, galerkin(): beyond = lax.ppermute(relay, both, last)  16.1 us
    ppermute x12, starting transfers between devices, xor_permute(): return lax.ppermute(value, axis, [(i, i ^ bit) for i in range(count)])  7.99 us
    all_to_all x1, starting transfers between devices, migrate(): lax.all_to_all(picked.astype(a_vals.dtype).reshape(rows_total, capacity,...  7.31 us
    dot_general x1, matrix products, migrate(): jnp.dot(sender.astype(jnp.bfloat16), a_vals, preferred_element_type=jnp.f...  4.93 us
    ppermute x1, waiting for transfers between devices, galerkin(): beyond = lax.ppermute(relay, both, last)  4.43 us
    reshape x1, local copies, waits for them, and re-layouts, galerkin(): a_own = a_vals.reshape(row_count * B, band * B)  4.19 us
  transfers between devices with their start and end apart: 15, of which 6 were waited for; matrix products, arithmetic and copies ran while one was open for 7% of the time, Pallas kernels for 16%

profile of v1, /device:TPU:0, one launch (start us, length us, event | category | flops | bytes accessed | tf_op | source)
XLA Modules:
  0.0 189.6 jit_solution(10658258794106951181)
XLA Ops:
  0.6 0.9 convert_reduce_fusion
  1.5 0.7 multiply_add_fusion
  2.3 4.9 %fusion = bf16[128,16384]{1,0:T(8,128)(2,1)} fusion(bf16[64,16384]{1,0:T(8,128)(2,1)} %param.4, pred[128]{0:T(512)(128)(4,1)S(1)} %fusion.2, s32[64]{0:T(128)S(1)} %multiply_add_fusion), kind=kOutput, calls=%fused_computation.1 | convolution fusion | flops 272637952 | bytes 6291840 | tf_op jit(solution)/shard_map/dot_general | solution.py:350
  7.2 7.3 %all-to-all-start = ((bf16[8,16,16384]{2,1,0:T(8,128)(2,1)}), bf16[8,16,16384]{2,1,0:T(8,128)(2,1)}, u32[]{:S(2)}, u32[]{:S(2)}) async-start(bf16[8,16,16384]{2,1,0:T(8,128)(2,1)} %bitcast.4), calls=%async_computation | async-start | bytes 8388608 | tf_op jit(solution)/shard_map/all_to_all | solution.py:355
  14.5 2.9 %reshape.46.refs_1_.refs_4_ = bf16[4096,256]{1,0:T(8,128)(2,1)S(1)} reshape(bf16[64,16384]{1,0:T(8,128)(2,1)} %param.6) | data formatting | bytes 4194304 | tf_op jit(solution)/shard_map/reshape | solution.py:198
  17.5 2.1 %collective-permute-start.6 = (bf16[4096,256]{1,0:T(8,128)(2,1)S(1)}, bf16[4096,256]{1,0:T(8,128)(2,1)}, u32[]{:S(2)}, u32[]{:S(2)}) collective-permute-start(bf16[4096,256]{1,0:T(8,128)(2,1)S(1)} %reshape.46.refs_1_.refs_4_), channel_id=1, source_target_pairs={{0,4},{4,0},{8,12},{12,8},{16,20},{20,16},{24,28},{28,24},{1,5},{5... | collective-permute-start | bytes 6291464 | tf_op jit(solution)/shard_map/ppermute | solution.py:18
  19.5 2.0 %collective-permute-start.7 = (bf16[4096,256]{1,0:T(8,128)(2,1)S(1)}, bf16[4096,256]{1,0:T(8,128)(2,1)}, u32[]{:S(2)}, u32[]{:S(2)}) collective-permute-start(bf16[4096,256]{1,0:T(8,128)(2,1)S(1)} %reshape.46.refs_1_.refs_4_), channel_id=1, source_target_pairs={{5,13},{9,1},{13,21},{17,9},{21,29},{25,17},{7,15},{11,3},{15,23},... | collective-permute-start | bytes 6291464 | tf_op jit(solution)/shard_map/ppermute | solution.py:218
  21.5 1.5 collective-permute-start.3
  23.0 4.2 %reshape.45.refs_0_ = bf16[4096,256]{1,0:T(8,128)(2,1)} reshape(bf16[64,16384]{1,0:T(8,128)(2,1)} %param.4) | data formatting | bytes 4194304 | tf_op jit(solution)/shard_map/reshape | solution.py:199
  27.7 1.5 collective-permute-start
  29.2 83.3 %collective-permute-done = s32[64,4]{0,1:T(4,128)S(1)} collective-permute-done((s32[64,4]{0,1:T(4,128)S(1)}, s32[64,4]{0,1:T(4,128)S(1)}, u32[]{:S(2)}, u32[]{:S(2)}) %collective-permute-start) | collective-permute-done | bytes 1056 | tf_op jit(solution)/shard_map/ppermute | solution.py:18
  112.5 1.2 collective-permute-done.9
  114.3 3.1 %broadcast_select_fusion = bf16[4096,256]{1,0:T(8,128)(2,1)} fusion(bf16[4096,256]{1,0:T(8,128)(2,1)} %collective-permute-done.6.refs_5_, bf16[4096,256]{1,0:T(8,128)(2,1)} %collective-permute-done.7, pred[]{:T(512)S(6)} %eq.111), kind=kLoop, calls=%fused_computation.2 | loop fusion | flops 1048576 | bytes 6291457 | tf_op jit(solution)/shard_map/jit(_where)/select_n | solution.py:219
  117.5 3.5 %collective-permute-done.1 = s32[64,4]{0,1:T(4,128)S(1)} collective-permute-done((s32[64,4]{0,1:T(4,128)S(1)}, s32[64,4]{0,1:T(4,128)S(1)}, u32[]{:S(2)}, u32[]{:S(2)}) %collective-permute-start.1) | collective-permute-done | bytes 1056 | tf_op jit(solution)/shard_map/ppermute | solution.py:18
  120.9 16.1 %collective-permute-start.8 = (bf16[4096,256]{1,0:T(8,128)(2,1)}, bf16[4096,256]{1,0:T(8,128)(2,1)}, u32[]{:S(2)}, u32[]{:S(2)}) collective-permute-start(bf16[4096,256]{1,0:T(8,128)(2,1)} %broadcast_select_fusion), channel_id=1, source_target_pairs={{0,8},{8,16},{12,4},{16,24},{20,12},{28,20},{2,10},{10,18},{14,6},... | collective-permute-start | bytes 6291464 | tf_op jit(solution)/shard_map/ppermute | solution.py:220
  139.7 15.5 %shard_map.59 = (f32[256,256]{1,0:T(8,128)}, bf16[4096,256]{1,0:T(8,128)(2,1)}, bf16[4096,256]{1,0:T(8,128)(2,1)}) custom-call(s32[512]{0:T(512)} %pad_add_fusion.1.codes, bf16[4096,256]{1,0:T(8,128)(2,1)} %reshape.45.refs_0_, bf16[4096,256]{1,0:T(8,128)(2,1)} %copy-done, bf16[4096,256]{1,0:T(8,128)(2,1)} %collective-permute-done.10.refs_2_, ...), custom_call_target="tpu_custom_call" | custom-call | flops 536870912 | bytes 8388608 | tf_op jit(solution)/shard_map/pallas_call | solution.py:171
  155.2 4.4 %collective-permute-done.8.refs_6_ = bf16[4096,256]{1,0:T(8,128)(2,1)} collective-permute-done((bf16[4096,256]{1,0:T(8,128)(2,1)}, bf16[4096,256]{1,0:T(8,128)(2,1)}, u32[]{:S(2)}, u32[]{:S(2)}) %collective-permute-start.8) | collective-permute-done | bytes 2097184 | tf_op jit(solution)/shard_map/ppermute | solution.py:220
  159.6 15.1 %shard_map.60 = (f32[128,768]{1,0:T(8,128)}, f32[128,768]{1,0:T(8,128)}) custom-call(s32[513]{0:T(1024)} %pad_add_fusion.codes, bf16[4096,256]{1,0:T(8,128)(2,1)} %collective-permute-done.2.refs_0_, bf16[4096,256]{1,0:T(8,128)(2,1)} %collective-permute-done.3.refs_1_, bf16[4096,256]{1,0:T(8,128)(2,1)} %collective-permute-done.4.refs_2_, ...), custom_call_target="tpu_custom_call" | custom-call | flops 536870912 | bytes 19136512 | tf_op jit(solution)/shard_map/pallas_call | solution.py:171
  174.8 1.9 %collective-permute-done.12 = f32[128,768]{1,0:T(8,128)S(1)} collective-permute-done((f32[128,768]{1,0:T(8,128)}, f32[128,768]{1,0:T(8,128)S(1)}, u32[]{:S(2)}, u32[]{:S(2)}) %collective-permute-start.12) | collective-permute-done | bytes 393248 | tf_op jit(solution)/shard_map/ppermute | solution.py:18
  176.7 1.0 add.160
  177.8 1.1 collective-permute-start.13
  178.9 5.9 %collective-permute-done.13 = f32[64,768]{1,0:T(8,128)S(1)} collective-permute-done((f32[64,768]{1,0:T(8,128)S(1)}, f32[64,768]{1,0:T(8,128)S(1)}, u32[]{:S(2)}, u32[]{:S(2)}) %collective-permute-start.13) | collective-permute-done | bytes 196640 | tf_op jit(solution)/shard_map/ppermute | solution.py:18
  184.9 0.6 pad_maximum_fusion
  185.5 4.1 %gather_chunks.1 = bf16[64,16384]{1,0:T(8,128)(2,1)} custom-call(bf16[128,16384]{1,0:T(8,128)(2,1)} %bitcast.1.source), custom_call_target="tpu_custom_call" | custom-call | tf_op jit(solution)/shard_map/gather_chunks/pallas_call | solution.py:323
  (37 shorter events, 4.0 us)
Async XLA Ops:
  7.2 178.3 %all-to-all-start = ((bf16[8,16,16384]{2,1,0:T(8,128)(2,1)}), bf16[8,16,16384]{2,1,0:T(8,128)(2,1)}, u32[]{:S(2)}, u32[]{:S(2)}) async-start(bf16[8,16,16384]{2,1,0:T(8,128)(2,1)} %bitcast.4), calls=%async_computation | async-start | bytes 8388608 | tf_op jit(solution)/shard_map/all_to_all | solution.py:355
  17.4 96.2 %copy-start = (bf16[4096,256]{1,0:T(8,128)(2,1)}, bf16[4096,256]{1,0:T(8,128)(2,1)S(1)}, u32[]{:S(2)}) copy-start(bf16[4096,256]{1,0:T(8,128)(2,1)S(1)} %reshape.46.refs_1_.refs_4_) | copy-start | bytes 6291460
  17.4 10.3 %copy-start.1 = (s32[64,4]{0,1:T(4,128)S(1)}, s32[64,4]{0,1:T(4,128)}, u32[]{:S(2)}) copy-start(s32[64,4]{0,1:T(4,128)} %param.5) | copy-start | bytes 3076
  17.5 96.4 %collective-permute-start.6 = (bf16[4096,256]{1,0:T(8,128)(2,1)S(1)}, bf16[4096,256]{1,0:T(8,128)(2,1)}, u32[]{:S(2)}, u32[]{:S(2)}) collective-permute-start(bf16[4096,256]{1,0:T(8,128)(2,1)S(1)} %reshape.46.refs_1_.refs_4_), channel_id=1, source_target_pairs={{0,4},{4,0},{8,12},{12,8},{16,20},{20,16},{24,28},{28,24},{1,5},{5... | collective-permute-start | bytes 6291464 | tf_op jit(solution)/shard_map/ppermute | solution.py:18
  19.5 94.6 %collective-permute-start.7 = (bf16[4096,256]{1,0:T(8,128)(2,1)S(1)}, bf16[4096,256]{1,0:T(8,128)(2,1)}, u32[]{:S(2)}, u32[]{:S(2)}) collective-permute-start(bf16[4096,256]{1,0:T(8,128)(2,1)S(1)} %reshape.46.refs_1_.refs_4_), channel_id=1, source_target_pairs={{5,13},{9,1},{13,21},{17,9},{21,29},{25,17},{7,15},{11,3},{15,23},... | collective-permute-start | bytes 6291464 | tf_op jit(solution)/shard_map/ppermute | solution.py:218
  21.5 115.6 %collective-permute-start.3 = (bf16[4096,256]{1,0:T(8,128)(2,1)S(1)}, bf16[4096,256]{1,0:T(8,128)(2,1)}, u32[]{:S(2)}, u32[]{:S(2)}) collective-permute-start(bf16[4096,256]{1,0:T(8,128)(2,1)S(1)} %reshape.46.refs_1_.refs_4_), channel_id=1, source_target_pairs={{0,2},{1,3},{2,0},{3,1},{4,6},{5,7},{6,4},{7,5},{8,10},{9,11},{10,... | collective-permute-start | bytes 6291464 | tf_op jit(solution)/shard_map/ppermute | solution.py:18
  27.2 109.9 %collective-permute-start.2 = (bf16[4096,256]{1,0:T(8,128)(2,1)}, bf16[4096,256]{1,0:T(8,128)(2,1)}, u32[]{:S(2)}, u32[]{:S(2)}) collective-permute-start(bf16[4096,256]{1,0:T(8,128)(2,1)} %reshape.45.refs_0_), channel_id=1, source_target_pairs={{0,2},{1,3},{2,0},{3,1},{4,6},{5,7},{6,4},{7,5},{8,10},{9,11},{10,... | collective-permute-start | bytes 6291464 | tf_op jit(solution)/shard_map/ppermute | solution.py:18
  27.7 84.7 %collective-permute-start = (s32[64,4]{0,1:T(4,128)S(1)}, s32[64,4]{0,1:T(4,128)S(1)}, u32[]{:S(2)}, u32[]{:S(2)}) collective-permute-start(s32[64,4]{0,1:T(4,128)S(1)} %copy-done.1), channel_id=1, source_target_pairs={{0,2},{1,3},{2,0},{3,1},{4,6},{5,7},{6,4},{7,5},{8,10},{9,11},{10,... | collective-permute-start | bytes 3080 | tf_op jit(solution)/shard_map/ppermute | solution.py:18
  112.5 1.2 collective-permute-start.9
  113.7 26.0 %collective-permute-start.11 = (bf16[4096,256]{1,0:T(8,128)(2,1)S(1)}, bf16[4096,256]{1,0:T(8,128)(2,1)}, u32[]{:S(2)}, u32[]{:S(2)}) collective-permute-start(bf16[4096,256]{1,0:T(8,128)(2,1)S(1)} %reshape.46.refs_1_.refs_4_), channel_id=1, source_target_pairs={{0,1},{1,0},{2,3},{3,2},{4,5},{5,4},{6,7},{7,6},{8,9},{9,8},{10,11... | collective-permute-start | bytes 6291464 | tf_op jit(solution)/shard_map/ppermute | solution.py:18
  113.8 25.9 %collective-permute-start.10 = (bf16[4096,256]{1,0:T(8,128)(2,1)}, bf16[4096,256]{1,0:T(8,128)(2,1)}, u32[]{:S(2)}, u32[]{:S(2)}) collective-permute-start(bf16[4096,256]{1,0:T(8,128)(2,1)} %reshape.45.refs_0_), channel_id=1, source_target_pairs={{0,1},{1,0},{2,3},{3,2},{4,5},{5,4},{6,7},{7,6},{8,9},{9,8},{10,11... | collective-permute-start | bytes 6291464 | tf_op jit(solution)/shard_map/ppermute | solution.py:18
  114.2 6.8 %collective-permute-start.1 = (s32[64,4]{0,1:T(4,128)S(1)}, s32[64,4]{0,1:T(4,128)S(1)}, u32[]{:S(2)}, u32[]{:S(2)}) collective-permute-start(s32[64,4]{0,1:T(4,128)S(1)} %collective-permute-done), channel_id=1, source_target_pairs={{0,1},{1,0},{2,3},{3,2},{4,5},{5,4},{6,7},{7,6},{8,9},{9,8},{10,11... | collective-permute-start | bytes 3080 | tf_op jit(solution)/shard_map/ppermute | solution.py:18
  120.9 38.6 %collective-permute-start.8 = (bf16[4096,256]{1,0:T(8,128)(2,1)}, bf16[4096,256]{1,0:T(8,128)(2,1)}, u32[]{:S(2)}, u32[]{:S(2)}) collective-permute-start(bf16[4096,256]{1,0:T(8,128)(2,1)} %broadcast_select_fusion), channel_id=1, source_target_pairs={{0,8},{8,16},{12,4},{16,24},{20,12},{28,20},{2,10},{10,18},{14,6},... | collective-permute-start | bytes 6291464 | tf_op jit(solution)/shard_map/ppermute | solution.py:220
  137.1 22.5 %collective-permute-start.5 = (bf16[4096,256]{1,0:T(8,128)(2,1)}, bf16[4096,256]{1,0:T(8,128)(2,1)}, u32[]{:S(2)}, u32[]{:S(2)}) collective-permute-start(bf16[4096,256]{1,0:T(8,128)(2,1)} %collective-permute-done.3.refs_1_), channel_id=1, source_target_pairs={{0,1},{1,0},{2,3},{3,2},{4,5},{5,4},{6,7},{7,6},{8,9},{9,8},{10,11... | collective-permute-start | bytes 6291464 | tf_op jit(solution)/shard_map/ppermute | solution.py:18
  137.1 22.5 %collective-permute-start.4 = (bf16[4096,256]{1,0:T(8,128)(2,1)}, bf16[4096,256]{1,0:T(8,128)(2,1)}, u32[]{:S(2)}, u32[]{:S(2)}) collective-permute-start(bf16[4096,256]{1,0:T(8,128)(2,1)} %collective-permute-done.2.refs_0_), channel_id=1, source_target_pairs={{0,1},{1,0},{2,3},{3,2},{4,5},{5,4},{6,7},{7,6},{8,9},{9,8},{10,11... | collective-permute-start | bytes 6291464 | tf_op jit(solution)/shard_map/ppermute | solution.py:18
  174.8 2.0 %collective-permute-start.12 = (f32[128,768]{1,0:T(8,128)}, f32[128,768]{1,0:T(8,128)S(1)}, u32[]{:S(2)}, u32[]{:S(2)}) collective-permute-start(f32[128,768]{1,0:T(8,128)} %get-tuple-element.11), channel_id=1, source_target_pairs={{0,1},{1,0},{2,3},{3,2},{4,5},{5,4},{6,7},{7,6},{8,9},{9,8},{10,11... | collective-permute-start | bytes 1179656 | tf_op jit(solution)/shard_map/ppermute | solution.py:18
  177.8 7.0 %collective-permute-start.13 = (f32[64,768]{1,0:T(8,128)S(1)}, f32[64,768]{1,0:T(8,128)S(1)}, u32[]{:S(2)}, u32[]{:S(2)}) collective-permute-start(f32[64,768]{1,0:T(8,128)S(1)} %slice.21), channel_id=1, source_target_pairs={{0,2},{1,3},{2,0},{3,1},{4,6},{5,7},{6,4},{7,5},{8,10},{9,11},{10,... | collective-permute-start | bytes 589832 | tf_op jit(solution)/shard_map/ppermute | solution.py:18

commit v2 on v1

--- a/solution.py
+++ b/solution.py
@@ -117,19 +117,26 @@
 
 def late_kernel(band, row_count, parts, codes, *refs):
     count = 2 * parts + SLOTS + 3
-    sources, refs = refs[:count], refs[count:]
+    sources, refs = refs[: count + 1], refs[count + 1 :]
     (keep, send), refs = refs[:2], refs[2:]
     buffers, refs = refs[:count], refs[count:]
     sums, order, sems = refs
     grp_pos = codes[parts * row_count * band]
     groups = 4
     share = keep.shape[0] // 2
+    odd_at = 2 * parts + SLOTS
+    sources, other = sources[:odd_at] + sources[odd_at + 1 :], sources[odd_at]
     copies = [
         pltpu.make_async_copy(src, dst, sems.at[i])
         for i, (src, dst) in enumerate(zip(sources, buffers))
     ]
-    for copy in copies:
-        copy.start()
+    other = pltpu.make_async_copy(other, buffers[odd_at - 1], sems.at[odd_at - 1])
+    for i, copy in enumerate(copies):
+        if i == odd_at - 1:
+            pl.when(lax.rem(grp_pos, 2) == 0)(copy.start)
+            pl.when(lax.rem(grp_pos, 2) == 1)(other.start)
+        else:
+            copy.start()
     clear(sums)
     for part in range(parts):
         copies[2 * part].wait()
@@ -166,19 +173,20 @@
                 send[at, columns] = piece
 
 
-def run_products(body, codes, arrays, outs, band, row_count, parts, flops):
+def run_products(body, codes, arrays, outs, band, row_count, parts, flops, skip=()):
     width = arrays[1].shape[1]
+    held = [x for i, x in enumerate(arrays) if i not in skip]
     return pl.pallas_call(
         functools.partial(body, band, row_count, parts),
         out_shape=outs,
         in_specs=[pl.BlockSpec(memory_space=pltpu.SMEM)]
         + [pl.BlockSpec(memory_space=pl.ANY)] * len(arrays),
         out_specs=jax.tree.map(lambda _: pl.BlockSpec(memory_space=pltpu.VMEM), outs),
-        scratch_shapes=[pltpu.VMEM(x.shape, x.dtype) for x in arrays]
+        scratch_shapes=[pltpu.VMEM(x.shape, x.dtype) for x in held]
         + [
             pltpu.VMEM(((SLOTS * row_count + 2) * B, width), jnp.float32),
             pltpu.SMEM((row_count * band + UNROLL,), jnp.int32),
-            pltpu.SemaphoreType.DMA((len(arrays),)),
+            pltpu.SemaphoreType.DMA((len(held),)),
         ],
         compiler_params=pltpu.CompilerParams(vmem_limit_bytes=56 << 20),
         cost_estimate=pl.CostEstimate(
@@ -207,17 +215,21 @@
         for j in [i + 2 if i % 2 else i - 2]
         if 0 <= j < rows_total
     ]
-    last = [
+    onward = [
         (i * groups + g, j * groups + g)
         for g in range(0, groups, 2)
         for i in range(rows_total)
         for j in [i - 2 if i % 2 else i + 2]
         if 0 <= j < rows_total
     ]
-    last += [(i * groups + g, (i ^ 1) * groups + g) for g in range(1, groups, 2) for i in range(rows_total)]
+    across = [
+        (i * groups + g, (i ^ 1) * groups + g)
+        for g in range(1, groups, 2)
+        for i in range(rows_total)
+    ]
     moved = lax.ppermute(p_own, both, ahead)
-    relay = jnp.where(grp_pos % 2 == 0, partner, moved)
-    beyond = lax.ppermute(relay, both, last)
+    beyond_even = lax.ppermute(partner, both, onward)
+    beyond_odd = lax.ppermute(moved, both, across)
 
     c_far = xor_permute(a_cols, "grp", 2)
     c_near = xor_permute(a_cols, "grp", 1)
@@ -249,12 +261,13 @@
     keep, send = run_products(
         late_kernel,
         jnp.concatenate([codes(c_far, c_last), grp_pos.reshape(1)]),
-        (a_far, p_far, a_last, p_last, p_own, partner, beyond, partial, kept_1, kept_2),
+        (a_far, p_far, a_last, p_last, p_own, partner, beyond_even, beyond_odd, partial, kept_1, kept_2),
         (half, half),
         band,
         row_count,
         2,
         flops,
+        skip=(4 + SLOTS,),
     )
     share = width // groups
     pair = keep + xor_permute(send, "grp", 1)
@@ -267,31 +280,62 @@
     )
 
 
-def gather_kernel(chunks, capacity, source, target, probe, buffer, sems_probe, sems_in, sems_out):
+def pack_kernel(chunks, capacity, slot_ref, a_ref, *outs):
+    slots = chunks * capacity
+    hot = lax.broadcasted_iota(jnp.int32, (slots, a_ref.shape[0]), 0) == slot_ref[...]
+    hot = hot.astype(jnp.float32)
+    filled = jnp.sum(hot, axis=1, keepdims=True) > 0.5
+    picked = jnp.dot(
+        hot.astype(jnp.bfloat16), a_ref[...], preferred_element_type=jnp.float32
+    )
+    picked = jnp.where(filled, picked, jnp.inf).astype(jnp.bfloat16)
+    for chunk in range(chunks):
+        outs[chunk][...] = picked[chunk * capacity : (chunk + 1) * capacity]
+
+
+def pack_chunks(a_vals, slot_of, chunks, capacity):
+    row_count, row_width = a_vals.shape
+    columns = 2048
+    return pl.pallas_call(
+        functools.partial(pack_kernel, chunks, capacity),
+        grid=(row_width // columns,),
+        out_shape=[jax.ShapeDtypeStruct((capacity, row_width), a_vals.dtype)] * chunks,
+        in_specs=[
+            pl.BlockSpec((1, row_count), lambda i: (0, 0)),
+            pl.BlockSpec((row_count, columns), lambda i: (0, i)),
+        ],
+        out_specs=[pl.BlockSpec((capacity, columns), lambda i: (0, i))] * chunks,
+        name="pack",
+    )(slot_of[None, :], a_vals)
+
+
+def gather_kernel(chunks, capacity, where, *refs):
+    sources, (target, probe, buffer, sems_probe, sems_in, sems_out) = refs[:chunks], refs[chunks:]
     probes = [
         pltpu.make_async_copy(
-            source.at[pl.ds(c * capacity, capacity), pl.ds(0, probe.shape[2])],
-            probe.at[c],
-            sems_probe.at[c],
+            sources[c].at[:, pl.ds(0, probe.shape[2])], probe.at[c], sems_probe.at[c]
         )
         for c in range(chunks)
     ]
     for copy in probes:
         copy.start()
-    full, place, at = [], [], jnp.int32(0)
-    limit = target.shape[0] // capacity - 1
+    full = []
     for c in range(chunks):
         probes[c].wait()
-        here = jnp.max(probe[c].astype(jnp.float32)) < jnp.inf
-        full.append(here)
-        place.append(pl.multiple_of(jnp.minimum(at, limit) * capacity, capacity))
-        at = at + jnp.where(here, 1, 0)
+        full.append(jnp.where(jnp.max(probe[c].astype(jnp.float32)) < jnp.inf, 1, 0))
+    limit = target.shape[0] // capacity - 1
+    place = []
+    for c in range(chunks):
+        sender = jnp.bitwise_xor(where[0], c)
+        ahead = jnp.int32(0)
+        for other in range(chunks):
+            first = jnp.bitwise_xor(where[0], other) < sender
+            ahead = ahead + jnp.where(first, full[other], 0)
+        place.append(pl.multiple_of(jnp.minimum(ahead, limit) * capacity, capacity))
 
     def loads(c):
         return pltpu.make_async_copy(
-            source.at[pl.ds(c * capacity, capacity), :],
-            buffer.at[pl.ds(place[c], capacity), :],
-            sems_in.at[c],
+            sources[c], buffer.at[pl.ds(place[c], capacity), :], sems_in.at[c]
         )
 
     def stores(c):
@@ -302,38 +346,41 @@
         )
 
     for c in range(chunks):
-        @pl.when(full[c])
-        def _():
-            loads(c).start()
-
+        pl.when(full[c] == 1)(lambda c=c: loads(c).start())
     for c in range(chunks):
-        @pl.when(full[c])
+        @pl.when(full[c] == 1)
         def _():
             loads(c).wait()
             stores(c).start()
 
     for c in range(chunks):
-        @pl.when(full[c])
-        def _():
-            stores(c).wait()
-
-
-def gather_chunks(incoming, row_count, chunks, capacity):
-    row_width = incoming.shape[1]
+        pl.when(full[c] == 1)(lambda c=c: stores(c).wait())
+
+
+def gather_chunks(incoming, rows_pos, row_count):
+    chunks = len(incoming)
+    capacity, row_width = incoming[0].shape
+    dtype = incoming[0].dtype
     return pl.pallas_call(
         functools.partial(gather_kernel, chunks, capacity),
-        out_shape=jax.ShapeDtypeStruct((row_count, row_width), incoming.dtype),
-        in_specs=[pl.BlockSpec(memory_space=pl.ANY)],
+        out_shape=jax.ShapeDtypeStruct((row_count, row_width), dtype),
+        in_specs=[pl.BlockSpec(memory_space=pltpu.SMEM)]
+        + [pl.BlockSpec(memory_space=pl.ANY)] * chunks,
         out_specs=pl.BlockSpec(memory_space=pl.ANY),
         scratch_shapes=[
-            pltpu.VMEM((chunks, capacity, 128), incoming.dtype),
-            pltpu.VMEM((row_count, row_width), incoming.dtype),
+            pltpu.VMEM((chunks, capacity, 128), dtype),
+            pltpu.VMEM((row_count, row_width), dtype),
             pltpu.SemaphoreType.DMA((chunks,)),
             pltpu.SemaphoreType.DMA((chunks,)),
             pltpu.SemaphoreType.DMA((chunks,)),
         ],
         name="gather_chunks",
-    )(incoming)
+    )(rows_pos.astype(jnp.int32).reshape(1), *incoming)
+
+
+def use_chunks(row_count, rows_total):
+    capacity = max(2, 2 * row_count // rows_total)
+    return capacity % 16 == 0 and rows_total & (rows_total - 1) == 0
 
 
 def migrate(a_vals, new_rows):
@@ -344,14 +391,20 @@
     earlier = jnp.arange(row_count)[None, :] < jnp.arange(row_count)[:, None]
     same = new_rows[:, None] == new_rows[None, :]
     ranking = jnp.sum((earlier & same).astype(jnp.int32), axis=1)
+    if use_chunks(row_count, rows_total):
+        rows_pos = lax.axis_index("rows")
+        slot_of = jnp.bitwise_xor(new_rows, rows_pos) * capacity + ranking
+        chunks = pack_chunks(a_vals, slot_of, rows_total, capacity)
+        incoming = [chunks[0]] + [
+            xor_permute(chunks[bit], "rows", bit)
+            for bit in range(1, rows_total)
+        ]
+        return gather_chunks(incoming, rows_pos, row_count)
     slot_of = new_rows * capacity + ranking
     slot_ids = jnp.arange(slot_total, dtype=jnp.int32)
     sender = slot_ids[:, None] == slot_of[None, :]
     picked = jnp.dot(sender.astype(jnp.bfloat16), a_vals, preferred_element_type=jnp.float32)
     filled = jnp.any(sender, axis=1)
-    chunked = capacity % 16 == 0
-    if chunked:
-        picked = jnp.where(filled[:, None], picked, jnp.inf)
     incoming = lax.all_to_all(
         picked.astype(a_vals.dtype).reshape(rows_total, capacity, row_width),
         "rows",
@@ -359,8 +412,6 @@
         concat_axis=0,
         tiled=True,
     ).reshape(slot_total, row_width)
-    if chunked:
-        return gather_chunks(incoming, row_count, rows_total, capacity)
     flags = lax.all_to_all(
         filled.astype(jnp.bfloat16).reshape(rows_total, capacity),
         "rows",

time: 190 us -> 255 us (1.34)
  the two profiles are of different devices: /device:TPU:0 before, /device:TPU:22 now
where the time goes in v2:
time: 255 us; the launch traced here: 254 us
  waiting for transfers between devices  177 us (69%)
  Pallas kernels  43.2 us (17%)
  starting transfers between devices  19.8 us (8%)
  local copies, waits for them, and re-layouts  9.23 us (4%)
  other arithmetic  3.67 us (1%)
    ppermute x19, waiting for transfers between devices, xor_permute(): return lax.ppermute(value, axis, [(i, i ^ bit) for i in range(count)])  177 us
    pallas_call x2, Pallas kernels, run_products(): pl.pallas_call(functools.partial(body, band, row_count, parts), out_shape...  32 us
    ppermute x19, starting transfers between devices, xor_permute(): return lax.ppermute(value, axis, [(i, i ^ bit) for i in range(count)])  14.7 us
    pallas_call x1, Pallas kernels, pack_chunks(): pl.pallas_call(functools.partial(pack_kernel, chunks, capacity), grid=(ro...  6.99 us
  transfers between devices with their start and end apart: 22, of which 8 were waited for; matrix products, arithmetic and copies ran while one was open for 3% of the time, Pallas kernels for 17%

profile of v2, /device:TPU:22, one launch (start us, length us, event | category | flops | bytes accessed | tf_op | source)
XLA Modules:
  0.0 254.1 jit_solution(2375317925899537796)
XLA Ops:
  0.6 2.9 %reshape.40.refs_1_.refs_4_ = bf16[4096,256]{1,0:T(8,128)(2,1)S(1)} reshape(bf16[64,16384]{1,0:T(8,128)(2,1)} %param.6) | data formatting | bytes 4194304 | tf_op jit(solution)/shard_map/reshape | solution.py:206
  4.2 1.5 collective-permute-start.7
  5.7 46.1 %collective-permute-done.7 = s32[64,4]{0,1:T(4,128)S(1)} collective-permute-done((s32[64,4]{0,1:T(4,128)S(1)}, s32[64,4]{0,1:T(4,128)S(1)}, u32[]{:S(2)}, u32[]{:S(2)}) %collective-permute-start.7) | collective-permute-done | bytes 1056 | tf_op jit(solution)/shard_map/ppermute | solution.py:18
  52.3 4.2 %reshape.39.refs_0_ = bf16[4096,256]{1,0:T(8,128)(2,1)} reshape(bf16[64,16384]{1,0:T(8,128)(2,1)} %a_ref.1) | data formatting | bytes 4194304 | tf_op jit(solution)/shard_map/reshape | solution.py:207
  56.5 2.0 collective-permute-start.15
  59.0 1.3 collective-permute-start.18
  60.3 39.6 %collective-permute-done.13.refs_5_ = bf16[4096,256]{1,0:T(8,128)(2,1)} collective-permute-done((bf16[4096,256]{1,0:T(8,128)(2,1)S(1)}, bf16[4096,256]{1,0:T(8,128)(2,1)}, u32[]{:S(2)}, u32[]{:S(2)}) %collective-permute-start.13) | collective-permute-done | bytes 2097184 | tf_op jit(solution)/shard_map/ppermute | solution.py:18
  99.9 2.3 collective-permute-start.14
  103.1 3.6 %collective-permute-done.9.refs_0_ = bf16[4096,256]{1,0:T(8,128)(2,1)} collective-permute-done((bf16[4096,256]{1,0:T(8,128)(2,1)}, bf16[4096,256]{1,0:T(8,128)(2,1)}, u32[]{:S(2)}, u32[]{:S(2)}) %collective-permute-start.9) | collective-permute-done | bytes 2097184 | tf_op jit(solution)/shard_map/ppermute | solution.py:18
  108.1 7.0 %pack.1 = (bf16[16,16384]{1,0:T(8,128)(2,1)}, bf16[16,16384]{1,0:T(8,128)(2,1)}, bf16[16,16384]{1,0:T(8,128)(2,1)}, bf16[16,16384]{1,0:T(8,128)(2,1)}, bf16[16,1...) custom-call(s32[1,64]{1,0:T(1,128)} %add_bitcast_fusion.slot_ref, ...), custom_call_target="tpu_custom_call" | custom-call | tf_op jit(solution)/shard_map/pack/pallas_call | solution.py:299
  117.4 2.3 collective-permute-start.1
  120.3 16.3 %shard_map.59 = (f32[256,256]{1,0:T(8,128)}, bf16[4096,256]{1,0:T(8,128)(2,1)}, bf16[4096,256]{1,0:T(8,128)(2,1)}) custom-call(s32[512]{0:T(512)} %pad_add_fusion.1.codes, bf16[4096,256]{1,0:T(8,128)(2,1)} %reshape.39.refs_0_, bf16[4096,256]{1,0:T(8,128)(2,1)} %copy-done, bf16[4096,256]{1,0:T(8,128)(2,1)} %collective-permute-done.18.refs_2_, ...), custom_call_target="tpu_custom_call" | custom-call | flops 536870912 | bytes 8388608 | tf_op jit(solution)/shard_map/pallas_call | solution.py:179
  136.6 1.3 copy-done.1
  137.9 15.7 %shard_map.60 = (f32[128,768]{1,0:T(8,128)}, f32[128,768]{1,0:T(8,128)}) custom-call(s32[513]{0:T(1024)} %pad_add_fusion.codes, bf16[4096,256]{1,0:T(8,128)(2,1)} %collective-permute-done.9.refs_0_, bf16[4096,256]{1,0:T(8,128)(2,1)} %collective-permute-done.10.refs_1_, bf16[4096,256]{1,0:T(8,128)(2,1)} %collective-permute-done.11.refs_2_, ...), custom_call_target="tpu_custom_call" | custom-call | flops 536870912 | bytes 21233664 | tf_op jit(solution)/shard_map/pallas_call | solution.py:179
  154.2 2.5 collective-permute-start.4
  156.7 1.6 collective-permute-start.5
  158.3 1.8 collective-permute-start.6
  160.1 1.0 add.156
  161.1 14.4 %collective-permute-done.2.refs_3_ = bf16[16,16384]{1,0:T(8,128)(2,1)S(1)} collective-permute-done((bf16[16,16384]{1,0:T(8,128)(2,1)S(1)}, bf16[16,16384]{1,0:T(8,128)(2,1)S(1)}, u32[]{:S(2)}, u32[]{:S(2)}) %collective-permute-start.2) | collective-permute-done | bytes 524320 | tf_op jit(solution)/shard_map/ppermute | solution.py:18
  175.5 36.3 %collective-permute-done.3.refs_4_ = bf16[16,16384]{1,0:T(8,128)(2,1)S(1)} collective-permute-done((bf16[16,16384]{1,0:T(8,128)(2,1)}, bf16[16,16384]{1,0:T(8,128)(2,1)S(1)}, u32[]{:S(2)}, u32[]{:S(2)}) %collective-permute-start.3) | collective-permute-done | bytes 524320 | tf_op jit(solution)/shard_map/ppermute | solution.py:18
  211.8 11.2 %collective-permute-done.4.refs_5_ = bf16[16,16384]{1,0:T(8,128)(2,1)S(1)} collective-permute-done((bf16[16,16384]{1,0:T(8,128)(2,1)}, bf16[16,16384]{1,0:T(8,128)(2,1)S(1)}, u32[]{:S(2)}, u32[]{:S(2)}) %collective-permute-start.4) | collective-permute-done | bytes 524320 | tf_op jit(solution)/shard_map/ppermute | solution.py:18
  223.1 12.6 %collective-permute-done.5.refs_6_ = bf16[16,16384]{1,0:T(8,128)(2,1)} collective-permute-done((bf16[16,16384]{1,0:T(8,128)(2,1)}, bf16[16,16384]{1,0:T(8,128)(2,1)}, u32[]{:S(2)}, u32[]{:S(2)}) %collective-permute-start.5) | collective-permute-done | bytes 524320 | tf_op jit(solution)/shard_map/ppermute | solution.py:18
  235.7 13.5 %collective-permute-done.6.refs_7_ = bf16[16,16384]{1,0:T(8,128)(2,1)} collective-permute-done((bf16[16,16384]{1,0:T(8,128)(2,1)}, bf16[16,16384]{1,0:T(8,128)(2,1)}, u32[]{:S(2)}, u32[]{:S(2)}) %collective-permute-start.6) | collective-permute-done | bytes 524320 | tf_op jit(solution)/shard_map/ppermute | solution.py:18
  249.2 4.2 %gather_chunks.1 = bf16[64,16384]{1,0:T(8,128)(2,1)} custom-call(s32[1]{0:T(128)} %bitcast.where, bf16[16,16384]{1,0:T(8,128)(2,1)} %get-tuple-element.15.refs_0_, bf16[16,16384]{1,0:T(8,128)(2,1)} %copy-done.2, bf16[16,16384]{1,0:T(8,128)(2,1)} %copy-done.3, bf16[16,16384]{1,0:T(8,128)(2,1)} %copy-done.4, bf16[16,16384]{1,0:T(8,128)(2,1)} %copy-done.5, ...), custom_call_target="tpu_custom_call" | custom-call | tf_op jit(solution)/shard_map/gather_chunks/pallas_call | solution.py:364
  (65 shorter events, 8.2 us)
Async XLA Ops:
  3.5 103.9 %copy-start.8 = (s32[64]{0:T(128)S(1)}, s32[64]{0:T(128)}, u32[]{:S(2)}) copy-start(s32[64]{0:T(128)} %param.7) | copy-start | bytes 772
  3.5 55.5 %collective-permute-start.19 = (bf16[4096,256]{1,0:T(8,128)(2,1)S(1)}, bf16[4096,256]{1,0:T(8,128)(2,1)}, u32[]{:S(2)}, u32[]{:S(2)}) collective-permute-start(bf16[4096,256]{1,0:T(8,128)(2,1)S(1)} %reshape.40.refs_1_.refs_4_), channel_id=1, source_target_pairs={{0,1},{1,0},{2,3},{3,2},{4,5},{5,4},{6,7},{7,6},{8,9},{9,8},{10,11... | collective-permute-start | bytes 6291464 | tf_op jit(solution)/shard_map/ppermute | solution.py:18
  3.6 56.6 %collective-permute-start.10 = (bf16[4096,256]{1,0:T(8,128)(2,1)S(1)}, bf16[4096,256]{1,0:T(8,128)(2,1)}, u32[]{:S(2)}, u32[]{:S(2)}) collective-permute-start(bf16[4096,256]{1,0:T(8,128)(2,1)S(1)} %reshape.40.refs_1_.refs_4_), channel_id=1, source_target_pairs={{0,2},{1,3},{2,0},{3,1},{4,6},{5,7},{6,4},{7,5},{8,10},{9,11},{10,... | collective-permute-start | bytes 6291464 | tf_op jit(solution)/shard_map/ppermute | solution.py:18
  4.2 47.6 %collective-permute-start.7 = (s32[64,4]{0,1:T(4,128)S(1)}, s32[64,4]{0,1:T(4,128)S(1)}, u32[]{:S(2)}, u32[]{:S(2)}) collective-permute-start(s32[64,4]{0,1:T(4,128)S(1)} %copy-done.7), channel_id=1, source_target_pairs={{0,2},{1,3},{2,0},{3,1},{4,6},{5,7},{6,4},{7,5},{8,10},{9,11},{10,... | collective-permute-start | bytes 3080 | tf_op jit(solution)/shard_map/ppermute | solution.py:18
  5.7 50.8 %collective-permute-start.17 = (s32[64,4]{0,1:T(4,128)S(1)}, s32[64,4]{0,1:T(4,128)S(1)}, u32[]{:S(2)}, u32[]{:S(2)}) collective-permute-start(s32[64,4]{0,1:T(4,128)S(1)} %copy-done.7), channel_id=1, source_target_pairs={{0,1},{1,0},{2,3},{3,2},{4,5},{5,4},{6,7},{7,6},{8,9},{9,8},{10,11... | collective-permute-start | bytes 3080 | tf_op jit(solution)/shard_map/ppermute | solution.py:18
  51.8 6.7 %collective-permute-start.8 = (s32[64,4]{0,1:T(4,128)S(1)}, s32[64,4]{0,1:T(4,128)S(1)}, u32[]{:S(2)}, u32[]{:S(2)}) collective-permute-start(s32[64,4]{0,1:T(4,128)S(1)} %collective-permute-done.7), channel_id=1, source_target_pairs={{0,1},{1,0},{2,3},{3,2},{4,5},{5,4},{6,7},{7,6},{8,9},{9,8},{10,11... | collective-permute-start | bytes 3080 | tf_op jit(solution)/shard_map/ppermute | solution.py:18
  51.8 48.1 %collective-permute-start.13 = (bf16[4096,256]{1,0:T(8,128)(2,1)S(1)}, bf16[4096,256]{1,0:T(8,128)(2,1)}, u32[]{:S(2)}, u32[]{:S(2)}) collective-permute-start(bf16[4096,256]{1,0:T(8,128)(2,1)S(1)} %reshape.40.refs_1_.refs_4_), channel_id=1, source_target_pairs={{0,4},{4,0},{8,12},{12,8},{16,20},{20,16},{24,28},{28,24},{1,5},{5... | collective-permute-start | bytes 6291464 | tf_op jit(solution)/shard_map/ppermute | solution.py:18
  56.5 45.8 %collective-permute-start.15 = (bf16[4096,256]{1,0:T(8,128)(2,1)S(1)}, bf16[4096,256]{1,0:T(8,128)(2,1)}, u32[]{:S(2)}, u32[]{:S(2)}) collective-permute-start(bf16[4096,256]{1,0:T(8,128)(2,1)S(1)} %reshape.40.refs_1_.refs_4_), channel_id=1, source_target_pairs={{5,13},{9,1},{13,21},{17,9},{21,29},{25,17},{7,15},{11,3},{15,23},... | collective-permute-start | bytes 6291464 | tf_op jit(solution)/shard_map/ppermute | solution.py:230
  58.5 48.3 %collective-permute-start.9 = (bf16[4096,256]{1,0:T(8,128)(2,1)}, bf16[4096,256]{1,0:T(8,128)(2,1)}, u32[]{:S(2)}, u32[]{:S(2)}) collective-permute-start(bf16[4096,256]{1,0:T(8,128)(2,1)} %reshape.39.refs_0_), channel_id=1, source_target_pairs={{0,2},{1,3},{2,0},{3,1},{4,6},{5,7},{6,4},{7,5},{8,10},{9,11},{10,... | collective-permute-start | bytes 6291464 | tf_op jit(solution)/shard_map/ppermute | solution.py:18
  59.0 57.6 %collective-permute-start.18 = (bf16[4096,256]{1,0:T(8,128)(2,1)}, bf16[4096,256]{1,0:T(8,128)(2,1)}, u32[]{:S(2)}, u32[]{:S(2)}) collective-permute-start(bf16[4096,256]{1,0:T(8,128)(2,1)} %reshape.39.refs_0_), channel_id=1, source_target_pairs={{0,1},{1,0},{2,3},{3,2},{4,5},{5,4},{6,7},{7,6},{8,9},{9,8},{10,11... | collective-permute-start | bytes 6291464 | tf_op jit(solution)/shard_map/ppermute | solution.py:18
  60.3 57.2 %collective-permute-start.12 = (bf16[4096,256]{1,0:T(8,128)(2,1)}, bf16[4096,256]{1,0:T(8,128)(2,1)}, u32[]{:S(2)}, u32[]{:S(2)}) collective-permute-start(bf16[4096,256]{1,0:T(8,128)(2,1)} %collective-permute-done.10.refs_1_), channel_id=1, source_target_pairs={{0,1},{1,0},{2,3},{3,2},{4,5},{5,4},{6,7},{7,6},{8,9},{9,8},{10,11... | collective-permute-start | bytes 6291464 | tf_op jit(solution)/shard_map/ppermute | solution.py:18
  99.9 36.7 %collective-permute-start.14 = (bf16[4096,256]{1,0:T(8,128)(2,1)}, bf16[4096,256]{1,0:T(8,128)(2,1)}, u32[]{:S(2)}, u32[]{:S(2)}) collective-permute-start(bf16[4096,256]{1,0:T(8,128)(2,1)} %collective-permute-done.13.refs_5_), channel_id=1, source_target_pairs={{0,8},{8,16},{12,4},{16,24},{20,12},{28,20},{2,10},{10,18},{14,6},... | collective-permute-start | bytes 6291464 | tf_op jit(solution)/shard_map/ppermute | solution.py:231
  102.3 34.3 %collective-permute-start.16 = (bf16[4096,256]{1,0:T(8,128)(2,1)}, bf16[4096,256]{1,0:T(8,128)(2,1)S(1)}, u32[]{:S(2)}, u32[]{:S(2)}) collective-permute-start(bf16[4096,256]{1,0:T(8,128)(2,1)} %collective-permute-done.15), channel_id=1, source_target_pairs={{1,5},{5,1},{9,13},{13,9},{17,21},{21,17},{25,29},{29,25},{3,7},{7... | collective-permute-start | bytes 6291464 | tf_op jit(solution)/shard_map/ppermute | solution.py:232
  106.7 29.9 %collective-permute-start.11 = (bf16[4096,256]{1,0:T(8,128)(2,1)}, bf16[4096,256]{1,0:T(8,128)(2,1)}, u32[]{:S(2)}, u32[]{:S(2)}) collective-permute-start(bf16[4096,256]{1,0:T(8,128)(2,1)} %collective-permute-done.9.refs_0_), channel_id=1, source_target_pairs={{0,1},{1,0},{2,3},{3,2},{4,5},{5,4},{6,7},{7,6},{8,9},{9,8},{10,11... | collective-permute-start | bytes 6291464 | tf_op jit(solution)/shard_map/ppermute | solution.py:18
  116.6 37.6 %collective-permute-start = (bf16[16,16384]{1,0:T(8,128)(2,1)}, bf16[16,16384]{1,0:T(8,128)(2,1)S(1)}, u32[]{:S(2)}, u32[]{:S(2)}) collective-permute-start(bf16[16,16384]{1,0:T(8,128)(2,1)} %get-tuple-element.16), channel_id=1, source_target_pairs={{0,4},{4,0},{8,12},{12,8},{16,20},{20,16},{24,28},{28,24},{1,5},{5... | collective-permute-start | bytes 1572872 | tf_op jit(solution)/shard_map/ppermute | solution.py:18
  117.4 39.2 %collective-permute-start.1 = (bf16[16,16384]{1,0:T(8,128)(2,1)}, bf16[16,16384]{1,0:T(8,128)(2,1)S(1)}, u32[]{:S(2)}, u32[]{:S(2)}) collective-permute-start(bf16[16,16384]{1,0:T(8,128)(2,1)} %get-tuple-element.17), channel_id=1, source_target_pairs={{0,8},{4,12},{8,0},{12,4},{16,24},{20,28},{24,16},{28,20},{1,9},{5... | collective-permute-start | bytes 1572872 | tf_op jit(solution)/shard_map/ppermute | solution.py:18
  153.6 4.6 %collective-permute-start.20 = (f32[128,768]{1,0:T(8,128)}, f32[128,768]{1,0:T(8,128)S(1)}, u32[]{:S(2)}, u32[]{:S(2)}) collective-permute-start(f32[128,768]{1,0:T(8,128)} %get-tuple-element.27), channel_id=1, source_target_pairs={{0,1},{1,0},{2,3},{3,2},{4,5},{5,4},{6,7},{7,6},{8,9},{9,8},{10,11... | collective-permute-start | bytes 1179656 | tf_op jit(solution)/shard_map/ppermute | solution.py:18
  153.7 21.8 %collective-permute-start.2 = (bf16[16,16384]{1,0:T(8,128)(2,1)S(1)}, bf16[16,16384]{1,0:T(8,128)(2,1)S(1)}, u32[]{:S(2)}, u32[]{:S(2)}) collective-permute-start(bf16[16,16384]{1,0:T(8,128)(2,1)S(1)} %copy-done.9), channel_id=1, source_target_pairs={{0,12},{4,8},{8,4},{12,0},{16,28},{20,24},{24,20},{28,16},{1,13},{... | collective-permute-start | bytes 1572872 | tf_op jit(solution)/shard_map/ppermute | solution.py:18
  154.2 57.6 %collective-permute-start.3 = (bf16[16,16384]{1,0:T(8,128)(2,1)}, bf16[16,16384]{1,0:T(8,128)(2,1)S(1)}, u32[]{:S(2)}, u32[]{:S(2)}) collective-permute-start(bf16[16,16384]{1,0:T(8,128)(2,1)} %get-tuple-element.19), channel_id=1, source_target_pairs={{0,16},{4,20},{8,24},{12,28},{16,0},{20,4},{24,8},{28,12},{1,17},{... | collective-permute-start | bytes 1572872 | tf_op jit(solution)/shard_map/ppermute | solution.py:18
  154.2 94.9 %copy-start.2 = (bf16[16,16384]{1,0:T(8,128)(2,1)}, bf16[16,16384]{1,0:T(8,128)(2,1)S(1)}, u32[]{:S(2)}) copy-start(bf16[16,16384]{1,0:T(8,128)(2,1)S(1)} %collective-permute-done.refs_1_) | copy-start | bytes 1572868
  154.2 68.8 %collective-permute-start.4 = (bf16[16,16384]{1,0:T(8,128)(2,1)}, bf16[16,16384]{1,0:T(8,128)(2,1)S(1)}, u32[]{:S(2)}, u32[]{:S(2)}) collective-permute-start(bf16[16,16384]{1,0:T(8,128)(2,1)} %get-tuple-element.20), channel_id=1, source_target_pairs={{0,20},{4,16},{8,28},{12,24},{16,4},{20,0},{24,12},{28,8},{1,21},{... | collective-permute-start | bytes 1572872 | tf_op jit(solution)/shard_map/ppermute | solution.py:18
  156.7 79.0 %collective-permute-start.5 = (bf16[16,16384]{1,0:T(8,128)(2,1)}, bf16[16,16384]{1,0:T(8,128)(2,1)}, u32[]{:S(2)}, u32[]{:S(2)}) collective-permute-start(bf16[16,16384]{1,0:T(8,128)(2,1)} %get-tuple-element.21), channel_id=1, source_target_pairs={{0,24},{4,28},{8,16},{12,20},{16,8},{20,12},{24,0},{28,4},{1,25},{... | collective-permute-start | bytes 1572872 | tf_op jit(solution)/shard_map/ppermute | solution.py:18
  158.3 90.9 %collective-permute-start.6 = (bf16[16,16384]{1,0:T(8,128)(2,1)}, bf16[16,16384]{1,0:T(8,128)(2,1)}, u32[]{:S(2)}, u32[]{:S(2)}) collective-permute-start(bf16[16,16384]{1,0:T(8,128)(2,1)} %get-tuple-element.22), channel_id=1, source_target_pairs={{0,28},{4,24},{8,20},{12,16},{16,12},{20,8},{24,4},{28,0},{1,29},{... | collective-permute-start | bytes 1572872 | tf_op jit(solution)/shard_map/ppermute | solution.py:18
  175.5 77.9 %collective-permute-start.21 = (f32[64,768]{1,0:T(8,128)S(1)}, f32[64,768]{1,0:T(8,128)S(1)}, u32[]{:S(2)}, u32[]{:S(2)}) collective-permute-start(f32[64,768]{1,0:T(8,128)S(1)} %slice.21), channel_id=1, source_target_pairs={{0,2},{1,3},{2,0},{3,1},{4,6},{5,7},{6,4},{7,5},{8,10},{9,11},{10,... | collective-permute-start | bytes 589832 | tf_op jit(solution)/shard_map/ppermute | solution.py:18
  (8 other events, 303.3 us)

commit v3 on v2

--- a/solution.py
+++ b/solution.py
@@ -284,13 +284,19 @@
     slots = chunks * capacity
     hot = lax.broadcasted_iota(jnp.int32, (slots, a_ref.shape[0]), 0) == slot_ref[...]
     hot = hot.astype(jnp.float32)
-    filled = jnp.sum(hot, axis=1, keepdims=True) > 0.5
     picked = jnp.dot(
         hot.astype(jnp.bfloat16), a_ref[...], preferred_element_type=jnp.float32
-    )
-    picked = jnp.where(filled, picked, jnp.inf).astype(jnp.bfloat16)
+    ).astype(jnp.bfloat16)
     for chunk in range(chunks):
         outs[chunk][...] = picked[chunk * capacity : (chunk + 1) * capacity]
+
+    @pl.when(pl.program_id(0) == 0)
+    def _():
+        empty = jnp.sum(hot, axis=1, keepdims=True) < 0.5
+        marked = jnp.where(empty, jnp.inf, picked[:, :128].astype(jnp.float32))
+        marked = marked.astype(jnp.bfloat16)
+        for chunk in range(chunks):
+            outs[chunk][:, :128] = marked[chunk * capacity : (chunk + 1) * capacity]
 
 
 def pack_chunks(a_vals, slot_of, chunks, capacity):

time: 255 us -> 255 us (level)
  no operation moved by 1% of the time
where the time goes in v3:
time: 255 us; the launch traced here: 254 us
  waiting for transfers between devices  177 us (69%)
  Pallas kernels  43.4 us (17%)
  starting transfers between devices  19.8 us (8%)
  local copies, waits for them, and re-layouts  9.23 us (4%)
  other arithmetic  3.67 us (1%)
    ppermute x19, waiting for transfers between devices, xor_permute(): return lax.ppermute(value, axis, [(i, i ^ bit) for i in range(count)])  177 us
    pallas_call x2, Pallas kernels, run_products(): pl.pallas_call(functools.partial(body, band, row_count, parts), out_shape...  32 us
    ppermute x19, starting transfers between devices, xor_permute(): return lax.ppermute(value, axis, [(i, i ^ bit) for i in range(count)])  14.7 us
    pallas_call x1, Pallas kernels, pack_chunks(): pl.pallas_call(functools.partial(pack_kernel, chunks, capacity), grid=(ro...  7.2 us
  transfers between devices with their start and end apart: 22, of which 8 were waited for; matrix products, arithmetic and copies ran while one was open for 3% of the time, Pallas kernels for 17%

profile of v3, /device:TPU:22, one launch (start us, length us, event | category | flops | bytes accessed | tf_op | source)
XLA Modules:
  0.0 254.3 jit_solution(17814889304246472829)
XLA Ops:
  0.6 2.9 %reshape.40.refs_1_.refs_4_ = bf16[4096,256]{1,0:T(8,128)(2,1)S(1)} reshape(bf16[64,16384]{1,0:T(8,128)(2,1)} %param.6) | data formatting | bytes 4194304 | tf_op jit(solution)/shard_map/reshape | solution.py:206
  4.2 1.5 collective-permute-start.7
  5.7 46.1 %collective-permute-done.7 = s32[64,4]{0,1:T(4,128)S(1)} collective-permute-done((s32[64,4]{0,1:T(4,128)S(1)}, s32[64,4]{0,1:T(4,128)S(1)}, u32[]{:S(2)}, u32[]{:S(2)}) %collective-permute-start.7) | collective-permute-done | bytes 1056 | tf_op jit(solution)/shard_map/ppermute | solution.py:18
  52.3 4.2 %reshape.39.refs_0_ = bf16[4096,256]{1,0:T(8,128)(2,1)} reshape(bf16[64,16384]{1,0:T(8,128)(2,1)} %a_ref.1) | data formatting | bytes 4194304 | tf_op jit(solution)/shard_map/reshape | solution.py:207
  56.5 2.0 collective-permute-start.15
  59.0 1.3 collective-permute-start.18
  60.3 39.6 %collective-permute-done.13.refs_5_ = bf16[4096,256]{1,0:T(8,128)(2,1)} collective-permute-done((bf16[4096,256]{1,0:T(8,128)(2,1)S(1)}, bf16[4096,256]{1,0:T(8,128)(2,1)}, u32[]{:S(2)}, u32[]{:S(2)}) %collective-permute-start.13) | collective-permute-done | bytes 2097184 | tf_op jit(solution)/shard_map/ppermute | solution.py:18
  99.9 2.3 collective-permute-start.14
  103.1 3.6 %collective-permute-done.9.refs_0_ = bf16[4096,256]{1,0:T(8,128)(2,1)} collective-permute-done((bf16[4096,256]{1,0:T(8,128)(2,1)}, bf16[4096,256]{1,0:T(8,128)(2,1)}, u32[]{:S(2)}, u32[]{:S(2)}) %collective-permute-start.9) | collective-permute-done | bytes 2097184 | tf_op jit(solution)/shard_map/ppermute | solution.py:18
  108.1 7.2 %pack.1 = (bf16[16,16384]{1,0:T(8,128)(2,1)}, bf16[16,16384]{1,0:T(8,128)(2,1)}, bf16[16,16384]{1,0:T(8,128)(2,1)}, bf16[16,16384]{1,0:T(8,128)(2,1)}, bf16[16,1...) custom-call(s32[1,64]{1,0:T(1,128)} %add_bitcast_fusion.slot_ref, ...), custom_call_target="tpu_custom_call" | custom-call | tf_op jit(solution)/shard_map/pack/pallas_call | solution.py:305
  117.6 2.3 collective-permute-start.1
  120.5 16.3 %shard_map.59 = (f32[256,256]{1,0:T(8,128)}, bf16[4096,256]{1,0:T(8,128)(2,1)}, bf16[4096,256]{1,0:T(8,128)(2,1)}) custom-call(s32[512]{0:T(512)} %pad_add_fusion.1.codes, bf16[4096,256]{1,0:T(8,128)(2,1)} %reshape.39.refs_0_, bf16[4096,256]{1,0:T(8,128)(2,1)} %copy-done, bf16[4096,256]{1,0:T(8,128)(2,1)} %collective-permute-done.18.refs_2_, ...), custom_call_target="tpu_custom_call" | custom-call | flops 536870912 | bytes 8388608 | tf_op jit(solution)/shard_map/pallas_call | solution.py:179
  136.8 1.3 copy-done.1
  138.1 15.7 %shard_map.60 = (f32[128,768]{1,0:T(8,128)}, f32[128,768]{1,0:T(8,128)}) custom-call(s32[513]{0:T(1024)} %pad_add_fusion.codes, bf16[4096,256]{1,0:T(8,128)(2,1)} %collective-permute-done.9.refs_0_, bf16[4096,256]{1,0:T(8,128)(2,1)} %collective-permute-done.10.refs_1_, bf16[4096,256]{1,0:T(8,128)(2,1)} %collective-permute-done.11.refs_2_, ...), custom_call_target="tpu_custom_call" | custom-call | flops 536870912 | bytes 21233664 | tf_op jit(solution)/shard_map/pallas_call | solution.py:179
  154.4 2.3 collective-permute-start.4
  156.7 1.8 collective-permute-start.5
  158.5 1.8 collective-permute-start.6
  160.3 1.0 add.156
  161.3 14.4 %collective-permute-done.2.refs_3_ = bf16[16,16384]{1,0:T(8,128)(2,1)S(1)} collective-permute-done((bf16[16,16384]{1,0:T(8,128)(2,1)S(1)}, bf16[16,16384]{1,0:T(8,128)(2,1)S(1)}, u32[]{:S(2)}, u32[]{:S(2)}) %collective-permute-start.2) | collective-permute-done | bytes 524320 | tf_op jit(solution)/shard_map/ppermute | solution.py:18
  175.7 36.3 %collective-permute-done.3.refs_4_ = bf16[16,16384]{1,0:T(8,128)(2,1)S(1)} collective-permute-done((bf16[16,16384]{1,0:T(8,128)(2,1)}, bf16[16,16384]{1,0:T(8,128)(2,1)S(1)}, u32[]{:S(2)}, u32[]{:S(2)}) %collective-permute-start.3) | collective-permute-done | bytes 524320 | tf_op jit(solution)/shard_map/ppermute | solution.py:18
  212.0 11.2 %collective-permute-done.4.refs_5_ = bf16[16,16384]{1,0:T(8,128)(2,1)S(1)} collective-permute-done((bf16[16,16384]{1,0:T(8,128)(2,1)}, bf16[16,16384]{1,0:T(8,128)(2,1)S(1)}, u32[]{:S(2)}, u32[]{:S(2)}) %collective-permute-start.4) | collective-permute-done | bytes 524320 | tf_op jit(solution)/shard_map/ppermute | solution.py:18
  223.3 12.6 %collective-permute-done.5.refs_6_ = bf16[16,16384]{1,0:T(8,128)(2,1)} collective-permute-done((bf16[16,16384]{1,0:T(8,128)(2,1)}, bf16[16,16384]{1,0:T(8,128)(2,1)}, u32[]{:S(2)}, u32[]{:S(2)}) %collective-permute-start.5) | collective-permute-done | bytes 524320 | tf_op jit(solution)/shard_map/ppermute | solution.py:18
  235.9 13.5 %collective-permute-done.6.refs_7_ = bf16[16,16384]{1,0:T(8,128)(2,1)} collective-permute-done((bf16[16,16384]{1,0:T(8,128)(2,1)}, bf16[16,16384]{1,0:T(8,128)(2,1)}, u32[]{:S(2)}, u32[]{:S(2)}) %collective-permute-start.6) | collective-permute-done | bytes 524320 | tf_op jit(solution)/shard_map/ppermute | solution.py:18
  249.4 4.2 %gather_chunks.1 = bf16[64,16384]{1,0:T(8,128)(2,1)} custom-call(s32[1]{0:T(128)} %bitcast.where, bf16[16,16384]{1,0:T(8,128)(2,1)} %get-tuple-element.15.refs_0_, bf16[16,16384]{1,0:T(8,128)(2,1)} %copy-done.2, bf16[16,16384]{1,0:T(8,128)(2,1)} %copy-done.3, bf16[16,16384]{1,0:T(8,128)(2,1)} %copy-done.4, bf16[16,16384]{1,0:T(8,128)(2,1)} %copy-done.5, ...), custom_call_target="tpu_custom_call" | custom-call | tf_op jit(solution)/shard_map/gather_chunks/pallas_call | solution.py:370
  (65 shorter events, 8.2 us)
Async XLA Ops:
  3.5 103.9 %copy-start.8 = (s32[64]{0:T(128)S(1)}, s32[64]{0:T(128)}, u32[]{:S(2)}) copy-start(s32[64]{0:T(128)} %param.7) | copy-start | bytes 772
  3.5 55.5 %collective-permute-start.19 = (bf16[4096,256]{1,0:T(8,128)(2,1)S(1)}, bf16[4096,256]{1,0:T(8,128)(2,1)}, u32[]{:S(2)}, u32[]{:S(2)}) collective-permute-start(bf16[4096,256]{1,0:T(8,128)(2,1)S(1)} %reshape.40.refs_1_.refs_4_), channel_id=1, source_target_pairs={{0,1},{1,0},{2,3},{3,2},{4,5},{5,4},{6,7},{7,6},{8,9},{9,8},{10,11... | collective-permute-start | bytes 6291464 | tf_op jit(solution)/shard_map/ppermute | solution.py:18
  3.6 56.6 %collective-permute-start.10 = (bf16[4096,256]{1,0:T(8,128)(2,1)S(1)}, bf16[4096,256]{1,0:T(8,128)(2,1)}, u32[]{:S(2)}, u32[]{:S(2)}) collective-permute-start(bf16[4096,256]{1,0:T(8,128)(2,1)S(1)} %reshape.40.refs_1_.refs_4_), channel_id=1, source_target_pairs={{0,2},{1,3},{2,0},{3,1},{4,6},{5,7},{6,4},{7,5},{8,10},{9,11},{10,... | collective-permute-start | bytes 6291464 | tf_op jit(solution)/shard_map/ppermute | solution.py:18
  4.2 47.6 %collective-permute-start.7 = (s32[64,4]{0,1:T(4,128)S(1)}, s32[64,4]{0,1:T(4,128)S(1)}, u32[]{:S(2)}, u32[]{:S(2)}) collective-permute-start(s32[64,4]{0,1:T(4,128)S(1)} %copy-done.7), channel_id=1, source_target_pairs={{0,2},{1,3},{2,0},{3,1},{4,6},{5,7},{6,4},{7,5},{8,10},{9,11},{10,... | collective-permute-start | bytes 3080 | tf_op jit(solution)/shard_map/ppermute | solution.py:18
  5.7 50.8 %collective-permute-start.17 = (s32[64,4]{0,1:T(4,128)S(1)}, s32[64,4]{0,1:T(4,128)S(1)}, u32[]{:S(2)}, u32[]{:S(2)}) collective-permute-start(s32[64,4]{0,1:T(4,128)S(1)} %copy-done.7), channel_id=1, source_target_pairs={{0,1},{1,0},{2,3},{3,2},{4,5},{5,4},{6,7},{7,6},{8,9},{9,8},{10,11... | collective-permute-start | bytes 3080 | tf_op jit(solution)/shard_map/ppermute | solution.py:18
  51.8 6.7 %collective-permute-start.8 = (s32[64,4]{0,1:T(4,128)S(1)}, s32[64,4]{0,1:T(4,128)S(1)}, u32[]{:S(2)}, u32[]{:S(2)}) collective-permute-start(s32[64,4]{0,1:T(4,128)S(1)} %collective-permute-done.7), channel_id=1, source_target_pairs={{0,1},{1,0},{2,3},{3,2},{4,5},{5,4},{6,7},{7,6},{8,9},{9,8},{10,11... | collective-permute-start | bytes 3080 | tf_op jit(solution)/shard_map/ppermute | solution.py:18
  51.8 48.1 %collective-permute-start.13 = (bf16[4096,256]{1,0:T(8,128)(2,1)S(1)}, bf16[4096,256]{1,0:T(8,128)(2,1)}, u32[]{:S(2)}, u32[]{:S(2)}) collective-permute-start(bf16[4096,256]{1,0:T(8,128)(2,1)S(1)} %reshape.40.refs_1_.refs_4_), channel_id=1, source_target_pairs={{0,4},{4,0},{8,12},{12,8},{16,20},{20,16},{24,28},{28,24},{1,5},{5... | collective-permute-start | bytes 6291464 | tf_op jit(solution)/shard_map/ppermute | solution.py:18
  56.5 45.8 %collective-permute-start.15 = (bf16[4096,256]{1,0:T(8,128)(2,1)S(1)}, bf16[4096,256]{1,0:T(8,128)(2,1)}, u32[]{:S(2)}, u32[]{:S(2)}) collective-permute-start(bf16[4096,256]{1,0:T(8,128)(2,1)S(1)} %reshape.40.refs_1_.refs_4_), channel_id=1, source_target_pairs={{5,13},{9,1},{13,21},{17,9},{21,29},{25,17},{7,15},{11,3},{15,23},... | collective-permute-start | bytes 6291464 | tf_op jit(solution)/shard_map/ppermute | solution.py:230
  58.5 48.3 %collective-permute-start.9 = (bf16[4096,256]{1,0:T(8,128)(2,1)}, bf16[4096,256]{1,0:T(8,128)(2,1)}, u32[]{:S(2)}, u32[]{:S(2)}) collective-permute-start(bf16[4096,256]{1,0:T(8,128)(2,1)} %reshape.39.refs_0_), channel_id=1, source_target_pairs={{0,2},{1,3},{2,0},{3,1},{4,6},{5,7},{6,4},{7,5},{8,10},{9,11},{10,... | collective-permute-start | bytes 6291464 | tf_op jit(solution)/shard_map/ppermute | solution.py:18
  59.0 57.8 %collective-permute-start.18 = (bf16[4096,256]{1,0:T(8,128)(2,1)}, bf16[4096,256]{1,0:T(8,128)(2,1)}, u32[]{:S(2)}, u32[]{:S(2)}) collective-permute-start(bf16[4096,256]{1,0:T(8,128)(2,1)} %reshape.39.refs_0_), channel_id=1, source_target_pairs={{0,1},{1,0},{2,3},{3,2},{4,5},{5,4},{6,7},{7,6},{8,9},{9,8},{10,11... | collective-permute-start | bytes 6291464 | tf_op jit(solution)/shard_map/ppermute | solution.py:18
  60.3 57.4 %collective-permute-start.12 = (bf16[4096,256]{1,0:T(8,128)(2,1)}, bf16[4096,256]{1,0:T(8,128)(2,1)}, u32[]{:S(2)}, u32[]{:S(2)}) collective-permute-start(bf16[4096,256]{1,0:T(8,128)(2,1)} %collective-permute-done.10.refs_1_), channel_id=1, source_target_pairs={{0,1},{1,0},{2,3},{3,2},{4,5},{5,4},{6,7},{7,6},{8,9},{9,8},{10,11... | collective-permute-start | bytes 6291464 | tf_op jit(solution)/shard_map/ppermute | solution.py:18
  99.9 36.9 %collective-permute-start.14 = (bf16[4096,256]{1,0:T(8,128)(2,1)}, bf16[4096,256]{1,0:T(8,128)(2,1)}, u32[]{:S(2)}, u32[]{:S(2)}) collective-permute-start(bf16[4096,256]{1,0:T(8,128)(2,1)} %collective-permute-done.13.refs_5_), channel_id=1, source_target_pairs={{0,8},{8,16},{12,4},{16,24},{20,12},{28,20},{2,10},{10,18},{14,6},... | collective-permute-start | bytes 6291464 | tf_op jit(solution)/shard_map/ppermute | solution.py:231
  102.3 34.5 %collective-permute-start.16 = (bf16[4096,256]{1,0:T(8,128)(2,1)}, bf16[4096,256]{1,0:T(8,128)(2,1)S(1)}, u32[]{:S(2)}, u32[]{:S(2)}) collective-permute-start(bf16[4096,256]{1,0:T(8,128)(2,1)} %collective-permute-done.15), channel_id=1, source_target_pairs={{1,5},{5,1},{9,13},{13,9},{17,21},{21,17},{25,29},{29,25},{3,7},{7... | collective-permute-start | bytes 6291464 | tf_op jit(solution)/shard_map/ppermute | solution.py:232
  106.7 30.1 %collective-permute-start.11 = (bf16[4096,256]{1,0:T(8,128)(2,1)}, bf16[4096,256]{1,0:T(8,128)(2,1)}, u32[]{:S(2)}, u32[]{:S(2)}) collective-permute-start(bf16[4096,256]{1,0:T(8,128)(2,1)} %collective-permute-done.9.refs_0_), channel_id=1, source_target_pairs={{0,1},{1,0},{2,3},{3,2},{4,5},{5,4},{6,7},{7,6},{8,9},{9,8},{10,11... | collective-permute-start | bytes 6291464 | tf_op jit(solution)/shard_map/ppermute | solution.py:18
  116.8 37.6 %collective-permute-start = (bf16[16,16384]{1,0:T(8,128)(2,1)}, bf16[16,16384]{1,0:T(8,128)(2,1)S(1)}, u32[]{:S(2)}, u32[]{:S(2)}) collective-permute-start(bf16[16,16384]{1,0:T(8,128)(2,1)} %get-tuple-element.16), channel_id=1, source_target_pairs={{0,4},{4,0},{8,12},{12,8},{16,20},{20,16},{24,28},{28,24},{1,5},{5... | collective-permute-start | bytes 1572872 | tf_op jit(solution)/shard_map/ppermute | solution.py:18
  117.6 39.0 %collective-permute-start.1 = (bf16[16,16384]{1,0:T(8,128)(2,1)}, bf16[16,16384]{1,0:T(8,128)(2,1)S(1)}, u32[]{:S(2)}, u32[]{:S(2)}) collective-permute-start(bf16[16,16384]{1,0:T(8,128)(2,1)} %get-tuple-element.17), channel_id=1, source_target_pairs={{0,8},{4,12},{8,0},{12,4},{16,24},{20,28},{24,16},{28,20},{1,9},{5... | collective-permute-start | bytes 1572872 | tf_op jit(solution)/shard_map/ppermute | solution.py:18
  153.9 4.6 %collective-permute-start.20 = (f32[128,768]{1,0:T(8,128)}, f32[128,768]{1,0:T(8,128)S(1)}, u32[]{:S(2)}, u32[]{:S(2)}) collective-permute-start(f32[128,768]{1,0:T(8,128)} %get-tuple-element.27), channel_id=1, source_target_pairs={{0,1},{1,0},{2,3},{3,2},{4,5},{5,4},{6,7},{7,6},{8,9},{9,8},{10,11... | collective-permute-start | bytes 1179656 | tf_op jit(solution)/shard_map/ppermute | solution.py:18
  153.9 21.8 %collective-permute-start.2 = (bf16[16,16384]{1,0:T(8,128)(2,1)S(1)}, bf16[16,16384]{1,0:T(8,128)(2,1)S(1)}, u32[]{:S(2)}, u32[]{:S(2)}) collective-permute-start(bf16[16,16384]{1,0:T(8,128)(2,1)S(1)} %copy-done.9), channel_id=1, source_target_pairs={{0,12},{4,8},{8,4},{12,0},{16,28},{20,24},{24,20},{28,16},{1,13},{... | collective-permute-start | bytes 1572872 | tf_op jit(solution)/shard_map/ppermute | solution.py:18
  154.4 57.6 %collective-permute-start.3 = (bf16[16,16384]{1,0:T(8,128)(2,1)}, bf16[16,16384]{1,0:T(8,128)(2,1)S(1)}, u32[]{:S(2)}, u32[]{:S(2)}) collective-permute-start(bf16[16,16384]{1,0:T(8,128)(2,1)} %get-tuple-element.19), channel_id=1, source_target_pairs={{0,16},{4,20},{8,24},{12,28},{16,0},{20,4},{24,8},{28,12},{1,17},{... | collective-permute-start | bytes 1572872 | tf_op jit(solution)/shard_map/ppermute | solution.py:18
  154.4 94.9 %copy-start.2 = (bf16[16,16384]{1,0:T(8,128)(2,1)}, bf16[16,16384]{1,0:T(8,128)(2,1)S(1)}, u32[]{:S(2)}) copy-start(bf16[16,16384]{1,0:T(8,128)(2,1)S(1)} %collective-permute-done.refs_1_) | copy-start | bytes 1572868
  154.4 68.8 %collective-permute-start.4 = (bf16[16,16384]{1,0:T(8,128)(2,1)}, bf16[16,16384]{1,0:T(8,128)(2,1)S(1)}, u32[]{:S(2)}, u32[]{:S(2)}) collective-permute-start(bf16[16,16384]{1,0:T(8,128)(2,1)} %get-tuple-element.20), channel_id=1, source_target_pairs={{0,20},{4,16},{8,28},{12,24},{16,4},{20,0},{24,12},{28,8},{1,21},{... | collective-permute-start | bytes 1572872 | tf_op jit(solution)/shard_map/ppermute | solution.py:18
  156.7 79.2 %collective-permute-start.5 = (bf16[16,16384]{1,0:T(8,128)(2,1)}, bf16[16,16384]{1,0:T(8,128)(2,1)}, u32[]{:S(2)}, u32[]{:S(2)}) collective-permute-start(bf16[16,16384]{1,0:T(8,128)(2,1)} %get-tuple-element.21), channel_id=1, source_target_pairs={{0,24},{4,28},{8,16},{12,20},{16,8},{20,12},{24,0},{28,4},{1,25},{... | collective-permute-start | bytes 1572872 | tf_op jit(solution)/shard_map/ppermute | solution.py:18
  158.5 90.9 %collective-permute-start.6 = (bf16[16,16384]{1,0:T(8,128)(2,1)}, bf16[16,16384]{1,0:T(8,128)(2,1)}, u32[]{:S(2)}, u32[]{:S(2)}) collective-permute-start(bf16[16,16384]{1,0:T(8,128)(2,1)} %get-tuple-element.22), channel_id=1, source_target_pairs={{0,28},{4,24},{8,20},{12,16},{16,12},{20,8},{24,4},{28,0},{1,29},{... | collective-permute-start | bytes 1572872 | tf_op jit(solution)/shard_map/ppermute | solution.py:18
  175.7 77.9 %collective-permute-start.21 = (f32[64,768]{1,0:T(8,128)S(1)}, f32[64,768]{1,0:T(8,128)S(1)}, u32[]{:S(2)}, u32[]{:S(2)}) collective-permute-start(f32[64,768]{1,0:T(8,128)S(1)} %slice.21), channel_id=1, source_target_pairs={{0,2},{1,3},{2,0},{3,1},{4,6},{5,7},{6,4},{7,5},{8,10},{9,11},{10,... | collective-permute-start | bytes 589832 | tf_op jit(solution)/shard_map/ppermute | solution.py:18
  (8 other events, 303.4 us)

commit v4 on v2

--- a/solution.py
+++ b/solution.py
@@ -48,13 +48,13 @@
     lax.fori_loop(0, sums.shape[0] // rows, step, 0)
 
 
-def scatter_part(band, row_count, offset, code_ref, a_ref, p_ref, sums, order):
-    entries = row_count * band
+def scatter_part(band, row_count, offset, base, code_ref, a_ref, p_ref, sums, order):
+    entries = a_ref.shape[0] // B * band
     span = target_span(row_count)
-    dummy = SLOTS * row_count
+    dummy = base * band * span + SLOTS * row_count
 
     def collect(step, found):
-        code = code_ref[offset + step]
+        code = code_ref[offset + base * band + step]
         order[found] = code
         return found + jnp.where(code >= 0, 1, 0)
 
@@ -68,7 +68,7 @@
             code = order[step * UNROLL + lane]
             target = jnp.bitwise_and(code, span - 1)
             entry = lax.div(code, span)
-            row = lax.div(entry, band)
+            row = lax.div(entry, band) - base
             k = lax.rem(entry, band)
             start = pl.multiple_of(row * B, B)
             half = pl.multiple_of(lax.div(k, 2) * (2 * B), 2 * B)
@@ -90,24 +90,41 @@
     )
 
 
-def early_kernel(band, row_count, parts, codes, *refs):
-    sources, refs = refs[: 2 * parts], refs[2 * parts :]
-    partial, (kept_1, kept_2) = refs[0], refs[1:3]
-    buffers, refs = refs[3 : 3 + 2 * parts], refs[3 + 2 * parts :]
-    sums, order, sems = refs
-    copies = [
-        pltpu.make_async_copy(src, dst, sems.at[i])
-        for i, (src, dst) in enumerate(zip(sources, buffers))
-    ]
-    for copy in copies:
-        copy.start()
+def copies_of(loads, sources, buffers, sems, parity):
+    copies = []
+    for i, (source, start, buffer, at, rows, when) in enumerate(loads):
+        copy = pltpu.make_async_copy(
+            sources[source].at[pl.ds(start, rows), :],
+            buffers[buffer].at[pl.ds(at, rows), :],
+            sems.at[i],
+        )
+        copies.append((copy, when))
+        if when is None:
+            copy.start()
+        else:
+            pl.when(parity == when)(copy.start)
+
+    def wait(i):
+        copy, when = copies[i]
+        if when is None:
+            copy.wait()
+        else:
+            pl.when(parity == when)(copy.wait)
+
+    return wait
+
+
+def early_kernel(band, row_count, loads, inputs, codes, *refs):
+    sources, (partial, kept_1, kept_2), refs = refs[:inputs], refs[inputs : inputs + 3], refs[inputs + 3 :]
+    buffers, (sums, order, sems) = refs[:-3], refs[-3:]
+    wait = copies_of(loads, sources, buffers, sems, None)
     clear(sums)
-    for part in range(parts):
-        copies[2 * part].wait()
-        copies[2 * part + 1].wait()
+    for part in range(2):
+        for i in range(3):
+            wait(3 * part + i)
         a_ref, p_ref = buffers[2 * part : 2 * part + 2]
         scatter_part(
-            band, row_count, part * row_count * band, codes, a_ref, p_ref, sums, order
+            band, row_count, part * row_count * band, 0, codes, a_ref, p_ref, sums, order
         )
     size = row_count * B
     partial[...] = contract(sums[:size].astype(jnp.bfloat16), buffers[1][...])
@@ -115,54 +132,60 @@
     kept_2[...] = sums[2 * size : 3 * size].astype(jnp.bfloat16)
 
 
-def late_kernel(band, row_count, parts, codes, *refs):
-    count = 2 * parts + SLOTS + 3
-    sources, refs = refs[: count + 1], refs[count + 1 :]
-    (keep, send), refs = refs[:2], refs[2:]
-    buffers, refs = refs[:count], refs[count:]
-    sums, order, sems = refs
-    grp_pos = codes[parts * row_count * band]
-    groups = 4
-    share = keep.shape[0] // 2
-    odd_at = 2 * parts + SLOTS
-    sources, other = sources[:odd_at] + sources[odd_at + 1 :], sources[odd_at]
-    copies = [
-        pltpu.make_async_copy(src, dst, sems.at[i])
-        for i, (src, dst) in enumerate(zip(sources, buffers))
-    ]
-    other = pltpu.make_async_copy(other, buffers[odd_at - 1], sems.at[odd_at - 1])
-    for i, copy in enumerate(copies):
-        if i == odd_at - 1:
-            pl.when(lax.rem(grp_pos, 2) == 0)(copy.start)
-            pl.when(lax.rem(grp_pos, 2) == 1)(other.start)
-        else:
-            copy.start()
+def later_sums(band, row_count, base, wait, codes, buffers, sums, order):
     clear(sums)
-    for part in range(parts):
-        copies[2 * part].wait()
-        copies[2 * part + 1].wait()
+    for part in range(2):
+        wait(2 * part)
+        wait(2 * part + 1)
         a_ref, p_ref = buffers[2 * part : 2 * part + 2]
         scatter_part(
-            band, row_count, part * row_count * band, codes, a_ref, p_ref, sums, order
-        )
+            band, row_count, part * row_count * band, base, codes, a_ref, p_ref, sums, order
+        )
+
+
+def mid_kernel(band, row_count, loads, inputs, codes, *refs):
+    sources, result, refs = refs[:inputs], refs[inputs], refs[inputs + 1 :]
+    buffers, (sums, order, sems) = refs[:-3], refs[-3:]
+    parity = lax.rem(codes[2 * row_count * band], 2)
+    wait = copies_of(loads, sources, buffers, sems, parity)
+    later_sums(band, row_count, 0, wait, codes, buffers, sums, order)
+    for i in range(4, len(loads)):
+        wait(i)
     size = row_count * B
-    rest = buffers[2 * parts :]
-    rights, earlier, kept = rest[:SLOTS], rest[SLOTS], rest[SLOTS + 1 :]
-    for copy in copies[2 * parts :]:
-        copy.wait()
-    width = rights[0].shape[1]
+    rights, partial, kept = buffers[4 : 4 + SLOTS], buffers[4 + SLOTS], buffers[5 + SLOTS :]
+    width = partial.shape[1]
     for slot in range(SLOTS):
         right = rights[slot][...]
         here = contract(sums[slot * size : (slot + 1) * size].astype(jnp.bfloat16), right)
         if slot == 0:
-            here = here + earlier[...]
+            here = here + partial[...]
         else:
             here = here + contract(kept[slot - 1][...], right)
-        for block in range(groups):
+        result[:, slot * width : (slot + 1) * width] = here
+
+
+def late_kernel(band, row_count, loads, inputs, codes, *refs):
+    sources, (keep, send), refs = refs[:inputs], refs[inputs : inputs + 2], refs[inputs + 2 :]
+    buffers, (sums, order, sems) = refs[:-3], refs[-3:]
+    grp_pos = codes[2 * row_count * band]
+    wait = copies_of(loads, sources, buffers, sems, lax.rem(grp_pos, 2))
+    later_sums(band, row_count, row_count // 2, wait, codes, buffers, sums, order)
+    for i in range(4, len(loads)):
+        wait(i)
+    size = row_count * B
+    rights, earlier = buffers[4 : 4 + SLOTS], buffers[4 + SLOTS]
+    width = rights[0].shape[1]
+    share = keep.shape[0] // 2
+    for slot in range(SLOTS):
+        columns = slice(slot * width, (slot + 1) * width)
+        here = contract(
+            sums[slot * size : (slot + 1) * size].astype(jnp.bfloat16), rights[slot][...]
+        )
+        here = here + earlier[:, columns]
+        for block in range(width // share):
             piece = here[block * share : (block + 1) * share]
             place = jnp.bitwise_xor(block, grp_pos)
             at = pl.ds(pl.multiple_of(lax.div(place, 2) * share, share), share)
-            columns = slice(slot * width, (slot + 1) * width)
 
             @pl.when(lax.rem(place, 2) == 0)
             def _():
@@ -173,22 +196,22 @@
                 send[at, columns] = piece
 
 
-def run_products(body, codes, arrays, outs, band, row_count, parts, flops, skip=()):
-    width = arrays[1].shape[1]
-    held = [x for i, x in enumerate(arrays) if i not in skip]
+def run_products(body, codes, arrays, loads, buffers, outs, band, row_count, flops):
+    width = arrays[0].shape[1]
+    held = sum(x.size * x.dtype.itemsize for x in buffers) + SLOTS * row_count * B * width * 4
     return pl.pallas_call(
-        functools.partial(body, band, row_count, parts),
+        functools.partial(body, band, row_count, loads, len(arrays)),
         out_shape=outs,
         in_specs=[pl.BlockSpec(memory_space=pltpu.SMEM)]
         + [pl.BlockSpec(memory_space=pl.ANY)] * len(arrays),
         out_specs=jax.tree.map(lambda _: pl.BlockSpec(memory_space=pltpu.VMEM), outs),
-        scratch_shapes=[pltpu.VMEM(x.shape, x.dtype) for x in held]
+        scratch_shapes=[pltpu.VMEM(x.shape, x.dtype) for x in buffers]
         + [
             pltpu.VMEM(((SLOTS * row_count + 2) * B, width), jnp.float32),
             pltpu.SMEM((row_count * band + UNROLL,), jnp.int32),
-            pltpu.SemaphoreType.DMA((len(held),)),
+            pltpu.SemaphoreType.DMA((len(loads),)),
         ],
-        compiler_params=pltpu.CompilerParams(vmem_limit_bytes=56 << 20),
+        compiler_params=pltpu.CompilerParams(vmem_limit_bytes=held + (16 << 20)),
         cost_estimate=pl.CostEstimate(
             flops=flops,
             bytes_accessed=sum(x.size * x.dtype.itemsize for x in arrays),
@@ -204,7 +227,8 @@
     rows_pos, grp_pos = lax.axis_index("rows"), lax.axis_index("grp")
     assert groups == 4 and rows_total % 2 == 0
     p_own = p_vals.reshape(row_count * B, width)
-    a_own = a_vals.reshape(row_count * B, band * B)
+    cut = row_count // 2
+    a_own = [a_vals[i * cut : (i + 1) * cut].reshape(cut * B, band * B) for i in range(2)]
 
     partner = xor_permute(p_own, "rows", 1)
     both = ("rows", "grp")
@@ -235,39 +259,81 @@
     c_near = xor_permute(a_cols, "grp", 1)
     c_last = xor_permute(c_far, "grp", 1)
     p_far = xor_permute(p_own, "grp", 2)
-    a_far = xor_permute(a_own, "grp", 2)
     p_near = xor_permute(p_own, "grp", 1)
-    a_near = xor_permute(a_own, "grp", 1)
     p_last = xor_permute(p_far, "grp", 1)
-    a_last = xor_permute(a_far, "grp", 1)
+    a_far = [xor_permute(a_own[i], "grp", 2) for i in range(2)]
+    a_near = [xor_permute(a_own[i], "grp", 1) for i in range(2)]
+    a_last = [xor_permute(a_far[i], "grp", 1) for i in range(2)]
 
     def codes(*cols):
-        return jnp.concatenate([entry_codes(c, rows_pos, grp_pos, groups) for c in cols])
+        return [entry_codes(c, rows_pos, grp_pos, groups) for c in cols]
 
     flops = 4 * row_count * band * B * B * width // 2
-    kept = jax.ShapeDtypeStruct((row_count * B, width), jnp.bfloat16)
+    full, part = row_count * B, cut * B
+    whole = jax.ShapeDtypeStruct((full, width), jnp.bfloat16)
+    piece = jax.ShapeDtypeStruct((part, width), jnp.bfloat16)
     square = jax.ShapeDtypeStruct((width, width), jnp.float32)
+    wide = jax.ShapeDtypeStruct((width, SLOTS * width), jnp.float32)
+    half = jax.ShapeDtypeStruct((width // 2, SLOTS * width), jnp.float32)
     partial, kept_1, kept_2 = run_products(
         early_kernel,
-        codes(a_cols, c_near),
-        (a_own, p_own, a_near, p_near),
-        (square, kept, kept),
+        jnp.concatenate(codes(a_cols, c_near)),
+        (*a_own, p_own, *a_near, p_near),
+        [
+            (0, 0, 0, 0, part, None),
+            (1, 0, 0, part, part, None),
+            (2, 0, 1, 0, full, None),
+            (3, 0, 2, 0, part, None),
+            (4, 0, 2, part, part, None),
+            (5, 0, 3, 0, full, None),
+        ],
+        [whole] * 4,
+        (square, whole, whole),
         band,
         row_count,
-        2,
         flops,
     )
-    half = jax.ShapeDtypeStruct((width // 2, SLOTS * width), jnp.float32)
+    later_codes = jnp.concatenate([*codes(c_far, c_last), grp_pos.reshape(1)])
+
+    def later_loads(start):
+        return [
+            (0, 0, 0, 0, part, None),
+            (1, start, 1, 0, part, None),
+            (2, 0, 2, 0, part, None),
+            (3, start, 3, 0, part, None),
+            (4, 0, 4, 0, full, None),
+            (5, 0, 5, 0, full, None),
+            (6, 0, 6, 0, full, 0),
+            (7, 0, 6, 0, full, 1),
+        ]
+
+    rights = (p_own, partner, beyond_even, beyond_odd)
+    earlier = run_products(
+        mid_kernel,
+        later_codes,
+        (a_far[0], p_far, a_last[0], p_last, *rights, partial, kept_1, kept_2),
+        later_loads(0)
+        + [
+            (8, 0, 7, 0, width, None),
+            (9, 0, 8, 0, full, None),
+            (10, 0, 9, 0, full, None),
+        ],
+        [piece] * 4 + [whole] * 3 + [square, whole, whole],
+        wide,
+        band,
+        row_count,
+        flops,
+    )
     keep, send = run_products(
         late_kernel,
-        jnp.concatenate([codes(c_far, c_last), grp_pos.reshape(1)]),
-        (a_far, p_far, a_last, p_last, p_own, partner, beyond_even, beyond_odd, partial, kept_1, kept_2),
+        later_codes,
+        (a_far[1], p_far, a_last[1], p_last, *rights, earlier),
+        later_loads(part) + [(8, 0, 7, 0, width, None)],
+        [piece] * 4 + [whole] * 3 + [wide],
         (half, half),
         band,
         row_count,
-        2,
         flops,
-        skip=(4 + SLOTS,),
     )
     share = width // groups
     pair = keep + xor_permute(send, "grp", 1)
@@ -280,33 +346,70 @@
     )
 
 
-def pack_kernel(chunks, capacity, slot_ref, a_ref, *outs):
-    slots = chunks * capacity
-    hot = lax.broadcasted_iota(jnp.int32, (slots, a_ref.shape[0]), 0) == slot_ref[...]
-    hot = hot.astype(jnp.float32)
-    filled = jnp.sum(hot, axis=1, keepdims=True) > 0.5
-    picked = jnp.dot(
-        hot.astype(jnp.bfloat16), a_ref[...], preferred_element_type=jnp.float32
-    )
-    picked = jnp.where(filled, picked, jnp.inf).astype(jnp.bfloat16)
-    for chunk in range(chunks):
-        outs[chunk][...] = picked[chunk * capacity : (chunk + 1) * capacity]
-
-
-def pack_chunks(a_vals, slot_of, chunks, capacity):
+def pack_kernel(names, capacity, pieces, slot_ref, a_hbm, *refs):
+    count = len(names)
+    outs, (a_ref, packed, sems_in, sems_out) = refs[:count], refs[count:]
+    columns = a_ref.shape[1] // pieces
+    loads = [
+        pltpu.make_async_copy(
+            a_hbm.at[:, pl.ds(i * columns, columns)],
+            a_ref.at[:, pl.ds(i * columns, columns)],
+            sems_in.at[i],
+        )
+        for i in range(pieces)
+    ]
+    for copy in loads:
+        copy.start()
+    shape = (capacity, a_ref.shape[0])
+    hot = jnp.concatenate(
+        [
+            (lax.broadcasted_iota(jnp.int32, shape, 0) + name * capacity == slot_ref[...]).astype(
+                jnp.float32
+            )
+            for name in names
+        ],
+        axis=0,
+    )
+    empty = jnp.sum(hot, axis=1, keepdims=True) < 0.5
+    hot = hot.astype(jnp.bfloat16)
+    stores = []
+    for i in range(pieces):
+        loads[i].wait()
+        at = slice(i * columns, (i + 1) * columns)
+        packed[:, at] = jnp.dot(
+            hot, a_ref[:, at], preferred_element_type=jnp.float32
+        ).astype(jnp.bfloat16)
+        if i == 0:
+            first = packed[:, :128].astype(jnp.float32)
+            packed[:, :128] = jnp.where(empty, jnp.inf, first).astype(jnp.bfloat16)
+        for chunk in range(count):
+            copy = pltpu.make_async_copy(
+                packed.at[pl.ds(chunk * capacity, capacity), pl.ds(i * columns, columns)],
+                outs[chunk].at[:, pl.ds(i * columns, columns)],
+                sems_out.at[chunk * pieces + i],
+            )
+            copy.start()
+            stores.append(copy)
+    for copy in stores:
+        copy.wait()
+
+
+def pack_chunks(a_vals, slot_of, names, capacity):
     row_count, row_width = a_vals.shape
-    columns = 2048
-    return pl.pallas_call(
-        functools.partial(pack_kernel, chunks, capacity),
-        grid=(row_width // columns,),
-        out_shape=[jax.ShapeDtypeStruct((capacity, row_width), a_vals.dtype)] * chunks,
-        in_specs=[
-            pl.BlockSpec((1, row_count), lambda i: (0, 0)),
-            pl.BlockSpec((row_count, columns), lambda i: (0, i)),
+    pieces, count = 4, len(names)
+    out = pl.pallas_call(
+        functools.partial(pack_kernel, names, capacity, pieces),
+        out_shape=[jax.ShapeDtypeStruct((capacity, row_width), a_vals.dtype)] * count,
+        in_specs=[pl.BlockSpec(memory_space=pltpu.VMEM), pl.BlockSpec(memory_space=pl.ANY)],
+        out_specs=[pl.BlockSpec(memory_space=pl.ANY)] * count,
+        scratch_shapes=[
+            pltpu.VMEM((row_count, row_width), a_vals.dtype),
+            pltpu.VMEM((count * capacity, row_width), a_vals.dtype),
+            pltpu.SemaphoreType.DMA((pieces,)),
+            pltpu.SemaphoreType.DMA((count * pieces,)),
         ],
-        out_specs=[pl.BlockSpec((capacity, columns), lambda i: (0, i))] * chunks,
-        name="pack",
     )(slot_of[None, :], a_vals)
+    return dict(zip(names, out))
 
 
 def gather_kernel(chunks, capacity, where, *refs):
@@ -394,7 +497,10 @@
     if use_chunks(row_count, rows_total):
         rows_pos = lax.axis_index("rows")
         slot_of = jnp.bitwise_xor(new_rows, rows_pos) * capacity + ranking
-        chunks = pack_chunks(a_vals, slot_of, rows_total, capacity)
+        first = tuple(range(rows_total // 2, rows_total, 2))
+        rest = tuple(i for i in range(rows_total) if i not in first)
+        chunks = pack_chunks(a_vals, slot_of, first, capacity)
+        chunks |= pack_chunks(a_vals, slot_of, rest, capacity)
         incoming = [chunks[0]] + [
             xor_permute(chunks[bit], "rows", bit)
             for bit in range(1, rows_total)

time: 255 us -> 259 us (1.016)
  the two profiles are of different devices: /device:TPU:22 before, /device:TPU:16 now
where the time goes in v4:
time: 259 us
  waiting for transfers between devices  166 us (64%)
  Pallas kernels  43.6 us (17%)
  starting transfers between devices  28.8 us (11%)
  local copies, waits for them, and re-layouts  18.2 us (7%)
    ppermute x22, waiting for transfers between devices, xor_permute(): return lax.ppermute(value, axis, [(i, i ^ bit) for i in range(count)])  166 us
    pallas_call x3, Pallas kernels, run_products(): pl.pallas_call(functools.partial(body, band, row_count, loads, len(arrays...  31.8 us
    ppermute x22, starting transfers between devices, xor_permute(): return lax.ppermute(value, axis, [(i, i ^ bit) for i in range(count)])  21.2 us
    unnamed x26, local copies, waits for them, and re-layouts  9 us
    pallas_call x2, Pallas kernels, pack_chunks(): pl.pallas_call(functools.partial(pack_kernel, names, capacity, pieces), o...  7.53 us
  transfers between devices with their start and end apart: 25, of which 10 were waited for; matrix products, arithmetic and copies ran while one was open for 3% of the time, Pallas kernels for 17%

profile of v4, /device:TPU:16, one launch (start us, length us, event | category | flops | bytes accessed | tf_op | source)
XLA Modules:
  0.0 258.9 jit_solution(10835979333546440461)
XLA Ops:
  0.6 2.6 %fusion.38 = (bf16[32,16384]{1,0:T(8,128)(2,1)S(1)}, bf16[32,16384]{1,0:T(8,128)(2,1)}) fusion(bf16[64,16384]{1,0:T(8,128)(2,1)} %a_hbm.3), kind=kLoop, calls=%fused_computation.101 | loop fusion | bytes 4194304 | tf_op jit(solution)/shard_map/slice | solution.py:231
  3.9 2.9 %reshape.43.refs_2_.refs_4_ = bf16[4096,256]{1,0:T(8,128)(2,1)S(1)} reshape(bf16[64,16384]{1,0:T(8,128)(2,1)} %param.6) | data formatting | bytes 4194304 | tf_op jit(solution)/shard_map/reshape | solution.py:229
  9.9 2.0 collective-permute-start.15
  12.4 42.6 %collective-permute-done.7 = s32[64,4]{0,1:T(4,128)S(1)} collective-permute-done((s32[64,4]{0,1:T(4,128)S(1)}, s32[64,4]{0,1:T(4,128)S(1)}, u32[]{:S(2)}, u32[]{:S(2)}) %collective-permute-start.7) | collective-permute-done | bytes 1056 | tf_op jit(solution)/shard_map/ppermute | solution.py:18
  56.3 2.3 reshape.42.refs_1_
  62.9 21.5 %collective-permute-done.17.refs_0_ = bf16[2048,256]{1,0:T(8,128)(2,1)} collective-permute-done((bf16[2048,256]{1,0:T(8,128)(2,1)S(1)}, bf16[2048,256]{1,0:T(8,128)(2,1)}, u32[]{:S(2)}, u32[]{:S(2)}) %collective-permute-start.17) | collective-permute-done | bytes 1048608 | tf_op jit(solution)/shard_map/ppermute | solution.py:18
  85.9 3.5 %collective-permute-start.14 = (bf16[4096,256]{1,0:T(8,128)(2,1)}, bf16[4096,256]{1,0:T(8,128)(2,1)}, u32[]{:S(2)}, u32[]{:S(2)}) collective-permute-start(bf16[4096,256]{1,0:T(8,128)(2,1)} %collective-permute-done.13.refs_5_), channel_id=1, source_target_pairs={{0,8},{8,16},{12,4},{16,24},{20,12},{28,20},{2,10},{10,18},{14,6},... | collective-permute-start | bytes 6291464 | tf_op jit(solution)/shard_map/ppermute | solution.py:255
  89.4 2.0 collective-permute-start.16
  91.4 17.7 %collective-permute-done.9.refs_0_ = bf16[2048,256]{1,0:T(8,128)(2,1)} collective-permute-done((bf16[2048,256]{1,0:T(8,128)(2,1)}, bf16[2048,256]{1,0:T(8,128)(2,1)}, u32[]{:S(2)}, u32[]{:S(2)}) %collective-permute-start.9) | collective-permute-done | bytes 1048608 | tf_op jit(solution)/shard_map/ppermute | solution.py:18
  111.6 4.2 %shard_map.59 = (bf16[16,16384]{1,0:T(8,128)(2,1)}, bf16[16,16384]{1,0:T(8,128)(2,1)}, bf16[16,16384]{1,0:T(8,128)(2,1)}, bf16[16,16384]{1,0:T(8,128)(2,1)}, bf1...) custom-call(s32[1,64]{1,0:T(1,128)} %add_bitcast_fusion.slot_ref, bf16[64,16384]{1,0:T(8,128)(2,1)} %a_hbm.3), custom_call_target="tpu_custom_call" | custom-call | tf_op jit(solution)/shard_map/pallas_call | solution.py:400
  121.1 1.6 copy-done.2
  124.0 14.3 %shard_map.61 = (f32[256,256]{1,0:T(8,128)S(1)}, bf16[4096,256]{1,0:T(8,128)(2,1)S(1)}, bf16[4096,256]{1,0:T(8,128)(2,1)S(1)}) custom-call(s32[512]{0:T(512)S(1)} %pad_add_fusion.1.codes, bf16[2048,256]{1,0:T(8,128)(2,1)S(1)} %reshape.44.refs_0_, bf16[2048,256]{1,0:T(8,128)(2,1)S(1)} %copy-done, bf16[4096,256]{1,0:T(8,128)(2,1)S(1)} %reshape.43.refs_2_.refs_4_, ...), custom_call_target="tpu_custom_call" | custom-call | flops 536870912 | bytes 8388608 | tf_op jit(solution)/shard_map/pallas_call | solution.py:202
  140.9 8.4 %shard_map.62.refs_8_ = f32[256,768]{1,0:T(8,128)S(1)} custom-call(s32[513]{0:T(1024)S(1)} %pad_add_fusion.codes, bf16[2048,256]{1,0:T(8,128)(2,1)} %collective-permute-done.17.refs_0_, bf16[4096,256]{1,0:T(8,128)(2,1)} %collective-permute-done.10.refs_1_, bf16[2048,256]{1,0:T(8,128)(2,1)} %collective-permute-done.18.refs_2_, ...), custom_call_target="tpu_custom_call" | custom-call | flops 536870912 | bytes 19136512 | tf_op jit(solution)/shard_map/pallas_call | solution.py:202
  149.4 9.1 %shard_map.63 = (f32[128,768]{1,0:T(8,128)S(1)}, f32[128,768]{1,0:T(8,128)S(1)}) custom-call(s32[513]{0:T(1024)S(1)} %pad_add_fusion.codes, bf16[2048,256]{1,0:T(8,128)(2,1)} %collective-permute-done.9.refs_0_, bf16[4096,256]{1,0:T(8,128)(2,1)} %collective-permute-done.10.refs_1_, bf16[2048,256]{1,0:T(8,128)(2,1)} %collective-permute-done.11.refs_2_, ...), custom_call_target="tpu_custom_call" | custom-call | flops 536870912 | bytes 15466496 | tf_op jit(solution)/shard_map/pallas_call | solution.py:202
  160.1 3.3 %shard_map.60 = (bf16[16,16384]{1,0:T(8,128)(2,1)}, bf16[16,16384]{1,0:T(8,128)(2,1)}) custom-call(s32[1,64]{1,0:T(1,128)} %add_bitcast_fusion.slot_ref, bf16[64,16384]{1,0:T(8,128)(2,1)} %a_hbm.3), custom_call_target="tpu_custom_call" | custom-call | tf_op jit(solution)/shard_map/pallas_call | solution.py:400
  163.4 2.3 collective-permute-start.6
  165.7 1.6 collective-permute-start.3
  168.9 10.1 %collective-permute-done.2.refs_3_ = bf16[16,16384]{1,0:T(8,128)(2,1)S(1)} collective-permute-done((bf16[16,16384]{1,0:T(8,128)(2,1)}, bf16[16,16384]{1,0:T(8,128)(2,1)S(1)}, u32[]{:S(2)}, u32[]{:S(2)}) %collective-permute-start.2) | collective-permute-done | bytes 524320 | tf_op jit(solution)/shard_map/ppermute | solution.py:18
  179.0 3.0 %collective-permute-start.24 = (f32[64,768]{1,0:T(8,128)S(1)}, f32[64,768]{1,0:T(8,128)S(1)}, u32[]{:S(2)}, u32[]{:S(2)}) collective-permute-start(f32[64,768]{1,0:T(8,128)S(1)} %slice.29), channel_id=1, source_target_pairs={{0,2},{1,3},{2,0},{3,1},{4,6},{5,7},{6,4},{7,5},{8,10},{9,11},{10,... | collective-permute-start | bytes 589832 | tf_op jit(solution)/shard_map/ppermute | solution.py:18
  182.0 35.7 %collective-permute-done.4.refs_5_ = bf16[16,16384]{1,0:T(8,128)(2,1)S(1)} collective-permute-done((bf16[16,16384]{1,0:T(8,128)(2,1)}, bf16[16,16384]{1,0:T(8,128)(2,1)S(1)}, u32[]{:S(2)}, u32[]{:S(2)}) %collective-permute-start.4) | collective-permute-done | bytes 524320 | tf_op jit(solution)/shard_map/ppermute | solution.py:18
  217.7 14.7 %collective-permute-done.6.refs_7_ = bf16[16,16384]{1,0:T(8,128)(2,1)S(1)} collective-permute-done((bf16[16,16384]{1,0:T(8,128)(2,1)}, bf16[16,16384]{1,0:T(8,128)(2,1)S(1)}, u32[]{:S(2)}, u32[]{:S(2)}) %collective-permute-start.6) | collective-permute-done | bytes 524320 | tf_op jit(solution)/shard_map/ppermute | solution.py:18
  232.3 7.8 %collective-permute-done.3.refs_4_ = bf16[16,16384]{1,0:T(8,128)(2,1)S(1)} collective-permute-done((bf16[16,16384]{1,0:T(8,128)(2,1)}, bf16[16,16384]{1,0:T(8,128)(2,1)S(1)}, u32[]{:S(2)}, u32[]{:S(2)}) %collective-permute-start.3) | collective-permute-done | bytes 524320 | tf_op jit(solution)/shard_map/ppermute | solution.py:18
  240.1 13.8 %collective-permute-done.5.refs_6_ = bf16[16,16384]{1,0:T(8,128)(2,1)} collective-permute-done((bf16[16,16384]{1,0:T(8,128)(2,1)}, bf16[16,16384]{1,0:T(8,128)(2,1)}, u32[]{:S(2)}, u32[]{:S(2)}) %collective-permute-start.5) | collective-permute-done | bytes 524320 | tf_op jit(solution)/shard_map/ppermute | solution.py:18
  254.0 4.2 %gather_chunks.1 = bf16[64,16384]{1,0:T(8,128)(2,1)} custom-call(s32[1]{0:T(128)} %bitcast.where, bf16[16,16384]{1,0:T(8,128)(2,1)} %get-tuple-element.15.refs_0_, bf16[16,16384]{1,0:T(8,128)(2,1)} %collective-permute-done.refs_1_, bf16[16,16384]{1,0:T(8,128)(2,1)} %collective-permute-done.1.refs_2_, bf16[16,16384]{1,0:T(8,128)(2,1)} %copy-done.7, ...), custom_call_target="tpu_custom_call" | custom-call | tf_op jit(solution)/shard_map/gather_chunks/pallas_call | solution.py:467
  (81 shorter events, 26.9 us)
Async XLA Ops:
  3.8 55.2 %collective-permute-start.20 = (bf16[2048,256]{1,0:T(8,128)(2,1)S(1)}, bf16[2048,256]{1,0:T(8,128)(2,1)}, u32[]{:S(2)}, u32[]{:S(2)}) collective-permute-start(bf16[2048,256]{1,0:T(8,128)(2,1)S(1)} %reshape.44.refs_0_), channel_id=1, source_target_pairs={{0,1},{1,0},{2,3},{3,2},{4,5},{5,4},{6,7},{7,6},{8,9},{9,8},{10,11... | collective-permute-start | bytes 3145736 | tf_op jit(solution)/shard_map/ppermute | solution.py:18
  6.8 79.1 %collective-permute-start.10 = (bf16[4096,256]{1,0:T(8,128)(2,1)S(1)}, bf16[4096,256]{1,0:T(8,128)(2,1)}, u32[]{:S(2)}, u32[]{:S(2)}) collective-permute-start(bf16[4096,256]{1,0:T(8,128)(2,1)S(1)} %reshape.43.refs_2_.refs_4_), channel_id=1, source_target_pairs={{0,2},{1,3},{2,0},{3,1},{4,6},{5,7},{6,4},{7,5},{8,10},{9,11},{10,... | collective-permute-start | bytes 6291464 | tf_op jit(solution)/shard_map/ppermute | solution.py:18
  8.3 77.5 %collective-permute-start.13 = (bf16[4096,256]{1,0:T(8,128)(2,1)S(1)}, bf16[4096,256]{1,0:T(8,128)(2,1)}, u32[]{:S(2)}, u32[]{:S(2)}) collective-permute-start(bf16[4096,256]{1,0:T(8,128)(2,1)S(1)} %reshape.43.refs_2_.refs_4_), channel_id=1, source_target_pairs={{0,4},{4,0},{8,12},{12,8},{16,20},{20,16},{24,28},{28,24},{1,5},{5... | collective-permute-start | bytes 6291464 | tf_op jit(solution)/shard_map/ppermute | solution.py:18
  9.9 79.5 %collective-permute-start.15 = (bf16[4096,256]{1,0:T(8,128)(2,1)S(1)}, bf16[4096,256]{1,0:T(8,128)(2,1)}, u32[]{:S(2)}, u32[]{:S(2)}) collective-permute-start(bf16[4096,256]{1,0:T(8,128)(2,1)S(1)} %reshape.43.refs_2_.refs_4_), channel_id=1, source_target_pairs={{5,13},{9,1},{13,21},{17,9},{21,29},{25,17},{7,15},{11,3},{15,23},... | collective-permute-start | bytes 6291464 | tf_op jit(solution)/shard_map/ppermute | solution.py:254
  11.9 43.1 %collective-permute-start.7 = (s32[64,4]{0,1:T(4,128)S(1)}, s32[64,4]{0,1:T(4,128)S(1)}, u32[]{:S(2)}, u32[]{:S(2)}) collective-permute-start(s32[64,4]{0,1:T(4,128)S(1)} %copy-done.11), channel_id=1, source_target_pairs={{0,2},{1,3},{2,0},{3,1},{4,6},{5,7},{6,4},{7,5},{8,10},{9,11},{10,... | collective-permute-start | bytes 3080 | tf_op jit(solution)/shard_map/ppermute | solution.py:18
  56.2 2.5 collective-permute-start.8
  58.7 2.9 %collective-permute-start.21 = (bf16[2048,256]{1,0:T(8,128)(2,1)}, bf16[2048,256]{1,0:T(8,128)(2,1)S(1)}, u32[]{:S(2)}, u32[]{:S(2)}) collective-permute-start(bf16[2048,256]{1,0:T(8,128)(2,1)} %reshape.42.refs_1_), channel_id=1, source_target_pairs={{0,1},{1,0},{2,3},{3,2},{4,5},{5,4},{6,7},{7,6},{8,9},{9,8},{10,11... | collective-permute-start | bytes 3145736 | tf_op jit(solution)/shard_map/ppermute | solution.py:18
  59.0 25.3 %collective-permute-start.17 = (bf16[2048,256]{1,0:T(8,128)(2,1)S(1)}, bf16[2048,256]{1,0:T(8,128)(2,1)}, u32[]{:S(2)}, u32[]{:S(2)}) collective-permute-start(bf16[2048,256]{1,0:T(8,128)(2,1)S(1)} %reshape.44.refs_0_), channel_id=1, source_target_pairs={{0,2},{1,3},{2,0},{3,1},{4,6},{5,7},{6,4},{7,5},{8,10},{9,11},{10,... | collective-permute-start | bytes 3145736 | tf_op jit(solution)/shard_map/ppermute | solution.py:18
  62.5 46.5 %collective-permute-start.22 = (bf16[4096,256]{1,0:T(8,128)(2,1)S(1)}, bf16[4096,256]{1,0:T(8,128)(2,1)S(1)}, u32[]{:S(2)}, u32[]{:S(2)}) collective-permute-start(bf16[4096,256]{1,0:T(8,128)(2,1)S(1)} %reshape.43.refs_2_.refs_4_), channel_id=1, source_target_pairs={{0,1},{1,0},{2,3},{3,2},{4,5},{5,4},{6,7},{7,6},{8,9},{9,8},{10,11... | collective-permute-start | bytes 6291464 | tf_op jit(solution)/shard_map/ppermute | solution.py:18
  84.4 24.7 %collective-permute-start.9 = (bf16[2048,256]{1,0:T(8,128)(2,1)}, bf16[2048,256]{1,0:T(8,128)(2,1)}, u32[]{:S(2)}, u32[]{:S(2)}) collective-permute-start(bf16[2048,256]{1,0:T(8,128)(2,1)} %reshape.42.refs_1_), channel_id=1, source_target_pairs={{0,2},{1,3},{2,0},{3,1},{4,6},{5,7},{6,4},{7,5},{8,10},{9,11},{10,... | collective-permute-start | bytes 3145736 | tf_op jit(solution)/shard_map/ppermute | solution.py:18
  85.9 32.5 %collective-permute-start.12 = (bf16[4096,256]{1,0:T(8,128)(2,1)}, bf16[4096,256]{1,0:T(8,128)(2,1)}, u32[]{:S(2)}, u32[]{:S(2)}) collective-permute-start(bf16[4096,256]{1,0:T(8,128)(2,1)} %collective-permute-done.10.refs_1_), channel_id=1, source_target_pairs={{0,1},{1,0},{2,3},{3,2},{4,5},{5,4},{6,7},{7,6},{8,9},{9,8},{10,11... | collective-permute-start | bytes 6291464 | tf_op jit(solution)/shard_map/ppermute | solution.py:18
  85.9 55.0 %collective-permute-start.14 = (bf16[4096,256]{1,0:T(8,128)(2,1)}, bf16[4096,256]{1,0:T(8,128)(2,1)}, u32[]{:S(2)}, u32[]{:S(2)}) collective-permute-start(bf16[4096,256]{1,0:T(8,128)(2,1)} %collective-permute-done.13.refs_5_), channel_id=1, source_target_pairs={{0,8},{8,16},{12,4},{16,24},{20,12},{28,20},{2,10},{10,18},{14,6},... | collective-permute-start | bytes 6291464 | tf_op jit(solution)/shard_map/ppermute | solution.py:255
  89.4 51.5 %collective-permute-start.16 = (bf16[4096,256]{1,0:T(8,128)(2,1)}, bf16[4096,256]{1,0:T(8,128)(2,1)}, u32[]{:S(2)}, u32[]{:S(2)}) collective-permute-start(bf16[4096,256]{1,0:T(8,128)(2,1)} %collective-permute-done.15), channel_id=1, source_target_pairs={{1,5},{5,1},{9,13},{13,9},{17,21},{21,17},{25,29},{29,25},{3,7},{7... | collective-permute-start | bytes 6291464 | tf_op jit(solution)/shard_map/ppermute | solution.py:256
  109.0 7.7 %collective-permute-start.18 = (bf16[2048,256]{1,0:T(8,128)(2,1)}, bf16[2048,256]{1,0:T(8,128)(2,1)}, u32[]{:S(2)}, u32[]{:S(2)}) collective-permute-start(bf16[2048,256]{1,0:T(8,128)(2,1)} %collective-permute-done.17.refs_0_), channel_id=1, source_target_pairs={{0,1},{1,0},{2,3},{3,2},{4,5},{5,4},{6,7},{7,6},{8,9},{9,8},{10,11... | collective-permute-start | bytes 3145736 | tf_op jit(solution)/shard_map/ppermute | solution.py:18
  110.4 39.0 %collective-permute-start.11 = (bf16[2048,256]{1,0:T(8,128)(2,1)}, bf16[2048,256]{1,0:T(8,128)(2,1)}, u32[]{:S(2)}, u32[]{:S(2)}) collective-permute-start(bf16[2048,256]{1,0:T(8,128)(2,1)} %collective-permute-done.9.refs_0_), channel_id=1, source_target_pairs={{0,1},{1,0},{2,3},{3,2},{4,5},{5,4},{6,7},{7,6},{8,9},{9,8},{10,11... | collective-permute-start | bytes 3145736 | tf_op jit(solution)/shard_map/ppermute | solution.py:18
  116.7 46.7 %collective-permute-start = (bf16[16,16384]{1,0:T(8,128)(2,1)}, bf16[16,16384]{1,0:T(8,128)(2,1)}, u32[]{:S(2)}, u32[]{:S(2)}) collective-permute-start(bf16[16,16384]{1,0:T(8,128)(2,1)} %get-tuple-element.16), channel_id=1, source_target_pairs={{0,4},{4,0},{8,12},{12,8},{16,20},{20,16},{24,28},{28,24},{1,5},{5... | collective-permute-start | bytes 1572872 | tf_op jit(solution)/shard_map/ppermute | solution.py:18
  118.3 47.4 %collective-permute-start.1 = (bf16[16,16384]{1,0:T(8,128)(2,1)}, bf16[16,16384]{1,0:T(8,128)(2,1)}, u32[]{:S(2)}, u32[]{:S(2)}) collective-permute-start(bf16[16,16384]{1,0:T(8,128)(2,1)} %get-tuple-element.17), channel_id=1, source_target_pairs={{0,8},{4,12},{8,0},{12,4},{16,24},{20,28},{24,16},{28,20},{1,9},{5... | collective-permute-start | bytes 1572872 | tf_op jit(solution)/shard_map/ppermute | solution.py:18
  158.5 8.9 %collective-permute-start.23 = (f32[128,768]{1,0:T(8,128)S(1)}, f32[128,768]{1,0:T(8,128)S(1)}, u32[]{:S(2)}, u32[]{:S(2)}) collective-permute-start(f32[128,768]{1,0:T(8,128)S(1)} %get-tuple-element.27), channel_id=1, source_target_pairs={{0,1},{1,0},{2,3},{3,2},{4,5},{5,4},{6,7},{7,6},{8,9},{9,8},{10,11... | collective-permute-start | bytes 1179656 | tf_op jit(solution)/shard_map/ppermute | solution.py:18
  158.5 20.5 %collective-permute-start.2 = (bf16[16,16384]{1,0:T(8,128)(2,1)}, bf16[16,16384]{1,0:T(8,128)(2,1)S(1)}, u32[]{:S(2)}, u32[]{:S(2)}) collective-permute-start(bf16[16,16384]{1,0:T(8,128)(2,1)} %get-tuple-element.18), channel_id=1, source_target_pairs={{0,12},{4,8},{8,4},{12,0},{16,28},{20,24},{24,20},{28,16},{1,13},{... | collective-permute-start | bytes 1572872 | tf_op jit(solution)/shard_map/ppermute | solution.py:18
  158.6 59.1 %collective-permute-start.4 = (bf16[16,16384]{1,0:T(8,128)(2,1)}, bf16[16,16384]{1,0:T(8,128)(2,1)S(1)}, u32[]{:S(2)}, u32[]{:S(2)}) collective-permute-start(bf16[16,16384]{1,0:T(8,128)(2,1)} %get-tuple-element.20), channel_id=1, source_target_pairs={{0,20},{4,16},{8,28},{12,24},{16,4},{20,0},{24,12},{28,8},{1,21},{... | collective-permute-start | bytes 1572872 | tf_op jit(solution)/shard_map/ppermute | solution.py:18
  163.4 68.9 %collective-permute-start.6 = (bf16[16,16384]{1,0:T(8,128)(2,1)}, bf16[16,16384]{1,0:T(8,128)(2,1)S(1)}, u32[]{:S(2)}, u32[]{:S(2)}) collective-permute-start(bf16[16,16384]{1,0:T(8,128)(2,1)} %get-tuple-element.22), channel_id=1, source_target_pairs={{0,28},{4,24},{8,20},{12,16},{16,12},{20,8},{24,4},{28,0},{1,29},{... | collective-permute-start | bytes 1572872 | tf_op jit(solution)/shard_map/ppermute | solution.py:18
  165.7 74.4 %collective-permute-start.3 = (bf16[16,16384]{1,0:T(8,128)(2,1)}, bf16[16,16384]{1,0:T(8,128)(2,1)S(1)}, u32[]{:S(2)}, u32[]{:S(2)}) collective-permute-start(bf16[16,16384]{1,0:T(8,128)(2,1)} %get-tuple-element.19), channel_id=1, source_target_pairs={{0,16},{4,20},{8,24},{12,28},{16,0},{20,4},{24,8},{28,12},{1,17},{... | collective-permute-start | bytes 1572872 | tf_op jit(solution)/shard_map/ppermute | solution.py:18
  167.3 86.6 %collective-permute-start.5 = (bf16[16,16384]{1,0:T(8,128)(2,1)}, bf16[16,16384]{1,0:T(8,128)(2,1)}, u32[]{:S(2)}, u32[]{:S(2)}) collective-permute-start(bf16[16,16384]{1,0:T(8,128)(2,1)} %get-tuple-element.21), channel_id=1, source_target_pairs={{0,24},{4,28},{8,16},{12,20},{16,8},{20,12},{24,0},{28,4},{1,25},{... | collective-permute-start | bytes 1572872 | tf_op jit(solution)/shard_map/ppermute | solution.py:18
  179.0 79.2 %collective-permute-start.24 = (f32[64,768]{1,0:T(8,128)S(1)}, f32[64,768]{1,0:T(8,128)S(1)}, u32[]{:S(2)}, u32[]{:S(2)}) collective-permute-start(f32[64,768]{1,0:T(8,128)S(1)} %slice.29), channel_id=1, source_target_pairs={{0,2},{1,3},{2,0},{3,1},{4,6},{5,7},{6,4},{7,5},{8,10},{9,11},{10,... | collective-permute-start | bytes 589832 | tf_op jit(solution)/shard_map/ppermute | solution.py:18
  (14 other events, 269.1 us)

commit v5 on v4

--- a/solution.py
+++ b/solution.py
@@ -412,33 +412,49 @@
     return dict(zip(names, out))
 
 
-def gather_kernel(chunks, capacity, where, *refs):
-    sources, (target, probe, buffer, sems_probe, sems_in, sems_out) = refs[:chunks], refs[chunks:]
-    probes = [
-        pltpu.make_async_copy(
-            sources[c].at[:, pl.ds(0, probe.shape[2])], probe.at[c], sems_probe.at[c]
-        )
-        for c in range(chunks)
-    ]
-    for copy in probes:
-        copy.start()
+def toward(position, bit):
+    return (position % 2 == 0) == ((position ^ bit) > position)
+
+
+def gather_kernel(names, split, capacity, where, *refs):
+    chunks, total = len(names), len(names) + len(split)
+    sources, (target, probe, buffer, sems_probe, sems_in, sems_out) = refs[:total], refs[total:]
+    me = where[0]
+    even = jnp.where(lax.rem(me, 2) == 0, 1, 0)
+
+    def each(c, make, act):
+        if names[c] not in split:
+            act(make(sources[c]))
+            return
+        above = jnp.where(me > jnp.bitwise_xor(me, names[c]), 1, 0)
+        other = sources[chunks + split.index(names[c])]
+        pl.when(even == above)(lambda: act(make(sources[c])))
+        pl.when(even != above)(lambda: act(make(other)))
+
+    def probes(c):
+        return lambda source: pltpu.make_async_copy(
+            source.at[:, pl.ds(0, probe.shape[2])], probe.at[c], sems_probe.at[c]
+        )
+
+    for c in range(chunks):
+        each(c, probes(c), lambda copy: copy.start())
     full = []
     for c in range(chunks):
-        probes[c].wait()
+        each(c, probes(c), lambda copy: copy.wait())
         full.append(jnp.where(jnp.max(probe[c].astype(jnp.float32)) < jnp.inf, 1, 0))
     limit = target.shape[0] // capacity - 1
     place = []
     for c in range(chunks):
-        sender = jnp.bitwise_xor(where[0], c)
+        sender = jnp.bitwise_xor(me, names[c])
         ahead = jnp.int32(0)
         for other in range(chunks):
-            first = jnp.bitwise_xor(where[0], other) < sender
+            first = jnp.bitwise_xor(me, names[other]) < sender
             ahead = ahead + jnp.where(first, full[other], 0)
         place.append(pl.multiple_of(jnp.minimum(ahead, limit) * capacity, capacity))
 
     def loads(c):
-        return pltpu.make_async_copy(
-            sources[c], buffer.at[pl.ds(place[c], capacity), :], sems_in.at[c]
+        return lambda source: pltpu.make_async_copy(
+            source, buffer.at[pl.ds(place[c], capacity), :], sems_in.at[c]
         )
 
     def stores(c):
@@ -449,26 +465,30 @@
         )
 
     for c in range(chunks):
-        pl.when(full[c] == 1)(lambda c=c: loads(c).start())
+        @pl.when(full[c] == 1)
+        def _():
+            each(c, loads(c), lambda copy: copy.start())
+
     for c in range(chunks):
         @pl.when(full[c] == 1)
         def _():
-            loads(c).wait()
+            each(c, loads(c), lambda copy: copy.wait())
             stores(c).start()
 
     for c in range(chunks):
         pl.when(full[c] == 1)(lambda c=c: stores(c).wait())
 
 
-def gather_chunks(incoming, rows_pos, row_count):
-    chunks = len(incoming)
+def gather_chunks(incoming, others, rows_pos, row_count):
+    names, split = tuple(incoming), tuple(others)
+    chunks = len(names)
     capacity, row_width = incoming[0].shape
     dtype = incoming[0].dtype
     return pl.pallas_call(
-        functools.partial(gather_kernel, chunks, capacity),
+        functools.partial(gather_kernel, names, split, capacity),
         out_shape=jax.ShapeDtypeStruct((row_count, row_width), dtype),
         in_specs=[pl.BlockSpec(memory_space=pltpu.SMEM)]
-        + [pl.BlockSpec(memory_space=pl.ANY)] * chunks,
+        + [pl.BlockSpec(memory_space=pl.ANY)] * (chunks + len(split)),
         out_specs=pl.BlockSpec(memory_space=pl.ANY),
         scratch_shapes=[
             pltpu.VMEM((chunks, capacity, 128), dtype),
@@ -478,7 +498,7 @@
             pltpu.SemaphoreType.DMA((chunks,)),
         ],
         name="gather_chunks",
-    )(rows_pos.astype(jnp.int32).reshape(1), *incoming)
+    )(rows_pos.astype(jnp.int32).reshape(1), *incoming.values(), *others.values())
 
 
 def use_chunks(row_count, rows_total):
@@ -501,11 +521,15 @@
         rest = tuple(i for i in range(rows_total) if i not in first)
         chunks = pack_chunks(a_vals, slot_of, first, capacity)
         chunks |= pack_chunks(a_vals, slot_of, rest, capacity)
-        incoming = [chunks[0]] + [
-            xor_permute(chunks[bit], "rows", bit)
-            for bit in range(1, rows_total)
-        ]
-        return gather_chunks(incoming, rows_pos, row_count)
+        incoming, others = {0: chunks[0]}, {}
+        for bit in range(1, rows_total):
+            pairs = [(i, i ^ bit) for i in range(rows_total)]
+            if bit in first:
+                back = [pair for pair in pairs if not toward(pair[0], bit)]
+                pairs = [pair for pair in pairs if toward(pair[0], bit)]
+                others[bit] = lax.ppermute(chunks[bit], "rows", back)
+            incoming[bit] = lax.ppermute(chunks[bit], "rows", pairs)
+        return gather_chunks(incoming, others, rows_pos, row_count)
     slot_of = new_rows * capacity + ranking
     slot_ids = jnp.arange(slot_total, dtype=jnp.int32)
     sender = slot_ids[:, None] == slot_of[None, :]

time: 259 us -> 240 us (0.927)
  the two profiles are of different devices: /device:TPU:16 before, /device:TPU:12 now
where the time goes in v5:
time: 240 us; the launch traced here: 239 us
  waiting for transfers between devices  139 us (58%)
  Pallas kernels  43.6 us (18%)
  starting transfers between devices  35.2 us (15%)
  local copies, waits for them, and re-layouts  19.2 us (8%)
    ppermute x15, waiting for transfers between devices, xor_permute(): return lax.ppermute(value, axis, [(i, i ^ bit) for i in range(count)])  86.1 us
    ppermute x7, waiting for transfers between devices, migrate(): incoming[bit] = lax.ppermute(chunks[bit], 'rows', pairs)  52.6 us
    pallas_call x3, Pallas kernels, run_products(): pl.pallas_call(functools.partial(body, band, row_count, loads, len(arrays...  31.7 us
    ppermute x2, starting transfers between devices, migrate(): others[bit] = lax.ppermute(chunks[bit], 'rows', back)  10.9 us
    unnamed x26, local copies, waits for them, and re-layouts  10 us
    ppermute x7, starting transfers between devices, migrate(): incoming[bit] = lax.ppermute(chunks[bit], 'rows', pairs)  9.37 us
    ppermute x15, starting transfers between devices, xor_permute(): return lax.ppermute(value, axis, [(i, i ^ bit) for i in range(count)])  8.54 us
    pallas_call x2, Pallas kernels, pack_chunks(): pl.pallas_call(functools.partial(pack_kernel, names, capacity, pieces), o...  7.66 us
  transfers between devices with their start and end apart: 27, of which 7 were waited for; matrix products, arithmetic and copies ran while one was open for 3% of the time, Pallas kernels for 18%

profile of v5, /device:TPU:12, one launch (start us, length us, event | category | flops | bytes accessed | tf_op | source)
XLA Modules:
  0.0 239.2 jit_solution(3307388528297590628)
XLA Ops:
  0.6 2.6 %fusion.38 = (bf16[32,16384]{1,0:T(8,128)(2,1)S(1)}, bf16[32,16384]{1,0:T(8,128)(2,1)}) fusion(bf16[64,16384]{1,0:T(8,128)(2,1)} %a_hbm.3), kind=kLoop, calls=%fused_computation.101 | loop fusion | bytes 4194304 | tf_op jit(solution)/shard_map/slice | solution.py:231
  3.9 2.9 %reshape.43.refs_2_.refs_4_ = bf16[4096,256]{1,0:T(8,128)(2,1)S(1)} reshape(bf16[64,16384]{1,0:T(8,128)(2,1)} %param.6) | data formatting | bytes 4194304 | tf_op jit(solution)/shard_map/reshape | solution.py:229
  6.8 1.6 collective-permute-start.12
  8.8 2.0 collective-permute-start.17
  11.4 43.6 %collective-permute-done.9 = s32[64,4]{0,1:T(4,128)S(1)} collective-permute-done((s32[64,4]{0,1:T(4,128)S(1)}, s32[64,4]{0,1:T(4,128)S(1)}, u32[]{:S(2)}, u32[]{:S(2)}) %collective-permute-start.9) | collective-permute-done | bytes 1056 | tf_op jit(solution)/shard_map/ppermute | solution.py:18
  56.3 2.3 reshape.42.refs_1_
  59.0 1.5 collective-permute-start.19
  62.9 21.5 %collective-permute-done.19.refs_0_ = bf16[2048,256]{1,0:T(8,128)(2,1)} collective-permute-done((bf16[2048,256]{1,0:T(8,128)(2,1)S(1)}, bf16[2048,256]{1,0:T(8,128)(2,1)}, u32[]{:S(2)}, u32[]{:S(2)}) %collective-permute-start.19) | collective-permute-done | bytes 1048608 | tf_op jit(solution)/shard_map/ppermute | solution.py:18
  85.9 2.4 collective-permute-start.16
  88.3 2.0 collective-permute-start.18
  90.3 18.8 %collective-permute-done.11.refs_0_ = bf16[2048,256]{1,0:T(8,128)(2,1)} collective-permute-done((bf16[2048,256]{1,0:T(8,128)(2,1)}, bf16[2048,256]{1,0:T(8,128)(2,1)}, u32[]{:S(2)}, u32[]{:S(2)}) %collective-permute-start.11) | collective-permute-done | bytes 1048608 | tf_op jit(solution)/shard_map/ppermute | solution.py:18
  111.7 4.3 %shard_map.59 = (bf16[16,16384]{1,0:T(8,128)(2,1)}, bf16[16,16384]{1,0:T(8,128)(2,1)}, bf16[16,16384]{1,0:T(8,128)(2,1)}, bf16[16,16384]{1,0:T(8,128)(2,1)}, bf1...) custom-call(s32[1,64]{1,0:T(1,128)} %add_bitcast_fusion.slot_ref, bf16[64,16384]{1,0:T(8,128)(2,1)} %a_hbm.3), custom_call_target="tpu_custom_call" | custom-call | tf_op jit(solution)/shard_map/pallas_call | solution.py:400
  117.7 2.8 %collective-permute-start.2 = (bf16[16,16384]{1,0:T(8,128)(2,1)}, bf16[16,16384]{1,0:T(8,128)(2,1)}, u32[]{:S(2)}, u32[]{:S(2)}) collective-permute-start(bf16[16,16384]{1,0:T(8,128)(2,1)} %get-tuple-element.18), channel_id=1, source_target_pairs={{0,12},{4,8},{8,4},{12,0},{16,28},{20,24},{24,20},{28,16},{1,13},{... | collective-permute-start | bytes 1572872 | tf_op jit(solution)/shard_map/ppermute | solution.py:531
  120.5 2.5 %collective-permute-start.4 = (bf16[16,16384]{1,0:T(8,128)(2,1)}, bf16[16,16384]{1,0:T(8,128)(2,1)}, u32[]{:S(2)}, u32[]{:S(2)}) collective-permute-start(bf16[16,16384]{1,0:T(8,128)(2,1)} %get-tuple-element.20), channel_id=1, source_target_pairs={{0,20},{4,16},{8,28},{12,24},{16,4},{20,0},{24,12},{28,8},{1,21},{... | collective-permute-start | bytes 1572872 | tf_op jit(solution)/shard_map/ppermute | solution.py:531
  124.3 1.6 copy-done.2
  127.1 13.5 %shard_map.61 = (f32[256,256]{1,0:T(8,128)S(1)}, bf16[4096,256]{1,0:T(8,128)(2,1)S(1)}, bf16[4096,256]{1,0:T(8,128)(2,1)S(1)}) custom-call(s32[512]{0:T(512)S(1)} %pad_add_fusion.1.codes, bf16[2048,256]{1,0:T(8,128)(2,1)S(1)} %reshape.44.refs_0_, bf16[2048,256]{1,0:T(8,128)(2,1)S(1)} %copy-done, bf16[4096,256]{1,0:T(8,128)(2,1)S(1)} %reshape.43.refs_2_.refs_4_, ...), custom_call_target="tpu_custom_call" | custom-call | flops 536870912 | bytes 8388608 | tf_op jit(solution)/shard_map/pallas_call | solution.py:202
  143.2 8.9 %shard_map.62.refs_8_ = f32[256,768]{1,0:T(8,128)S(1)} custom-call(s32[513]{0:T(1024)S(1)} %pad_add_fusion.codes, bf16[2048,256]{1,0:T(8,128)(2,1)} %collective-permute-done.19.refs_0_, bf16[4096,256]{1,0:T(8,128)(2,1)} %collective-permute-done.12.refs_1_, bf16[2048,256]{1,0:T(8,128)(2,1)} %collective-permute-done.20.refs_2_, ...), custom_call_target="tpu_custom_call" | custom-call | flops 536870912 | bytes 19136512 | tf_op jit(solution)/shard_map/pallas_call | solution.py:202
  152.1 9.4 %shard_map.63 = (f32[128,768]{1,0:T(8,128)S(1)}, f32[128,768]{1,0:T(8,128)}) custom-call(s32[513]{0:T(1024)S(1)} %pad_add_fusion.codes, bf16[2048,256]{1,0:T(8,128)(2,1)} %collective-permute-done.11.refs_0_, bf16[4096,256]{1,0:T(8,128)(2,1)} %collective-permute-done.12.refs_1_, bf16[2048,256]{1,0:T(8,128)(2,1)} %collective-permute-done.13.refs_2_, ...), custom_call_target="tpu_custom_call" | custom-call | flops 536870912 | bytes 15466496 | tf_op jit(solution)/shard_map/pallas_call | solution.py:202
  162.8 3.4 %shard_map.60 = (bf16[16,16384]{1,0:T(8,128)(2,1)}, bf16[16,16384]{1,0:T(8,128)(2,1)}) custom-call(s32[1,64]{1,0:T(1,128)} %add_bitcast_fusion.slot_ref, bf16[64,16384]{1,0:T(8,128)(2,1)} %a_hbm.3), custom_call_target="tpu_custom_call" | custom-call | tf_op jit(solution)/shard_map/pallas_call | solution.py:400
  167.5 5.5 %collective-permute-start.7 = (bf16[16,16384]{1,0:T(8,128)(2,1)}, bf16[16,16384]{1,0:T(8,128)(2,1)S(1)}, u32[]{:S(2)}, u32[]{:S(2)}) collective-permute-start(bf16[16,16384]{1,0:T(8,128)(2,1)} %get-tuple-element.19), channel_id=1, source_target_pairs={{4,20},{12,28},{16,0},{24,8},{5,21},{13,29},{17,1},{25,9},{6,22},{... | collective-permute-start | bytes 1572872 | tf_op jit(solution)/shard_map/ppermute | solution.py:530
  174.4 5.4 %collective-permute-start.8 = (bf16[16,16384]{1,0:T(8,128)(2,1)}, bf16[16,16384]{1,0:T(8,128)(2,1)}, u32[]{:S(2)}, u32[]{:S(2)}) collective-permute-start(bf16[16,16384]{1,0:T(8,128)(2,1)} %get-tuple-element.21), channel_id=1, source_target_pairs={{4,28},{12,20},{16,8},{24,0},{5,29},{13,21},{17,9},{25,1},{6,30},{... | collective-permute-start | bytes 1572872 | tf_op jit(solution)/shard_map/ppermute | solution.py:530
  179.8 32.0 %collective-permute-done.6.refs_7_ = bf16[16,16384]{1,0:T(8,128)(2,1)S(1)} collective-permute-done((bf16[16,16384]{1,0:T(8,128)(2,1)}, bf16[16,16384]{1,0:T(8,128)(2,1)S(1)}, u32[]{:S(2)}, u32[]{:S(2)}) %collective-permute-start.6) | collective-permute-done | bytes 524320 | tf_op jit(solution)/shard_map/ppermute | solution.py:531
  212.7 20.6 %collective-permute-done.5.refs_6_ = bf16[16,16384]{1,0:T(8,128)(2,1)S(1)} collective-permute-done((bf16[16,16384]{1,0:T(8,128)(2,1)}, bf16[16,16384]{1,0:T(8,128)(2,1)S(1)}, u32[]{:S(2)}, u32[]{:S(2)}) %collective-permute-start.5) | collective-permute-done | bytes 524320 | tf_op jit(solution)/shard_map/ppermute | solution.py:531
  234.3 4.2 %gather_chunks.1 = bf16[64,16384]{1,0:T(8,128)(2,1)} custom-call(s32[1]{0:T(128)} %bitcast.where, bf16[16,16384]{1,0:T(8,128)(2,1)} %get-tuple-element.15.refs_0_, bf16[16,16384]{1,0:T(8,128)(2,1)} %collective-permute-done.refs_1_, bf16[16,16384]{1,0:T(8,128)(2,1)} %collective-permute-done.1.refs_2_, bf16[16,16384]{1,0:T(8,128)(2,1)} %collective-permute-done.2.refs_3_, ...), custom_call_target="tpu_custom_call" | custom-call | tf_op jit(solution)/shard_map/gather_chunks/pallas_call | solution.py:487
  (85 shorter events, 23.1 us)
Async XLA Ops:
  3.8 55.2 %collective-permute-start.22 = (bf16[2048,256]{1,0:T(8,128)(2,1)S(1)}, bf16[2048,256]{1,0:T(8,128)(2,1)}, u32[]{:S(2)}, u32[]{:S(2)}) collective-permute-start(bf16[2048,256]{1,0:T(8,128)(2,1)S(1)} %reshape.44.refs_0_), channel_id=1, source_target_pairs={{0,1},{1,0},{2,3},{3,2},{4,5},{5,4},{6,7},{7,6},{8,9},{9,8},{10,11... | collective-permute-start | bytes 3145736 | tf_op jit(solution)/shard_map/ppermute | solution.py:18
  6.8 79.1 %collective-permute-start.12 = (bf16[4096,256]{1,0:T(8,128)(2,1)S(1)}, bf16[4096,256]{1,0:T(8,128)(2,1)}, u32[]{:S(2)}, u32[]{:S(2)}) collective-permute-start(bf16[4096,256]{1,0:T(8,128)(2,1)S(1)} %reshape.43.refs_2_.refs_4_), channel_id=1, source_target_pairs={{0,2},{1,3},{2,0},{3,1},{4,6},{5,7},{6,4},{7,5},{8,10},{9,11},{10,... | collective-permute-start | bytes 6291464 | tf_op jit(solution)/shard_map/ppermute | solution.py:18
  8.3 77.5 %collective-permute-start.15 = (bf16[4096,256]{1,0:T(8,128)(2,1)S(1)}, bf16[4096,256]{1,0:T(8,128)(2,1)}, u32[]{:S(2)}, u32[]{:S(2)}) collective-permute-start(bf16[4096,256]{1,0:T(8,128)(2,1)S(1)} %reshape.43.refs_2_.refs_4_), channel_id=1, source_target_pairs={{0,4},{4,0},{8,12},{12,8},{16,20},{20,16},{24,28},{28,24},{1,5},{5... | collective-permute-start | bytes 6291464 | tf_op jit(solution)/shard_map/ppermute | solution.py:18
  8.8 79.4 %collective-permute-start.17 = (bf16[4096,256]{1,0:T(8,128)(2,1)S(1)}, bf16[4096,256]{1,0:T(8,128)(2,1)}, u32[]{:S(2)}, u32[]{:S(2)}) collective-permute-start(bf16[4096,256]{1,0:T(8,128)(2,1)S(1)} %reshape.43.refs_2_.refs_4_), channel_id=1, source_target_pairs={{5,13},{9,1},{13,21},{17,9},{21,29},{25,17},{7,15},{11,3},{15,23},... | collective-permute-start | bytes 6291464 | tf_op jit(solution)/shard_map/ppermute | solution.py:254
  10.9 44.1 %collective-permute-start.9 = (s32[64,4]{0,1:T(4,128)S(1)}, s32[64,4]{0,1:T(4,128)S(1)}, u32[]{:S(2)}, u32[]{:S(2)}) collective-permute-start(s32[64,4]{0,1:T(4,128)S(1)} %copy-done.11), channel_id=1, source_target_pairs={{0,2},{1,3},{2,0},{3,1},{4,6},{5,7},{6,4},{7,5},{8,10},{9,11},{10,... | collective-permute-start | bytes 3080 | tf_op jit(solution)/shard_map/ppermute | solution.py:18
  59.0 25.3 %collective-permute-start.19 = (bf16[2048,256]{1,0:T(8,128)(2,1)S(1)}, bf16[2048,256]{1,0:T(8,128)(2,1)}, u32[]{:S(2)}, u32[]{:S(2)}) collective-permute-start(bf16[2048,256]{1,0:T(8,128)(2,1)S(1)} %reshape.44.refs_0_), channel_id=1, source_target_pairs={{0,2},{1,3},{2,0},{3,1},{4,6},{5,7},{6,4},{7,5},{8,10},{9,11},{10,... | collective-permute-start | bytes 3145736 | tf_op jit(solution)/shard_map/ppermute | solution.py:18
  62.5 46.5 %collective-permute-start.24 = (bf16[4096,256]{1,0:T(8,128)(2,1)S(1)}, bf16[4096,256]{1,0:T(8,128)(2,1)S(1)}, u32[]{:S(2)}, u32[]{:S(2)}) collective-permute-start(bf16[4096,256]{1,0:T(8,128)(2,1)S(1)} %reshape.43.refs_2_.refs_4_), channel_id=1, source_target_pairs={{0,1},{1,0},{2,3},{3,2},{4,5},{5,4},{6,7},{7,6},{8,9},{9,8},{10,11... | collective-permute-start | bytes 6291464 | tf_op jit(solution)/shard_map/ppermute | solution.py:18
  84.4 24.7 %collective-permute-start.11 = (bf16[2048,256]{1,0:T(8,128)(2,1)}, bf16[2048,256]{1,0:T(8,128)(2,1)}, u32[]{:S(2)}, u32[]{:S(2)}) collective-permute-start(bf16[2048,256]{1,0:T(8,128)(2,1)} %reshape.42.refs_1_), channel_id=1, source_target_pairs={{0,2},{1,3},{2,0},{3,1},{4,6},{5,7},{6,4},{7,5},{8,10},{9,11},{10,... | collective-permute-start | bytes 3145736 | tf_op jit(solution)/shard_map/ppermute | solution.py:18
  85.9 31.6 %collective-permute-start.14 = (bf16[4096,256]{1,0:T(8,128)(2,1)}, bf16[4096,256]{1,0:T(8,128)(2,1)}, u32[]{:S(2)}, u32[]{:S(2)}) collective-permute-start(bf16[4096,256]{1,0:T(8,128)(2,1)} %collective-permute-done.12.refs_1_), channel_id=1, source_target_pairs={{0,1},{1,0},{2,3},{3,2},{4,5},{5,4},{6,7},{7,6},{8,9},{9,8},{10,11... | collective-permute-start | bytes 6291464 | tf_op jit(solution)/shard_map/ppermute | solution.py:18
  85.9 31.8 %collective-permute-start.16 = (bf16[4096,256]{1,0:T(8,128)(2,1)}, bf16[4096,256]{1,0:T(8,128)(2,1)}, u32[]{:S(2)}, u32[]{:S(2)}) collective-permute-start(bf16[4096,256]{1,0:T(8,128)(2,1)} %collective-permute-done.15.refs_5_), channel_id=1, source_target_pairs={{0,8},{8,16},{12,4},{16,24},{20,12},{28,20},{2,10},{10,18},{14,6},... | collective-permute-start | bytes 6291464 | tf_op jit(solution)/shard_map/ppermute | solution.py:255
  88.3 32.2 %collective-permute-start.18 = (bf16[4096,256]{1,0:T(8,128)(2,1)}, bf16[4096,256]{1,0:T(8,128)(2,1)}, u32[]{:S(2)}, u32[]{:S(2)}) collective-permute-start(bf16[4096,256]{1,0:T(8,128)(2,1)} %collective-permute-done.17), channel_id=1, source_target_pairs={{1,5},{5,1},{9,13},{13,9},{17,21},{21,17},{25,29},{29,25},{3,7},{7... | collective-permute-start | bytes 6291464 | tf_op jit(solution)/shard_map/ppermute | solution.py:256
  109.1 7.8 %collective-permute-start.20 = (bf16[2048,256]{1,0:T(8,128)(2,1)}, bf16[2048,256]{1,0:T(8,128)(2,1)}, u32[]{:S(2)}, u32[]{:S(2)}) collective-permute-start(bf16[2048,256]{1,0:T(8,128)(2,1)} %collective-permute-done.19.refs_0_), channel_id=1, source_target_pairs={{0,1},{1,0},{2,3},{3,2},{4,5},{5,4},{6,7},{7,6},{8,9},{9,8},{10,11... | collective-permute-start | bytes 3145736 | tf_op jit(solution)/shard_map/ppermute | solution.py:18
  110.4 41.7 %collective-permute-start.13 = (bf16[2048,256]{1,0:T(8,128)(2,1)}, bf16[2048,256]{1,0:T(8,128)(2,1)}, u32[]{:S(2)}, u32[]{:S(2)}) collective-permute-start(bf16[2048,256]{1,0:T(8,128)(2,1)} %collective-permute-done.11.refs_0_), channel_id=1, source_target_pairs={{0,1},{1,0},{2,3},{3,2},{4,5},{5,4},{6,7},{7,6},{8,9},{9,8},{10,11... | collective-permute-start | bytes 3145736 | tf_op jit(solution)/shard_map/ppermute | solution.py:18
  116.8 45.3 %collective-permute-start = (bf16[16,16384]{1,0:T(8,128)(2,1)}, bf16[16,16384]{1,0:T(8,128)(2,1)}, u32[]{:S(2)}, u32[]{:S(2)}) collective-permute-start(bf16[16,16384]{1,0:T(8,128)(2,1)} %get-tuple-element.16), channel_id=1, source_target_pairs={{0,4},{4,0},{8,12},{12,8},{16,20},{20,16},{24,28},{28,24},{1,5},{5... | collective-permute-start | bytes 1572872 | tf_op jit(solution)/shard_map/ppermute | solution.py:531
  117.5 48.8 %collective-permute-start.1 = (bf16[16,16384]{1,0:T(8,128)(2,1)}, bf16[16,16384]{1,0:T(8,128)(2,1)}, u32[]{:S(2)}, u32[]{:S(2)}) collective-permute-start(bf16[16,16384]{1,0:T(8,128)(2,1)} %get-tuple-element.17), channel_id=1, source_target_pairs={{0,8},{4,12},{8,0},{12,4},{16,24},{20,28},{24,16},{28,20},{1,9},{5... | collective-permute-start | bytes 1572872 | tf_op jit(solution)/shard_map/ppermute | solution.py:531
  117.7 49.8 %collective-permute-start.2 = (bf16[16,16384]{1,0:T(8,128)(2,1)}, bf16[16,16384]{1,0:T(8,128)(2,1)}, u32[]{:S(2)}, u32[]{:S(2)}) collective-permute-start(bf16[16,16384]{1,0:T(8,128)(2,1)} %get-tuple-element.18), channel_id=1, source_target_pairs={{0,12},{4,8},{8,4},{12,0},{16,28},{20,24},{24,20},{28,16},{1,13},{... | collective-permute-start | bytes 1572872 | tf_op jit(solution)/shard_map/ppermute | solution.py:531
  120.5 52.6 %collective-permute-start.4 = (bf16[16,16384]{1,0:T(8,128)(2,1)}, bf16[16,16384]{1,0:T(8,128)(2,1)}, u32[]{:S(2)}, u32[]{:S(2)}) collective-permute-start(bf16[16,16384]{1,0:T(8,128)(2,1)} %get-tuple-element.20), channel_id=1, source_target_pairs={{0,20},{4,16},{8,28},{12,24},{16,4},{20,0},{24,12},{28,8},{1,21},{... | collective-permute-start | bytes 1572872 | tf_op jit(solution)/shard_map/ppermute | solution.py:531
  161.5 12.8 %collective-permute-start.25 = (f32[128,768]{1,0:T(8,128)}, f32[128,768]{1,0:T(8,128)S(1)}, u32[]{:S(2)}, u32[]{:S(2)}) collective-permute-start(f32[128,768]{1,0:T(8,128)} %get-tuple-element.27), channel_id=1, source_target_pairs={{0,1},{1,0},{2,3},{3,2},{4,5},{5,4},{6,7},{7,6},{8,9},{9,8},{10,11... | collective-permute-start | bytes 1179656 | tf_op jit(solution)/shard_map/ppermute | solution.py:18
  162.2 49.6 %collective-permute-start.6 = (bf16[16,16384]{1,0:T(8,128)(2,1)}, bf16[16,16384]{1,0:T(8,128)(2,1)S(1)}, u32[]{:S(2)}, u32[]{:S(2)}) collective-permute-start(bf16[16,16384]{1,0:T(8,128)(2,1)} %get-tuple-element.22), channel_id=1, source_target_pairs={{0,28},{4,24},{8,20},{12,16},{16,12},{20,8},{24,4},{28,0},{1,29},{... | collective-permute-start | bytes 1572872 | tf_op jit(solution)/shard_map/ppermute | solution.py:531
  166.2 46.5 %collective-permute-start.3 = (bf16[16,16384]{1,0:T(8,128)(2,1)}, bf16[16,16384]{1,0:T(8,128)(2,1)S(1)}, u32[]{:S(2)}, u32[]{:S(2)}) collective-permute-start(bf16[16,16384]{1,0:T(8,128)(2,1)} %get-tuple-element.19), channel_id=1, source_target_pairs={{0,16},{8,24},{20,4},{28,12},{1,17},{9,25},{21,5},{29,13},{2,18},{... | collective-permute-start | bytes 1572872 | tf_op jit(solution)/shard_map/ppermute | solution.py:531
  167.5 65.8 %collective-permute-start.7 = (bf16[16,16384]{1,0:T(8,128)(2,1)}, bf16[16,16384]{1,0:T(8,128)(2,1)S(1)}, u32[]{:S(2)}, u32[]{:S(2)}) collective-permute-start(bf16[16,16384]{1,0:T(8,128)(2,1)} %get-tuple-element.19), channel_id=1, source_target_pairs={{4,20},{12,28},{16,0},{24,8},{5,21},{13,29},{17,1},{25,9},{6,22},{... | collective-permute-start | bytes 1572872 | tf_op jit(solution)/shard_map/ppermute | solution.py:530
  173.1 60.2 %collective-permute-start.5 = (bf16[16,16384]{1,0:T(8,128)(2,1)}, bf16[16,16384]{1,0:T(8,128)(2,1)S(1)}, u32[]{:S(2)}, u32[]{:S(2)}) collective-permute-start(bf16[16,16384]{1,0:T(8,128)(2,1)} %get-tuple-element.21), channel_id=1, source_target_pairs={{0,24},{8,16},{20,12},{28,4},{1,25},{9,17},{21,13},{29,5},{2,26},{... | collective-permute-start | bytes 1572872 | tf_op jit(solution)/shard_map/ppermute | solution.py:531
  174.4 58.9 %collective-permute-start.8 = (bf16[16,16384]{1,0:T(8,128)(2,1)}, bf16[16,16384]{1,0:T(8,128)(2,1)}, u32[]{:S(2)}, u32[]{:S(2)}) collective-permute-start(bf16[16,16384]{1,0:T(8,128)(2,1)} %get-tuple-element.21), channel_id=1, source_target_pairs={{4,28},{12,20},{16,8},{24,0},{5,29},{13,21},{17,9},{25,1},{6,30},{... | collective-permute-start | bytes 1572872 | tf_op jit(solution)/shard_map/ppermute | solution.py:530
  211.8 26.7 %collective-permute-start.26 = (f32[64,768]{1,0:T(8,128)S(1)}, f32[64,768]{1,0:T(8,128)S(1)}, u32[]{:S(2)}, u32[]{:S(2)}) collective-permute-start(f32[64,768]{1,0:T(8,128)S(1)} %slice.29), channel_id=1, source_target_pairs={{0,2},{1,3},{2,0},{3,1},{4,6},{5,7},{6,4},{7,5},{8,10},{9,11},{10,... | collective-permute-start | bytes 589832 | tf_op jit(solution)/shard_map/ppermute | solution.py:18
  (16 other events, 170.7 us)

commit v6 on v4

--- a/solution.py
+++ b/solution.py
@@ -90,34 +90,23 @@
     )
 
 
-def copies_of(loads, sources, buffers, sems, parity):
+def copies_of(loads, sources, buffers, sems):
     copies = []
-    for i, (source, start, buffer, at, rows, when) in enumerate(loads):
+    for i, (source, start, buffer, at, rows) in enumerate(loads):
         copy = pltpu.make_async_copy(
             sources[source].at[pl.ds(start, rows), :],
             buffers[buffer].at[pl.ds(at, rows), :],
             sems.at[i],
         )
-        copies.append((copy, when))
-        if when is None:
-            copy.start()
-        else:
-            pl.when(parity == when)(copy.start)
-
-    def wait(i):
-        copy, when = copies[i]
-        if when is None:
-            copy.wait()
-        else:
-            pl.when(parity == when)(copy.wait)
-
-    return wait
+        copies.append(copy)
+        copy.start()
+    return lambda i: copies[i].wait()
 
 
 def early_kernel(band, row_count, loads, inputs, codes, *refs):
     sources, (partial, kept_1, kept_2), refs = refs[:inputs], refs[inputs : inputs + 3], refs[inputs + 3 :]
     buffers, (sums, order, sems) = refs[:-3], refs[-3:]
-    wait = copies_of(loads, sources, buffers, sems, None)
+    wait = copies_of(loads, sources, buffers, sems)
     clear(sums)
     for part in range(2):
         for i in range(3):
@@ -127,9 +116,15 @@
             band, row_count, part * row_count * band, 0, codes, a_ref, p_ref, sums, order
         )
     size = row_count * B
+    stores = []
+    for slot, kept in ((1, kept_1), (2, kept_2)):
+        staged = buffers[2 * (slot - 1)]
+        staged[...] = sums[slot * size : (slot + 1) * size].astype(jnp.bfloat16)
+        stores.append(pltpu.make_async_copy(staged, kept, sems.at[len(loads) + slot - 1]))
+        stores[-1].start()
     partial[...] = contract(sums[:size].astype(jnp.bfloat16), buffers[1][...])
-    kept_1[...] = sums[size : 2 * size].astype(jnp.bfloat16)
-    kept_2[...] = sums[2 * size : 3 * size].astype(jnp.bfloat16)
+    for copy in stores:
+        copy.wait()
 
 
 def later_sums(band, row_count, base, wait, codes, buffers, sums, order):
@@ -146,8 +141,7 @@
 def mid_kernel(band, row_count, loads, inputs, codes, *refs):
     sources, result, refs = refs[:inputs], refs[inputs], refs[inputs + 1 :]
     buffers, (sums, order, sems) = refs[:-3], refs[-3:]
-    parity = lax.rem(codes[2 * row_count * band], 2)
-    wait = copies_of(loads, sources, buffers, sems, parity)
+    wait = copies_of(loads, sources, buffers, sems)
     later_sums(band, row_count, 0, wait, codes, buffers, sums, order)
     for i in range(4, len(loads)):
         wait(i)
@@ -168,7 +162,7 @@
     sources, (keep, send), refs = refs[:inputs], refs[inputs : inputs + 2], refs[inputs + 2 :]
     buffers, (sums, order, sems) = refs[:-3], refs[-3:]
     grp_pos = codes[2 * row_count * band]
-    wait = copies_of(loads, sources, buffers, sems, lax.rem(grp_pos, 2))
+    wait = copies_of(loads, sources, buffers, sems)
     later_sums(band, row_count, row_count // 2, wait, codes, buffers, sums, order)
     for i in range(4, len(loads)):
         wait(i)
@@ -196,22 +190,22 @@
                 send[at, columns] = piece
 
 
-def run_products(body, codes, arrays, loads, buffers, outs, band, row_count, flops):
+def run_products(body, codes, arrays, loads, buffers, outs, band, row_count, flops, out_specs=None):
     width = arrays[0].shape[1]
-    held = sum(x.size * x.dtype.itemsize for x in buffers) + SLOTS * row_count * B * width * 4
     return pl.pallas_call(
         functools.partial(body, band, row_count, loads, len(arrays)),
         out_shape=outs,
         in_specs=[pl.BlockSpec(memory_space=pltpu.SMEM)]
-        + [pl.BlockSpec(memory_space=pl.ANY)] * len(arrays),
-        out_specs=jax.tree.map(lambda _: pl.BlockSpec(memory_space=pltpu.VMEM), outs),
+        + [pl.BlockSpec(memory_space=pltpu.HBM)] * len(arrays),
+        out_specs=out_specs
+        or jax.tree.map(lambda _: pl.BlockSpec(memory_space=pltpu.VMEM), outs),
         scratch_shapes=[pltpu.VMEM(x.shape, x.dtype) for x in buffers]
         + [
             pltpu.VMEM(((SLOTS * row_count + 2) * B, width), jnp.float32),
             pltpu.SMEM((row_count * band + UNROLL,), jnp.int32),
-            pltpu.SemaphoreType.DMA((len(loads),)),
+            pltpu.SemaphoreType.DMA((len(loads) + 2,)),
         ],
-        compiler_params=pltpu.CompilerParams(vmem_limit_bytes=held + (16 << 20)),
+        compiler_params=pltpu.CompilerParams(vmem_limit_bytes=60 << 20),
         cost_estimate=pl.CostEstimate(
             flops=flops,
             bytes_accessed=sum(x.size * x.dtype.itemsize for x in arrays),
@@ -230,30 +224,15 @@
     cut = row_count // 2
     a_own = [a_vals[i * cut : (i + 1) * cut].reshape(cut * B, band * B) for i in range(2)]
 
-    partner = xor_permute(p_own, "rows", 1)
-    both = ("rows", "grp")
-    ahead = [
-        (i * groups + g, j * groups + g)
-        for g in range(1, groups, 2)
-        for i in range(rows_total)
-        for j in [i + 2 if i % 2 else i - 2]
-        if 0 <= j < rows_total
-    ]
-    onward = [
-        (i * groups + g, j * groups + g)
-        for g in range(0, groups, 2)
-        for i in range(rows_total)
-        for j in [i - 2 if i % 2 else i + 2]
-        if 0 <= j < rows_total
-    ]
-    across = [
-        (i * groups + g, (i ^ 1) * groups + g)
-        for g in range(1, groups, 2)
-        for i in range(rows_total)
-    ]
-    moved = lax.ppermute(p_own, both, ahead)
-    beyond_even = lax.ppermute(partner, both, onward)
-    beyond_odd = lax.ppermute(moved, both, across)
+    cut = row_count // 2
+    p_own = lax.optimization_barrier(p_own)
+    p_half = [p_own[i * cut * B : (i + 1) * cut * B] for i in range(2)]
+    partner = [xor_permute(p_half[i], "rows", 1) for i in range(2)]
+    onward = [(i, j) for i in range(rows_total) for j in [i - 2 if i % 2 else i + 2]]
+    ahead = [(i, j) for i in range(rows_total) for j in [i + 2 if i % 2 else i - 2]]
+    onward, ahead = ([p for p in pairs if 0 <= p[1] < rows_total] for pairs in (onward, ahead))
+    moved = lax.ppermute(p_half[1], "rows", ahead)
+    beyond = [lax.ppermute(partner[0], "rows", onward), xor_permute(moved, "rows", 1)]
 
     c_far = xor_permute(a_cols, "grp", 2)
     c_near = xor_permute(a_cols, "grp", 1)
@@ -280,43 +259,45 @@
         jnp.concatenate(codes(a_cols, c_near)),
         (*a_own, p_own, *a_near, p_near),
         [
-            (0, 0, 0, 0, part, None),
-            (1, 0, 0, part, part, None),
-            (2, 0, 1, 0, full, None),
-            (3, 0, 2, 0, part, None),
-            (4, 0, 2, part, part, None),
-            (5, 0, 3, 0, full, None),
+            (0, 0, 0, 0, part),
+            (1, 0, 0, part, part),
+            (2, 0, 1, 0, full),
+            (3, 0, 2, 0, part),
+            (4, 0, 2, part, part),
+            (5, 0, 3, 0, full),
         ],
         [whole] * 4,
         (square, whole, whole),
         band,
         row_count,
         flops,
+        (pl.BlockSpec(memory_space=pltpu.VMEM),) + (pl.BlockSpec(memory_space=pltpu.HBM),) * 2,
     )
     later_codes = jnp.concatenate([*codes(c_far, c_last), grp_pos.reshape(1)])
 
     def later_loads(start):
         return [
-            (0, 0, 0, 0, part, None),
-            (1, start, 1, 0, part, None),
-            (2, 0, 2, 0, part, None),
-            (3, start, 3, 0, part, None),
-            (4, 0, 4, 0, full, None),
-            (5, 0, 5, 0, full, None),
-            (6, 0, 6, 0, full, 0),
-            (7, 0, 6, 0, full, 1),
+            (0, 0, 0, 0, part),
+            (1, start, 1, 0, part),
+            (2, 0, 2, 0, part),
+            (3, start, 3, 0, part),
+            (4, 0, 4, 0, full),
+            (5, 0, 5, 0, part),
+            (6, 0, 5, part, part),
+            (7, 0, 6, 0, part),
+            (8, 0, 6, part, part),
         ]
 
-    rights = (p_own, partner, beyond_even, beyond_odd)
+    rights = (p_own, *partner, *beyond)
     earlier = run_products(
         mid_kernel,
         later_codes,
         (a_far[0], p_far, a_last[0], p_last, *rights, partial, kept_1, kept_2),
         later_loads(0)
         + [
-            (8, 0, 7, 0, width, None),
-            (9, 0, 8, 0, full, None),
-            (10, 0, 9, 0, full, None),
+            (9, 0, 7, 0, width),
+            (10, 0, 8, 0, full),
+            (11, 0, 9, 0, full),
         ],
         [piece] * 4 + [whole] * 3 + [square, whole, whole],
         wide,
@@ -328,7 +309,7 @@
         late_kernel,
         later_codes,
         (a_far[1], p_far, a_last[1], p_last, *rights, earlier),
-        later_loads(part) + [(8, 0, 7, 0, width, None)],
+        later_loads(part) + [(9, 0, 7, 0, width)],
         [piece] * 4 + [whole] * 3 + [wide],
         (half, half),
         band,
@@ -412,8 +393,10 @@
     return dict(zip(names, out))
 
 
-def gather_kernel(chunks, capacity, where, *refs):
+def gather_kernel(names, capacity, where, *refs):
+    chunks = len(names)
     sources, (target, probe, buffer, sems_probe, sems_in, sems_out) = refs[:chunks], refs[chunks:]
+    me = where[0]
     probes = [
         pltpu.make_async_copy(
             sources[c].at[:, pl.ds(0, probe.shape[2])], probe.at[c], sems_probe.at[c]
@@ -429,10 +412,10 @@
     limit = target.shape[0] // capacity - 1
     place = []
     for c in range(chunks):
-        sender = jnp.bitwise_xor(where[0], c)
+        sender = jnp.bitwise_xor(me, names[c])
         ahead = jnp.int32(0)
         for other in range(chunks):
-            first = jnp.bitwise_xor(where[0], other) < sender
+            first = jnp.bitwise_xor(me, names[other]) < sender
             ahead = ahead + jnp.where(first, full[other], 0)
         place.append(pl.multiple_of(jnp.minimum(ahead, limit) * capacity, capacity))
 
@@ -460,12 +443,13 @@
         pl.when(full[c] == 1)(lambda c=c: stores(c).wait())
 
 
-def gather_chunks(incoming, rows_pos, row_count):
-    chunks = len(incoming)
+def gather_chunks(incoming, where, row_count):
+    names = tuple(incoming)
+    chunks = len(names)
     capacity, row_width = incoming[0].shape
     dtype = incoming[0].dtype
     return pl.pallas_call(
-        functools.partial(gather_kernel, chunks, capacity),
+        functools.partial(gather_kernel, names, capacity),
         out_shape=jax.ShapeDtypeStruct((row_count, row_width), dtype),
         in_specs=[pl.BlockSpec(memory_space=pltpu.SMEM)]
         + [pl.BlockSpec(memory_space=pl.ANY)] * chunks,
@@ -478,7 +462,7 @@
             pltpu.SemaphoreType.DMA((chunks,)),
         ],
         name="gather_chunks",
-    )(rows_pos.astype(jnp.int32).reshape(1), *incoming)
+    )(where, *incoming.values())
 
 
 def use_chunks(row_count, rows_total):
@@ -501,11 +485,11 @@
         rest = tuple(i for i in range(rows_total) if i not in first)
         chunks = pack_chunks(a_vals, slot_of, first, capacity)
         chunks |= pack_chunks(a_vals, slot_of, rest, capacity)
-        incoming = [chunks[0]] + [
-            xor_permute(chunks[bit], "rows", bit)
-            for bit in range(1, rows_total)
-        ]
-        return gather_chunks(incoming, rows_pos, row_count)
+        incoming = {
+            bit: xor_permute(chunks[bit], "rows", bit) if bit else chunks[0]
+            for bit in range(rows_total)
+        }
+        return gather_chunks(incoming, rows_pos.astype(jnp.int32).reshape(1), row_count)
     slot_of = new_rows * capacity + ranking
     slot_ids = jnp.arange(slot_total, dtype=jnp.int32)
     sender = slot_ids[:, None] == slot_of[None, :]
@@ -542,9 +526,9 @@
 
 def solution(mesh):
     in_specs = (
-        P(("rows", "grp"), None),
-        P(("rows", "grp"), None),
-        P(("rows", "grp"), None),
+        P(("rows", "grp")),
+        P(("rows", "grp")),
+        P(("rows", "grp")),
         P(("rows", "grp")),
     )
     out_specs = (P(("rows", "grp"), None), P(("rows", "grp"), None))

time: 259 us -> 257 us (level)
  the two profiles are of different devices: /device:TPU:16 before, /device:TPU:12 now
where the time goes in v6:
time: 257 us; the launch traced here: 256 us
  waiting for transfers between devices  165 us (64%)
  Pallas kernels  47.8 us (19%)
  starting transfers between devices  26.5 us (10%)
  local copies, waits for them, and re-layouts  12 us (5%)
  other arithmetic  3.73 us (1%)
    ppermute x24, waiting for transfers between devices, xor_permute(): return lax.ppermute(value, axis, [(i, i ^ bit) for i in range(count)])  143 us
    pallas_call x3, Pallas kernels, run_products(): pl.pallas_call(functools.partial(body, band, row_count, loads, len(arrays...  35.9 us
    ppermute x1, waiting for transfers between devices, galerkin(): moved = lax.ppermute(p_half[1], 'rows', ahead)  22 us
    ppermute x24, starting transfers between devices, xor_permute(): return lax.ppermute(value, axis, [(i, i ^ bit) for i in range(count)])  19.7 us
    pallas_call x2, Pallas kernels, pack_chunks(): pl.pallas_call(functools.partial(pack_kernel, names, capacity, pieces), o...  7.68 us
  transfers between devices with their start and end apart: 26, of which 11 were waited for; matrix products, arithmetic and copies ran while one was open for 4% of the time, Pallas kernels for 19%

profile of v6, /device:TPU:12, one launch (start us, length us, event | category | flops | bytes accessed | tf_op | source)
XLA Modules:
  0.0 256.1 jit_solution(5477932621890785268)
XLA Ops:
  0.6 2.9 %reshape.43.refs_2_.refs_4_ = bf16[4096,256]{1,0:T(8,128)(2,1)S(1)} reshape(bf16[64,16384]{1,0:T(8,128)(2,1)} %param.6) | data formatting | bytes 4194304 | tf_op jit(solution)/shard_map/reshape | solution.py:223
  3.5 1.6 collective-permute-start.10
  5.1 2.6 %fusion.38 = (bf16[32,16384]{1,0:T(8,128)(2,1)}, bf16[32,16384]{1,0:T(8,128)(2,1)S(1)}) fusion(bf16[64,16384]{1,0:T(8,128)(2,1)} %a_hbm.3), kind=kLoop, calls=%fused_computation.101 | loop fusion | bytes 4194304 | tf_op jit(solution)/shard_map/slice | solution.py:225
  7.7 2.3 reshape.44.refs_0_
  13.2 37.9 %collective-permute-done.7 = s32[64,4]{0,1:T(4,128)S(1)} collective-permute-done((s32[64,4]{0,1:T(4,128)S(1)}, s32[64,4]{0,1:T(4,128)S(1)}, u32[]{:S(2)}, u32[]{:S(2)}) %collective-permute-start.7) | collective-permute-done | bytes 1056 | tf_op jit(solution)/shard_map/ppermute | solution.py:18
  53.4 3.5 %collective-permute-start.16 = (bf16[2048,256]{1,0:T(8,128)(2,1)S(1)}, bf16[2048,256]{1,0:T(8,128)(2,1)}, u32[]{:S(2)}, u32[]{:S(2)}) collective-permute-start(bf16[2048,256]{1,0:T(8,128)(2,1)S(1)} %get-tuple-element.30), channel_id=1, source_target_pairs={{4,12},{8,0},{12,20},{16,8},{20,28},{24,16},{5,13},{9,1},{13,21},{... | collective-permute-start | bytes 3145736 | tf_op jit(solution)/shard_map/ppermute | solution.py:234
  58.7 22.0 %collective-permute-done.16 = bf16[2048,256]{1,0:T(8,128)(2,1)} collective-permute-done((bf16[2048,256]{1,0:T(8,128)(2,1)S(1)}, bf16[2048,256]{1,0:T(8,128)(2,1)}, u32[]{:S(2)}, u32[]{:S(2)}) %collective-permute-start.16) | collective-permute-done | bytes 1048608 | tf_op jit(solution)/shard_map/ppermute | solution.py:234
  82.6 3.2 %collective-permute-start.15 = (bf16[2048,256]{1,0:T(8,128)(2,1)S(1)}, bf16[2048,256]{1,0:T(8,128)(2,1)}, u32[]{:S(2)}, u32[]{:S(2)}) collective-permute-start(bf16[2048,256]{1,0:T(8,128)(2,1)S(1)} %collective-permute-done.13.refs_5_), channel_id=1, source_target_pairs={{0,8},{8,16},{12,4},{16,24},{20,12},{28,20},{1,9},{9,17},{13,5},{1... | collective-permute-start | bytes 3145736 | tf_op jit(solution)/shard_map/ppermute | solution.py:235
  86.4 19.0 %collective-permute-done.9.refs_0_ = bf16[2048,256]{1,0:T(8,128)(2,1)} collective-permute-done((bf16[2048,256]{1,0:T(8,128)(2,1)}, bf16[2048,256]{1,0:T(8,128)(2,1)}, u32[]{:S(2)}, u32[]{:S(2)}) %collective-permute-start.9) | collective-permute-done | bytes 1048608 | tf_op jit(solution)/shard_map/ppermute | solution.py:18
  107.6 4.3 %shard_map.59 = (bf16[16,16384]{1,0:T(8,128)(2,1)}, bf16[16,16384]{1,0:T(8,128)(2,1)}, bf16[16,16384]{1,0:T(8,128)(2,1)}, bf16[16,16384]{1,0:T(8,128)(2,1)}, bf1...) custom-call(s32[1,64]{1,0:T(1,128)} %add_bitcast_fusion.slot_ref, bf16[64,16384]{1,0:T(8,128)(2,1)} %a_hbm.3), custom_call_target="tpu_custom_call" | custom-call | tf_op jit(solution)/shard_map/pallas_call | solution.py:381
  114.0 1.7 collective-permute-start
  117.0 16.3 %shard_map.61 = (f32[256,256]{1,0:T(8,128)}, bf16[4096,256]{1,0:T(8,128)(2,1)}, bf16[4096,256]{1,0:T(8,128)(2,1)}) custom-call(s32[512]{0:T(512)} %pad_add_fusion.1.codes, bf16[2048,256]{1,0:T(8,128)(2,1)} %reshape.44.refs_0_, bf16[2048,256]{1,0:T(8,128)(2,1)} %reshape.42.refs_1_, bf16[4096,256]{1,0:T(8,128)(2,1)} %copy-done, ...), custom_call_target="tpu_custom_call" | custom-call | flops 536870912 | bytes 8388608 | tf_op jit(solution)/shard_map/pallas_call | solution.py:195
  133.3 10.0 %shard_map.62.refs_9_ = f32[256,768]{1,0:T(8,128)} custom-call(s32[513]{0:T(1024)} %pad_add_fusion.codes, bf16[2048,256]{1,0:T(8,128)(2,1)} %collective-permute-done.18.refs_0_, bf16[4096,256]{1,0:T(8,128)(2,1)} %collective-permute-done.10.refs_1_, bf16[2048,256]{1,0:T(8,128)(2,1)} %collective-permute-done.19.refs_2_, ...), custom_call_target="tpu_custom_call" | custom-call | flops 536870912 | bytes 17039360 | tf_op jit(solution)/shard_map/pallas_call | solution.py:195
  144.3 9.7 %shard_map.63 = (f32[128,768]{1,0:T(8,128)}, f32[128,768]{1,0:T(8,128)}) custom-call(s32[513]{0:T(1024)} %pad_add_fusion.codes, bf16[2048,256]{1,0:T(8,128)(2,1)} %collective-permute-done.9.refs_0_, bf16[4096,256]{1,0:T(8,128)(2,1)} %collective-permute-done.10.refs_1_, bf16[2048,256]{1,0:T(8,128)(2,1)} %copy-done.5, ...), custom_call_target="tpu_custom_call" | custom-call | flops 536870912 | bytes 13369344 | tf_op jit(solution)/shard_map/pallas_call | solution.py:195
  154.0 2.1 collective-permute-start.24
  156.1 2.1 collective-permute-start.4
  158.2 3.4 %shard_map.60 = (bf16[16,16384]{1,0:T(8,128)(2,1)}, bf16[16,16384]{1,0:T(8,128)(2,1)}) custom-call(s32[1,64]{1,0:T(1,128)} %add_bitcast_fusion.slot_ref, bf16[64,16384]{1,0:T(8,128)(2,1)} %a_hbm.3), custom_call_target="tpu_custom_call" | custom-call | tf_op jit(solution)/shard_map/pallas_call | solution.py:381
  161.6 1.8 collective-permute-start.6
  167.4 10.5 %collective-permute-done.2.refs_3_ = bf16[16,16384]{1,0:T(8,128)(2,1)S(1)} collective-permute-done((bf16[16,16384]{1,0:T(8,128)(2,1)}, bf16[16,16384]{1,0:T(8,128)(2,1)S(1)}, u32[]{:S(2)}, u32[]{:S(2)}) %collective-permute-start.2) | collective-permute-done | bytes 524320 | tf_op jit(solution)/shard_map/ppermute | solution.py:18
  178.0 38.0 %collective-permute-done.4.refs_5_ = bf16[16,16384]{1,0:T(8,128)(2,1)S(1)} collective-permute-done((bf16[16,16384]{1,0:T(8,128)(2,1)}, bf16[16,16384]{1,0:T(8,128)(2,1)S(1)}, u32[]{:S(2)}, u32[]{:S(2)}) %collective-permute-start.4) | collective-permute-done | bytes 524320 | tf_op jit(solution)/shard_map/ppermute | solution.py:18
  216.0 13.5 %collective-permute-done.6.refs_7_ = bf16[16,16384]{1,0:T(8,128)(2,1)S(1)} collective-permute-done((bf16[16,16384]{1,0:T(8,128)(2,1)}, bf16[16,16384]{1,0:T(8,128)(2,1)S(1)}, u32[]{:S(2)}, u32[]{:S(2)}) %collective-permute-start.6) | collective-permute-done | bytes 524320 | tf_op jit(solution)/shard_map/ppermute | solution.py:18
  229.5 9.0 %collective-permute-done.3.refs_4_ = bf16[16,16384]{1,0:T(8,128)(2,1)} collective-permute-done((bf16[16,16384]{1,0:T(8,128)(2,1)}, bf16[16,16384]{1,0:T(8,128)(2,1)}, u32[]{:S(2)}, u32[]{:S(2)}) %collective-permute-start.3) | collective-permute-done | bytes 524320 | tf_op jit(solution)/shard_map/ppermute | solution.py:18
  238.5 12.6 %collective-permute-done.5.refs_6_ = bf16[16,16384]{1,0:T(8,128)(2,1)} collective-permute-done((bf16[16,16384]{1,0:T(8,128)(2,1)}, bf16[16,16384]{1,0:T(8,128)(2,1)}, u32[]{:S(2)}, u32[]{:S(2)}) %collective-permute-start.5) | collective-permute-done | bytes 524320 | tf_op jit(solution)/shard_map/ppermute | solution.py:18
  251.2 4.2 %gather_chunks.1 = bf16[64,16384]{1,0:T(8,128)(2,1)} custom-call(s32[1]{0:T(128)} %bitcast.where, bf16[16,16384]{1,0:T(8,128)(2,1)} %get-tuple-element.15.refs_0_, bf16[16,16384]{1,0:T(8,128)(2,1)} %copy-done.6, bf16[16,16384]{1,0:T(8,128)(2,1)} %copy-done.7, bf16[16,16384]{1,0:T(8,128)(2,1)} %copy-done.8, bf16[16,16384]{1,0:T(8,128)(2,1)} %collective-permute-done.3.refs_4_, ...), custom_call_target="tpu_custom_call" | custom-call | tf_op jit(solution)/shard_map/gather_chunks/pallas_call | solution.py:451
  (88 shorter events, 21.0 us)
Async XLA Ops:
  3.5 78.6 %collective-permute-start.10 = (bf16[4096,256]{1,0:T(8,128)(2,1)S(1)}, bf16[4096,256]{1,0:T(8,128)(2,1)}, u32[]{:S(2)}, u32[]{:S(2)}) collective-permute-start(bf16[4096,256]{1,0:T(8,128)(2,1)S(1)} %reshape.43.refs_2_.refs_4_), channel_id=1, source_target_pairs={{0,2},{1,3},{2,0},{3,1},{4,6},{5,7},{6,4},{7,5},{8,10},{9,11},{10,... | collective-permute-start | bytes 6291464 | tf_op jit(solution)/shard_map/ppermute | solution.py:18
  10.1 46.8 %collective-permute-start.21 = (bf16[2048,256]{1,0:T(8,128)(2,1)}, bf16[2048,256]{1,0:T(8,128)(2,1)}, u32[]{:S(2)}, u32[]{:S(2)}) collective-permute-start(bf16[2048,256]{1,0:T(8,128)(2,1)} %reshape.44.refs_0_), channel_id=1, source_target_pairs={{0,1},{1,0},{2,3},{3,2},{4,5},{5,4},{6,7},{7,6},{8,9},{9,8},{10,11... | collective-permute-start | bytes 3145736 | tf_op jit(solution)/shard_map/ppermute | solution.py:18
  11.4 45.6 %collective-permute-start.22 = (bf16[2048,256]{1,0:T(8,128)(2,1)}, bf16[2048,256]{1,0:T(8,128)(2,1)S(1)}, u32[]{:S(2)}, u32[]{:S(2)}) collective-permute-start(bf16[2048,256]{1,0:T(8,128)(2,1)} %reshape.42.refs_1_), channel_id=1, source_target_pairs={{0,1},{1,0},{2,3},{3,2},{4,5},{5,4},{6,7},{7,6},{8,9},{9,8},{10,11... | collective-permute-start | bytes 3145736 | tf_op jit(solution)/shard_map/ppermute | solution.py:18
  12.0 45.1 %collective-permute-start.13 = (bf16[2048,256]{1,0:T(8,128)(2,1)S(1)}, bf16[2048,256]{1,0:T(8,128)(2,1)S(1)}, u32[]{:S(2)}, u32[]{:S(2)}) collective-permute-start(bf16[2048,256]{1,0:T(8,128)(2,1)S(1)} %get-tuple-element.31), channel_id=1, source_target_pairs={{0,4},{4,0},{8,12},{12,8},{16,20},{20,16},{24,28},{28,24},{1,5},{5... | collective-permute-start | bytes 3145736 | tf_op jit(solution)/shard_map/ppermute | solution.py:18
  12.6 38.5 %collective-permute-start.7 = (s32[64,4]{0,1:T(4,128)S(1)}, s32[64,4]{0,1:T(4,128)S(1)}, u32[]{:S(2)}, u32[]{:S(2)}) collective-permute-start(s32[64,4]{0,1:T(4,128)S(1)} %copy-done.13), channel_id=1, source_target_pairs={{0,2},{1,3},{2,0},{3,1},{4,6},{5,7},{6,4},{7,5},{8,10},{9,11},{10,... | collective-permute-start | bytes 3080 | tf_op jit(solution)/shard_map/ppermute | solution.py:18
  53.4 27.2 %collective-permute-start.16 = (bf16[2048,256]{1,0:T(8,128)(2,1)S(1)}, bf16[2048,256]{1,0:T(8,128)(2,1)}, u32[]{:S(2)}, u32[]{:S(2)}) collective-permute-start(bf16[2048,256]{1,0:T(8,128)(2,1)S(1)} %get-tuple-element.30), channel_id=1, source_target_pairs={{4,12},{8,0},{12,20},{16,8},{20,28},{24,16},{5,13},{9,1},{13,21},{... | collective-permute-start | bytes 3145736 | tf_op jit(solution)/shard_map/ppermute | solution.py:234
  56.9 48.5 %collective-permute-start.23 = (bf16[4096,256]{1,0:T(8,128)(2,1)S(1)}, bf16[4096,256]{1,0:T(8,128)(2,1)S(1)}, u32[]{:S(2)}, u32[]{:S(2)}) collective-permute-start(bf16[4096,256]{1,0:T(8,128)(2,1)S(1)} %reshape.43.refs_2_.refs_4_), channel_id=1, source_target_pairs={{0,1},{1,0},{2,3},{3,2},{4,5},{5,4},{6,7},{7,6},{8,9},{9,8},{10,11... | collective-permute-start | bytes 6291464 | tf_op jit(solution)/shard_map/ppermute | solution.py:18
  57.0 25.5 %collective-permute-start.14 = (bf16[2048,256]{1,0:T(8,128)(2,1)S(1)}, bf16[2048,256]{1,0:T(8,128)(2,1)S(1)}, u32[]{:S(2)}, u32[]{:S(2)}) collective-permute-start(bf16[2048,256]{1,0:T(8,128)(2,1)S(1)} %get-tuple-element.30), channel_id=1, source_target_pairs={{0,4},{4,0},{8,12},{12,8},{16,20},{20,16},{24,28},{28,24},{1,5},{5... | collective-permute-start | bytes 3145736 | tf_op jit(solution)/shard_map/ppermute | solution.py:18
  57.1 28.7 %collective-permute-start.18 = (bf16[2048,256]{1,0:T(8,128)(2,1)}, bf16[2048,256]{1,0:T(8,128)(2,1)}, u32[]{:S(2)}, u32[]{:S(2)}) collective-permute-start(bf16[2048,256]{1,0:T(8,128)(2,1)} %reshape.44.refs_0_), channel_id=1, source_target_pairs={{0,2},{1,3},{2,0},{3,1},{4,6},{5,7},{6,4},{7,5},{8,10},{9,11},{10,... | collective-permute-start | bytes 3145736 | tf_op jit(solution)/shard_map/ppermute | solution.py:18
  80.6 24.8 %collective-permute-start.9 = (bf16[2048,256]{1,0:T(8,128)(2,1)}, bf16[2048,256]{1,0:T(8,128)(2,1)}, u32[]{:S(2)}, u32[]{:S(2)}) collective-permute-start(bf16[2048,256]{1,0:T(8,128)(2,1)} %reshape.42.refs_1_), channel_id=1, source_target_pairs={{0,2},{1,3},{2,0},{3,1},{4,6},{5,7},{6,4},{7,5},{8,10},{9,11},{10,... | collective-permute-start | bytes 3145736 | tf_op jit(solution)/shard_map/ppermute | solution.py:18
  82.1 51.2 %collective-permute-start.12 = (bf16[4096,256]{1,0:T(8,128)(2,1)}, bf16[4096,256]{1,0:T(8,128)(2,1)}, u32[]{:S(2)}, u32[]{:S(2)}) collective-permute-start(bf16[4096,256]{1,0:T(8,128)(2,1)} %collective-permute-done.10.refs_1_), channel_id=1, source_target_pairs={{0,1},{1,0},{2,3},{3,2},{4,5},{5,4},{6,7},{7,6},{8,9},{9,8},{10,11... | collective-permute-start | bytes 6291464 | tf_op jit(solution)/shard_map/ppermute | solution.py:18
  82.6 31.4 %collective-permute-start.15 = (bf16[2048,256]{1,0:T(8,128)(2,1)S(1)}, bf16[2048,256]{1,0:T(8,128)(2,1)}, u32[]{:S(2)}, u32[]{:S(2)}) collective-permute-start(bf16[2048,256]{1,0:T(8,128)(2,1)S(1)} %collective-permute-done.13.refs_5_), channel_id=1, source_target_pairs={{0,8},{8,16},{12,4},{16,24},{20,12},{28,20},{1,9},{9,17},{13,5},{1... | collective-permute-start | bytes 3145736 | tf_op jit(solution)/shard_map/ppermute | solution.py:235
  85.8 29.8 %collective-permute-start.17 = (bf16[2048,256]{1,0:T(8,128)(2,1)}, bf16[2048,256]{1,0:T(8,128)(2,1)}, u32[]{:S(2)}, u32[]{:S(2)}) collective-permute-start(bf16[2048,256]{1,0:T(8,128)(2,1)} %collective-permute-done.16), channel_id=1, source_target_pairs={{0,4},{4,0},{8,12},{12,8},{16,20},{20,16},{24,28},{28,24},{1,5},{5... | collective-permute-start | bytes 3145736 | tf_op jit(solution)/shard_map/ppermute | solution.py:18
  105.4 27.8 %collective-permute-start.19 = (bf16[2048,256]{1,0:T(8,128)(2,1)}, bf16[2048,256]{1,0:T(8,128)(2,1)}, u32[]{:S(2)}, u32[]{:S(2)}) collective-permute-start(bf16[2048,256]{1,0:T(8,128)(2,1)} %collective-permute-done.18.refs_0_), channel_id=1, source_target_pairs={{0,1},{1,0},{2,3},{3,2},{4,5},{5,4},{6,7},{7,6},{8,9},{9,8},{10,11... | collective-permute-start | bytes 3145736 | tf_op jit(solution)/shard_map/ppermute | solution.py:18
  105.5 37.8 %collective-permute-start.11 = (bf16[2048,256]{1,0:T(8,128)(2,1)}, bf16[2048,256]{1,0:T(8,128)(2,1)S(1)}, u32[]{:S(2)}, u32[]{:S(2)}) collective-permute-start(bf16[2048,256]{1,0:T(8,128)(2,1)} %collective-permute-done.9.refs_0_), channel_id=1, source_target_pairs={{0,1},{1,0},{2,3},{3,2},{4,5},{5,4},{6,7},{7,6},{8,9},{9,8},{10,11... | collective-permute-start | bytes 3145736 | tf_op jit(solution)/shard_map/ppermute | solution.py:18
  114.0 47.6 %collective-permute-start = (bf16[16,16384]{1,0:T(8,128)(2,1)}, bf16[16,16384]{1,0:T(8,128)(2,1)S(1)}, u32[]{:S(2)}, u32[]{:S(2)}) collective-permute-start(bf16[16,16384]{1,0:T(8,128)(2,1)} %get-tuple-element.16), channel_id=1, source_target_pairs={{0,4},{4,0},{8,12},{12,8},{16,20},{20,16},{24,28},{28,24},{1,5},{5... | collective-permute-start | bytes 1572872 | tf_op jit(solution)/shard_map/ppermute | solution.py:18
  115.6 47.7 %collective-permute-start.1 = (bf16[16,16384]{1,0:T(8,128)(2,1)}, bf16[16,16384]{1,0:T(8,128)(2,1)S(1)}, u32[]{:S(2)}, u32[]{:S(2)}) collective-permute-start(bf16[16,16384]{1,0:T(8,128)(2,1)} %get-tuple-element.17), channel_id=1, source_target_pairs={{0,8},{4,12},{8,0},{12,4},{16,24},{20,28},{24,16},{28,20},{1,9},{5... | collective-permute-start | bytes 1572872 | tf_op jit(solution)/shard_map/ppermute | solution.py:18
  154.0 10.9 %collective-permute-start.24 = (f32[128,768]{1,0:T(8,128)}, f32[128,768]{1,0:T(8,128)S(1)}, u32[]{:S(2)}, u32[]{:S(2)}) collective-permute-start(f32[128,768]{1,0:T(8,128)} %get-tuple-element.27), channel_id=1, source_target_pairs={{0,1},{1,0},{2,3},{3,2},{4,5},{5,4},{6,7},{7,6},{8,9},{9,8},{10,11... | collective-permute-start | bytes 1179656 | tf_op jit(solution)/shard_map/ppermute | solution.py:18
  156.1 21.8 %collective-permute-start.2 = (bf16[16,16384]{1,0:T(8,128)(2,1)}, bf16[16,16384]{1,0:T(8,128)(2,1)S(1)}, u32[]{:S(2)}, u32[]{:S(2)}) collective-permute-start(bf16[16,16384]{1,0:T(8,128)(2,1)} %get-tuple-element.18), channel_id=1, source_target_pairs={{0,12},{4,8},{8,4},{12,0},{16,28},{20,24},{24,20},{28,16},{1,13},{... | collective-permute-start | bytes 1572872 | tf_op jit(solution)/shard_map/ppermute | solution.py:18
  156.1 59.9 %collective-permute-start.4 = (bf16[16,16384]{1,0:T(8,128)(2,1)}, bf16[16,16384]{1,0:T(8,128)(2,1)S(1)}, u32[]{:S(2)}, u32[]{:S(2)}) collective-permute-start(bf16[16,16384]{1,0:T(8,128)(2,1)} %get-tuple-element.20), channel_id=1, source_target_pairs={{0,20},{4,16},{8,28},{12,24},{16,4},{20,0},{24,12},{28,8},{1,21},{... | collective-permute-start | bytes 1572872 | tf_op jit(solution)/shard_map/ppermute | solution.py:18
  161.6 67.9 %collective-permute-start.6 = (bf16[16,16384]{1,0:T(8,128)(2,1)}, bf16[16,16384]{1,0:T(8,128)(2,1)S(1)}, u32[]{:S(2)}, u32[]{:S(2)}) collective-permute-start(bf16[16,16384]{1,0:T(8,128)(2,1)} %get-tuple-element.22), channel_id=1, source_target_pairs={{0,28},{4,24},{8,20},{12,16},{16,12},{20,8},{24,4},{28,0},{1,29},{... | collective-permute-start | bytes 1572872 | tf_op jit(solution)/shard_map/ppermute | solution.py:18
  163.4 75.1 %collective-permute-start.3 = (bf16[16,16384]{1,0:T(8,128)(2,1)}, bf16[16,16384]{1,0:T(8,128)(2,1)}, u32[]{:S(2)}, u32[]{:S(2)}) collective-permute-start(bf16[16,16384]{1,0:T(8,128)(2,1)} %get-tuple-element.19), channel_id=1, source_target_pairs={{0,16},{4,20},{8,24},{12,28},{16,0},{20,4},{24,8},{28,12},{1,17},{... | collective-permute-start | bytes 1572872 | tf_op jit(solution)/shard_map/ppermute | solution.py:18
  164.9 86.2 %collective-permute-start.5 = (bf16[16,16384]{1,0:T(8,128)(2,1)}, bf16[16,16384]{1,0:T(8,128)(2,1)}, u32[]{:S(2)}, u32[]{:S(2)}) collective-permute-start(bf16[16,16384]{1,0:T(8,128)(2,1)} %get-tuple-element.21), channel_id=1, source_target_pairs={{0,24},{4,28},{8,16},{12,20},{16,8},{20,12},{24,0},{28,4},{1,25},{... | collective-permute-start | bytes 1572872 | tf_op jit(solution)/shard_map/ppermute | solution.py:18
  178.0 77.4 %collective-permute-start.25 = (f32[64,768]{1,0:T(8,128)S(1)}, f32[64,768]{1,0:T(8,128)S(1)}, u32[]{:S(2)}, u32[]{:S(2)}) collective-permute-start(f32[64,768]{1,0:T(8,128)S(1)} %slice.39), channel_id=1, source_target_pairs={{0,2},{1,3},{2,0},{3,1},{4,6},{5,7},{6,4},{7,5},{8,10},{9,11},{10,... | collective-permute-start | bytes 589832 | tf_op jit(solution)/shard_map/ppermute | solution.py:18
  (17 other events, 623.9 us)

commit v7 on v6

--- a/solution.py
+++ b/solution.py
@@ -395,52 +395,34 @@
 
 def gather_kernel(names, capacity, where, *refs):
     chunks = len(names)
-    sources, (target, probe, buffer, sems_probe, sems_in, sems_out) = refs[:chunks], refs[chunks:]
+    sources, (target, buffer, sems_in, sems_out) = refs[:chunks], refs[chunks:]
     me = where[0]
-    probes = [
-        pltpu.make_async_copy(
-            sources[c].at[:, pl.ds(0, probe.shape[2])], probe.at[c], sems_probe.at[c]
-        )
-        for c in range(chunks)
+    loads = [
+        pltpu.make_async_copy(sources[c], buffer.at[c], sems_in.at[c]) for c in range(chunks)
     ]
-    for copy in probes:
+    for copy in loads:
         copy.start()
     full = []
     for c in range(chunks):
-        probes[c].wait()
-        full.append(jnp.where(jnp.max(probe[c].astype(jnp.float32)) < jnp.inf, 1, 0))
+        loads[c].wait()
+        head = buffer[c, :, :128].astype(jnp.float32)
+        full.append(jnp.where(jnp.max(head) < jnp.inf, 1, 0))
     limit = target.shape[0] // capacity - 1
-    place = []
+    stores = []
     for c in range(chunks):
         sender = jnp.bitwise_xor(me, names[c])
         ahead = jnp.int32(0)
         for other in range(chunks):
             first = jnp.bitwise_xor(me, names[other]) < sender
             ahead = ahead + jnp.where(first, full[other], 0)
-        place.append(pl.multiple_of(jnp.minimum(ahead, limit) * capacity, capacity))
-
-    def loads(c):
-        return pltpu.make_async_copy(
-            sources[c], buffer.at[pl.ds(place[c], capacity), :], sems_in.at[c]
-        )
-
-    def stores(c):
-        return pltpu.make_async_copy(
-            buffer.at[pl.ds(place[c], capacity), :],
-            target.at[pl.ds(place[c], capacity), :],
-            sems_out.at[c],
-        )
-
+        place = pl.multiple_of(jnp.minimum(ahead, limit) * capacity, capacity)
+        copy = pltpu.make_async_copy(
+            buffer.at[c], target.at[pl.ds(place, capacity), :], sems_out.at[c]
+        )
+        stores.append(copy)
+        pl.when(full[c] == 1)(copy.start)
     for c in range(chunks):
-        pl.when(full[c] == 1)(lambda c=c: loads(c).start())
-    for c in range(chunks):
-        @pl.when(full[c] == 1)
-        def _():
-            loads(c).wait()
-            stores(c).start()
-
-    for c in range(chunks):
-        pl.when(full[c] == 1)(lambda c=c: stores(c).wait())
+        pl.when(full[c] == 1)(stores[c].wait)
 
 
 def gather_chunks(incoming, where, row_count):
@@ -455,9 +437,7 @@
         + [pl.BlockSpec(memory_space=pl.ANY)] * chunks,
         out_specs=pl.BlockSpec(memory_space=pl.ANY),
         scratch_shapes=[
-            pltpu.VMEM((chunks, capacity, 128), dtype),
-            pltpu.VMEM((row_count, row_width), dtype),
-            pltpu.SemaphoreType.DMA((chunks,)),
+            pltpu.VMEM((chunks, capacity, row_width), dtype),
             pltpu.SemaphoreType.DMA((chunks,)),
             pltpu.SemaphoreType.DMA((chunks,)),
         ],
@@ -481,7 +461,7 @@
     if use_chunks(row_count, rows_total):
         rows_pos = lax.axis_index("rows")
         slot_of = jnp.bitwise_xor(new_rows, rows_pos) * capacity + ranking
-        first = tuple(range(rows_total // 2, rows_total, 2))
+        first = (rows_total // 2,)
         rest = tuple(i for i in range(rows_total) if i not in first)
         chunks = pack_chunks(a_vals, slot_of, first, capacity)
         chunks |= pack_chunks(a_vals, slot_of, rest, capacity)

time: 257 us -> 258 us (level)
  the two profiles are of different devices: /device:TPU:12 before, /device:TPU:0 now
where the time goes in v7:
time: 258 us
  waiting for transfers between devices  162 us (63%)
  Pallas kernels  47.6 us (18%)
  starting transfers between devices  30.6 us (12%)
  local copies, waits for them, and re-layouts  12.5 us (5%)
  other arithmetic  3.68 us (1%)
    ppermute x24, waiting for transfers between devices, xor_permute(): return lax.ppermute(value, axis, [(i, i ^ bit) for i in range(count)])  143 us
    pallas_call x3, Pallas kernels, run_products(): pl.pallas_call(functools.partial(body, band, row_count, loads, len(arrays...  36.3 us
    ppermute x24, starting transfers between devices, xor_permute(): return lax.ppermute(value, axis, [(i, i ^ bit) for i in range(count)])  25.8 us
    ppermute x1, waiting for transfers between devices, galerkin(): moved = lax.ppermute(p_half[1], 'rows', ahead)  19.5 us
    pallas_call x2, Pallas kernels, pack_chunks(): pl.pallas_call(functools.partial(pack_kernel, names, capacity, pieces), o...  7.59 us
  transfers between devices with their start and end apart: 26, of which 9 were waited for; matrix products, arithmetic and copies ran while one was open for 4% of the time, Pallas kernels for 18%

profile of v7, /device:TPU:0, one launch (start us, length us, event | category | flops | bytes accessed | tf_op | source)
XLA Modules:
  0.0 257.6 jit_solution(15929044196969343080)
XLA Ops:
  0.6 2.9 %reshape.43.refs_2_.refs_4_ = bf16[4096,256]{1,0:T(8,128)(2,1)S(1)} reshape(bf16[64,16384]{1,0:T(8,128)(2,1)} %param.6) | data formatting | bytes 4194304 | tf_op jit(solution)/shard_map/reshape | solution.py:223
  3.5 3.0 %collective-permute-start.10 = (bf16[4096,256]{1,0:T(8,128)(2,1)S(1)}, bf16[4096,256]{1,0:T(8,128)(2,1)}, u32[]{:S(2)}, u32[]{:S(2)}) collective-permute-start(bf16[4096,256]{1,0:T(8,128)(2,1)S(1)} %reshape.43.refs_2_.refs_4_), channel_id=1, source_target_pairs={{0,2},{1,3},{2,0},{3,1},{4,6},{5,7},{6,4},{7,5},{8,10},{9,11},{10,... | collective-permute-start | bytes 6291464 | tf_op jit(solution)/shard_map/ppermute | solution.py:18
  6.6 2.7 %fusion.38 = (bf16[32,16384]{1,0:T(8,128)(2,1)}, bf16[32,16384]{1,0:T(8,128)(2,1)S(1)}) fusion(bf16[64,16384]{1,0:T(8,128)(2,1)} %a_hbm.3), kind=kLoop, calls=%fused_computation.101 | loop fusion | bytes 4194304 | tf_op jit(solution)/shard_map/slice | solution.py:225
  9.2 2.3 reshape.44.refs_0_
  13.5 1.6 collective-permute-start.13
  15.7 36.6 %collective-permute-done.7 = s32[64,4]{0,1:T(4,128)S(1)} collective-permute-done((s32[64,4]{0,1:T(4,128)S(1)}, s32[64,4]{0,1:T(4,128)S(1)}, u32[]{:S(2)}, u32[]{:S(2)}) %collective-permute-start.7) | collective-permute-done | bytes 1056 | tf_op jit(solution)/shard_map/ppermute | solution.py:18
  56.2 4.8 %collective-permute-start.14 = (bf16[2048,256]{1,0:T(8,128)(2,1)S(1)}, bf16[2048,256]{1,0:T(8,128)(2,1)S(1)}, u32[]{:S(2)}, u32[]{:S(2)}) collective-permute-start(bf16[2048,256]{1,0:T(8,128)(2,1)S(1)} %get-tuple-element.28), channel_id=1, source_target_pairs={{0,4},{4,0},{8,12},{12,8},{16,20},{20,16},{24,28},{28,24},{1,5},{5... | collective-permute-start | bytes 3145736 | tf_op jit(solution)/shard_map/ppermute | solution.py:18
  61.0 1.5 collective-permute-start.18
  62.5 19.5 %collective-permute-done.16 = bf16[2048,256]{1,0:T(8,128)(2,1)} collective-permute-done((bf16[2048,256]{1,0:T(8,128)(2,1)S(1)}, bf16[2048,256]{1,0:T(8,128)(2,1)}, u32[]{:S(2)}, u32[]{:S(2)}) %collective-permute-start.16) | collective-permute-done | bytes 1048608 | tf_op jit(solution)/shard_map/ppermute | solution.py:234
  82.0 1.6 collective-permute-start.9
  84.7 3.5 %collective-permute-start.15 = (bf16[2048,256]{1,0:T(8,128)(2,1)S(1)}, bf16[2048,256]{1,0:T(8,128)(2,1)}, u32[]{:S(2)}, u32[]{:S(2)}) collective-permute-start(bf16[2048,256]{1,0:T(8,128)(2,1)S(1)} %collective-permute-done.13.refs_5_), channel_id=1, source_target_pairs={{0,8},{8,16},{12,4},{16,24},{20,12},{28,20},{1,9},{9,17},{13,5},{1... | collective-permute-start | bytes 3145736 | tf_op jit(solution)/shard_map/ppermute | solution.py:235
  88.3 20.7 %collective-permute-done.9.refs_0_ = bf16[2048,256]{1,0:T(8,128)(2,1)} collective-permute-done((bf16[2048,256]{1,0:T(8,128)(2,1)}, bf16[2048,256]{1,0:T(8,128)(2,1)}, u32[]{:S(2)}, u32[]{:S(2)}) %collective-permute-start.9) | collective-permute-done | bytes 1048608 | tf_op jit(solution)/shard_map/ppermute | solution.py:18
  111.1 4.4 %shard_map.59 = (bf16[16,16384]{1,0:T(8,128)(2,1)}, bf16[16,16384]{1,0:T(8,128)(2,1)}, bf16[16,16384]{1,0:T(8,128)(2,1)}, bf16[16,16384]{1,0:T(8,128)(2,1)}, bf1...) custom-call(s32[1,64]{1,0:T(1,128)} %add_bitcast_fusion.slot_ref, bf16[64,16384]{1,0:T(8,128)(2,1)} %a_hbm.3), custom_call_target="tpu_custom_call" | custom-call | tf_op jit(solution)/shard_map/pallas_call | solution.py:381
  118.7 16.3 %shard_map.61 = (f32[256,256]{1,0:T(8,128)}, bf16[4096,256]{1,0:T(8,128)(2,1)}, bf16[4096,256]{1,0:T(8,128)(2,1)}) custom-call(s32[512]{0:T(512)} %pad_add_fusion.1.codes, bf16[2048,256]{1,0:T(8,128)(2,1)} %reshape.44.refs_0_, bf16[2048,256]{1,0:T(8,128)(2,1)} %reshape.42.refs_1_, bf16[4096,256]{1,0:T(8,128)(2,1)} %copy-done, ...), custom_call_target="tpu_custom_call" | custom-call | flops 536870912 | bytes 8388608 | tf_op jit(solution)/shard_map/pallas_call | solution.py:195
  135.0 10.0 %shard_map.62.refs_9_ = f32[256,768]{1,0:T(8,128)} custom-call(s32[513]{0:T(1024)} %pad_add_fusion.codes, bf16[2048,256]{1,0:T(8,128)(2,1)} %collective-permute-done.18.refs_0_, bf16[4096,256]{1,0:T(8,128)(2,1)} %collective-permute-done.10.refs_1_, bf16[2048,256]{1,0:T(8,128)(2,1)} %collective-permute-done.19.refs_2_, ...), custom_call_target="tpu_custom_call" | custom-call | flops 536870912 | bytes 17039360 | tf_op jit(solution)/shard_map/pallas_call | solution.py:195
  146.0 10.1 %shard_map.63 = (f32[128,768]{1,0:T(8,128)}, f32[128,768]{1,0:T(8,128)}) custom-call(s32[513]{0:T(1024)} %pad_add_fusion.codes, bf16[2048,256]{1,0:T(8,128)(2,1)} %collective-permute-done.9.refs_0_, bf16[4096,256]{1,0:T(8,128)(2,1)} %collective-permute-done.10.refs_1_, bf16[2048,256]{1,0:T(8,128)(2,1)} %copy-done.5, ...), custom_call_target="tpu_custom_call" | custom-call | flops 536870912 | bytes 13369344 | tf_op jit(solution)/shard_map/pallas_call | solution.py:195
  156.2 4.1 %collective-permute-start.2 = (bf16[16,16384]{1,0:T(8,128)(2,1)}, bf16[16,16384]{1,0:T(8,128)(2,1)S(1)}, u32[]{:S(2)}, u32[]{:S(2)}) collective-permute-start(bf16[16,16384]{1,0:T(8,128)(2,1)} %get-tuple-element.17), channel_id=1, source_target_pairs={{0,12},{4,8},{8,4},{12,0},{16,28},{20,24},{24,20},{28,16},{1,13},{... | collective-permute-start | bytes 1572872 | tf_op jit(solution)/shard_map/ppermute | solution.py:18
  160.2 3.2 %shard_map.60 = bf16[16,16384]{1,0:T(8,128)(2,1)} custom-call(s32[1,64]{1,0:T(1,128)} %add_bitcast_fusion.slot_ref, bf16[64,16384]{1,0:T(8,128)(2,1)} %a_hbm.3), custom_call_target="tpu_custom_call" | custom-call | tf_op jit(solution)/shard_map/pallas_call | solution.py:381
  163.4 2.4 collective-permute-start.5
  165.8 3.2 %collective-permute-start.6 = (bf16[16,16384]{1,0:T(8,128)(2,1)}, bf16[16,16384]{1,0:T(8,128)(2,1)}, u32[]{:S(2)}, u32[]{:S(2)}) collective-permute-start(bf16[16,16384]{1,0:T(8,128)(2,1)} %get-tuple-element.20), channel_id=1, source_target_pairs={{0,28},{4,24},{8,20},{12,16},{16,12},{20,8},{24,4},{28,0},{1,29},{... | collective-permute-start | bytes 1572872 | tf_op jit(solution)/shard_map/ppermute | solution.py:18
  170.9 11.5 %collective-permute-done.2.refs_3_ = bf16[16,16384]{1,0:T(8,128)(2,1)S(1)} collective-permute-done((bf16[16,16384]{1,0:T(8,128)(2,1)}, bf16[16,16384]{1,0:T(8,128)(2,1)S(1)}, u32[]{:S(2)}, u32[]{:S(2)}) %collective-permute-start.2) | collective-permute-done | bytes 524320 | tf_op jit(solution)/shard_map/ppermute | solution.py:18
  182.4 39.6 %collective-permute-done.4.refs_5_ = bf16[16,16384]{1,0:T(8,128)(2,1)S(1)} collective-permute-done((bf16[16,16384]{1,0:T(8,128)(2,1)}, bf16[16,16384]{1,0:T(8,128)(2,1)S(1)}, u32[]{:S(2)}, u32[]{:S(2)}) %collective-permute-start.4) | collective-permute-done | bytes 524320 | tf_op jit(solution)/shard_map/ppermute | solution.py:18
  222.0 31.2 %collective-permute-done.3.refs_4_ = bf16[16,16384]{1,0:T(8,128)(2,1)} collective-permute-done((bf16[16,16384]{1,0:T(8,128)(2,1)}, bf16[16,16384]{1,0:T(8,128)(2,1)}, u32[]{:S(2)}, u32[]{:S(2)}) %collective-permute-start.3) | collective-permute-done | bytes 524320 | tf_op jit(solution)/shard_map/ppermute | solution.py:18
  253.2 3.7 %gather_chunks.1 = bf16[64,16384]{1,0:T(8,128)(2,1)} custom-call(s32[1]{0:T(128)} %bitcast.where, bf16[16,16384]{1,0:T(8,128)(2,1)} %get-tuple-element.14.refs_0_, bf16[16,16384]{1,0:T(8,128)(2,1)} %copy-done.6, bf16[16,16384]{1,0:T(8,128)(2,1)} %copy-done.7, bf16[16,16384]{1,0:T(8,128)(2,1)} %copy-done.8, bf16[16,16384]{1,0:T(8,128)(2,1)} %collective-permute-done.3.refs_4_, ...), custom_call_target="tpu_custom_call" | custom-call | tf_op jit(solution)/shard_map/gather_chunks/pallas_call | solution.py:433
  (88 shorter events, 16.4 us)
Async XLA Ops:
  3.5 80.1 %collective-permute-start.10 = (bf16[4096,256]{1,0:T(8,128)(2,1)S(1)}, bf16[4096,256]{1,0:T(8,128)(2,1)}, u32[]{:S(2)}, u32[]{:S(2)}) collective-permute-start(bf16[4096,256]{1,0:T(8,128)(2,1)S(1)} %reshape.43.refs_2_.refs_4_), channel_id=1, source_target_pairs={{0,2},{1,3},{2,0},{3,1},{4,6},{5,7},{6,4},{7,5},{8,10},{9,11},{10,... | collective-permute-start | bytes 6291464 | tf_op jit(solution)/shard_map/ppermute | solution.py:18
  11.6 44.4 %collective-permute-start.21 = (bf16[2048,256]{1,0:T(8,128)(2,1)}, bf16[2048,256]{1,0:T(8,128)(2,1)}, u32[]{:S(2)}, u32[]{:S(2)}) collective-permute-start(bf16[2048,256]{1,0:T(8,128)(2,1)} %reshape.44.refs_0_), channel_id=1, source_target_pairs={{0,1},{1,0},{2,3},{3,2},{4,5},{5,4},{6,7},{7,6},{8,9},{9,8},{10,11... | collective-permute-start | bytes 3145736 | tf_op jit(solution)/shard_map/ppermute | solution.py:18
  12.9 43.3 %collective-permute-start.22 = (bf16[2048,256]{1,0:T(8,128)(2,1)}, bf16[2048,256]{1,0:T(8,128)(2,1)S(1)}, u32[]{:S(2)}, u32[]{:S(2)}) collective-permute-start(bf16[2048,256]{1,0:T(8,128)(2,1)} %reshape.42.refs_1_), channel_id=1, source_target_pairs={{0,1},{1,0},{2,3},{3,2},{4,5},{5,4},{6,7},{7,6},{8,9},{9,8},{10,11... | collective-permute-start | bytes 3145736 | tf_op jit(solution)/shard_map/ppermute | solution.py:18
  13.5 47.5 %collective-permute-start.13 = (bf16[2048,256]{1,0:T(8,128)(2,1)S(1)}, bf16[2048,256]{1,0:T(8,128)(2,1)S(1)}, u32[]{:S(2)}, u32[]{:S(2)}) collective-permute-start(bf16[2048,256]{1,0:T(8,128)(2,1)S(1)} %get-tuple-element.29), channel_id=1, source_target_pairs={{0,4},{4,0},{8,12},{12,8},{16,20},{20,16},{24,28},{28,24},{1,5},{5... | collective-permute-start | bytes 3145736 | tf_op jit(solution)/shard_map/ppermute | solution.py:18
  15.1 37.2 %collective-permute-start.7 = (s32[64,4]{0,1:T(4,128)S(1)}, s32[64,4]{0,1:T(4,128)S(1)}, u32[]{:S(2)}, u32[]{:S(2)}) collective-permute-start(s32[64,4]{0,1:T(4,128)S(1)} %copy-done.13), channel_id=1, source_target_pairs={{0,2},{1,3},{2,0},{3,1},{4,6},{5,7},{6,4},{7,5},{8,10},{9,11},{10,... | collective-permute-start | bytes 3080 | tf_op jit(solution)/shard_map/ppermute | solution.py:18
  54.6 27.3 %collective-permute-start.16 = (bf16[2048,256]{1,0:T(8,128)(2,1)S(1)}, bf16[2048,256]{1,0:T(8,128)(2,1)}, u32[]{:S(2)}, u32[]{:S(2)}) collective-permute-start(bf16[2048,256]{1,0:T(8,128)(2,1)S(1)} %get-tuple-element.28), channel_id=1, source_target_pairs={{4,12},{8,0},{12,20},{16,8},{20,28},{24,16},{5,13},{9,1},{13,21},{... | collective-permute-start | bytes 3145736 | tf_op jit(solution)/shard_map/ppermute | solution.py:234
  56.0 53.0 %collective-permute-start.23 = (bf16[4096,256]{1,0:T(8,128)(2,1)S(1)}, bf16[4096,256]{1,0:T(8,128)(2,1)S(1)}, u32[]{:S(2)}, u32[]{:S(2)}) collective-permute-start(bf16[4096,256]{1,0:T(8,128)(2,1)S(1)} %reshape.43.refs_2_.refs_4_), channel_id=1, source_target_pairs={{0,1},{1,0},{2,3},{3,2},{4,5},{5,4},{6,7},{7,6},{8,9},{9,8},{10,11... | collective-permute-start | bytes 6291464 | tf_op jit(solution)/shard_map/ppermute | solution.py:18
  56.2 28.5 %collective-permute-start.14 = (bf16[2048,256]{1,0:T(8,128)(2,1)S(1)}, bf16[2048,256]{1,0:T(8,128)(2,1)S(1)}, u32[]{:S(2)}, u32[]{:S(2)}) collective-permute-start(bf16[2048,256]{1,0:T(8,128)(2,1)S(1)} %get-tuple-element.28), channel_id=1, source_target_pairs={{0,4},{4,0},{8,12},{12,8},{16,20},{20,16},{24,28},{28,24},{1,5},{5... | collective-permute-start | bytes 3145736 | tf_op jit(solution)/shard_map/ppermute | solution.py:18
  61.0 27.3 %collective-permute-start.18 = (bf16[2048,256]{1,0:T(8,128)(2,1)}, bf16[2048,256]{1,0:T(8,128)(2,1)}, u32[]{:S(2)}, u32[]{:S(2)}) collective-permute-start(bf16[2048,256]{1,0:T(8,128)(2,1)} %reshape.44.refs_0_), channel_id=1, source_target_pairs={{0,2},{1,3},{2,0},{3,1},{4,6},{5,7},{6,4},{7,5},{8,10},{9,11},{10,... | collective-permute-start | bytes 3145736 | tf_op jit(solution)/shard_map/ppermute | solution.py:18
  82.0 27.0 %collective-permute-start.9 = (bf16[2048,256]{1,0:T(8,128)(2,1)}, bf16[2048,256]{1,0:T(8,128)(2,1)}, u32[]{:S(2)}, u32[]{:S(2)}) collective-permute-start(bf16[2048,256]{1,0:T(8,128)(2,1)} %reshape.42.refs_1_), channel_id=1, source_target_pairs={{0,2},{1,3},{2,0},{3,1},{4,6},{5,7},{6,4},{7,5},{8,10},{9,11},{10,... | collective-permute-start | bytes 3145736 | tf_op jit(solution)/shard_map/ppermute | solution.py:18
  83.6 51.4 %collective-permute-start.12 = (bf16[4096,256]{1,0:T(8,128)(2,1)}, bf16[4096,256]{1,0:T(8,128)(2,1)}, u32[]{:S(2)}, u32[]{:S(2)}) collective-permute-start(bf16[4096,256]{1,0:T(8,128)(2,1)} %collective-permute-done.10.refs_1_), channel_id=1, source_target_pairs={{0,1},{1,0},{2,3},{3,2},{4,5},{5,4},{6,7},{7,6},{8,9},{9,8},{10,11... | collective-permute-start | bytes 6291464 | tf_op jit(solution)/shard_map/ppermute | solution.py:18
  84.7 32.9 %collective-permute-start.15 = (bf16[2048,256]{1,0:T(8,128)(2,1)S(1)}, bf16[2048,256]{1,0:T(8,128)(2,1)}, u32[]{:S(2)}, u32[]{:S(2)}) collective-permute-start(bf16[2048,256]{1,0:T(8,128)(2,1)S(1)} %collective-permute-done.13.refs_5_), channel_id=1, source_target_pairs={{0,8},{8,16},{12,4},{16,24},{20,12},{28,20},{1,9},{9,17},{13,5},{1... | collective-permute-start | bytes 3145736 | tf_op jit(solution)/shard_map/ppermute | solution.py:235
  88.3 29.7 %collective-permute-start.17 = (bf16[2048,256]{1,0:T(8,128)(2,1)}, bf16[2048,256]{1,0:T(8,128)(2,1)}, u32[]{:S(2)}, u32[]{:S(2)}) collective-permute-start(bf16[2048,256]{1,0:T(8,128)(2,1)} %collective-permute-done.16), channel_id=1, source_target_pairs={{0,4},{4,0},{8,12},{12,8},{16,20},{20,16},{24,28},{28,24},{1,5},{5... | collective-permute-start | bytes 3145736 | tf_op jit(solution)/shard_map/ppermute | solution.py:18
  109.0 26.0 %collective-permute-start.19 = (bf16[2048,256]{1,0:T(8,128)(2,1)}, bf16[2048,256]{1,0:T(8,128)(2,1)}, u32[]{:S(2)}, u32[]{:S(2)}) collective-permute-start(bf16[2048,256]{1,0:T(8,128)(2,1)} %collective-permute-done.18.refs_0_), channel_id=1, source_target_pairs={{0,1},{1,0},{2,3},{3,2},{4,5},{5,4},{6,7},{7,6},{8,9},{9,8},{10,11... | collective-permute-start | bytes 3145736 | tf_op jit(solution)/shard_map/ppermute | solution.py:18
  109.0 36.0 %collective-permute-start.11 = (bf16[2048,256]{1,0:T(8,128)(2,1)}, bf16[2048,256]{1,0:T(8,128)(2,1)S(1)}, u32[]{:S(2)}, u32[]{:S(2)}) collective-permute-start(bf16[2048,256]{1,0:T(8,128)(2,1)} %collective-permute-done.9.refs_0_), channel_id=1, source_target_pairs={{0,1},{1,0},{2,3},{3,2},{4,5},{5,4},{6,7},{7,6},{8,9},{9,8},{10,11... | collective-permute-start | bytes 3145736 | tf_op jit(solution)/shard_map/ppermute | solution.py:18
  117.6 45.8 %collective-permute-start = (bf16[16,16384]{1,0:T(8,128)(2,1)}, bf16[16,16384]{1,0:T(8,128)(2,1)S(1)}, u32[]{:S(2)}, u32[]{:S(2)}) collective-permute-start(bf16[16,16384]{1,0:T(8,128)(2,1)} %get-tuple-element.15), channel_id=1, source_target_pairs={{0,4},{4,0},{8,12},{12,8},{16,20},{20,16},{24,28},{28,24},{1,5},{5... | collective-permute-start | bytes 1572872 | tf_op jit(solution)/shard_map/ppermute | solution.py:18
  118.0 47.9 %collective-permute-start.1 = (bf16[16,16384]{1,0:T(8,128)(2,1)}, bf16[16,16384]{1,0:T(8,128)(2,1)S(1)}, u32[]{:S(2)}, u32[]{:S(2)}) collective-permute-start(bf16[16,16384]{1,0:T(8,128)(2,1)} %get-tuple-element.16), channel_id=1, source_target_pairs={{0,8},{4,12},{8,0},{12,4},{16,24},{20,28},{24,16},{28,20},{1,9},{5... | collective-permute-start | bytes 1572872 | tf_op jit(solution)/shard_map/ppermute | solution.py:18
  156.1 13.0 %collective-permute-start.24 = (f32[128,768]{1,0:T(8,128)}, f32[128,768]{1,0:T(8,128)S(1)}, u32[]{:S(2)}, u32[]{:S(2)}) collective-permute-start(f32[128,768]{1,0:T(8,128)} %get-tuple-element.25), channel_id=1, source_target_pairs={{0,1},{1,0},{2,3},{3,2},{4,5},{5,4},{6,7},{7,6},{8,9},{9,8},{10,11... | collective-permute-start | bytes 1179656 | tf_op jit(solution)/shard_map/ppermute | solution.py:18
  156.2 26.2 %collective-permute-start.2 = (bf16[16,16384]{1,0:T(8,128)(2,1)}, bf16[16,16384]{1,0:T(8,128)(2,1)S(1)}, u32[]{:S(2)}, u32[]{:S(2)}) collective-permute-start(bf16[16,16384]{1,0:T(8,128)(2,1)} %get-tuple-element.17), channel_id=1, source_target_pairs={{0,12},{4,8},{8,4},{12,0},{16,28},{20,24},{24,20},{28,16},{1,13},{... | collective-permute-start | bytes 1572872 | tf_op jit(solution)/shard_map/ppermute | solution.py:18
  160.2 61.7 %collective-permute-start.4 = (bf16[16,16384]{1,0:T(8,128)(2,1)}, bf16[16,16384]{1,0:T(8,128)(2,1)S(1)}, u32[]{:S(2)}, u32[]{:S(2)}) collective-permute-start(bf16[16,16384]{1,0:T(8,128)(2,1)} %get-tuple-element.18), channel_id=1, source_target_pairs={{0,20},{4,16},{8,28},{12,24},{16,4},{20,0},{24,12},{28,8},{1,21},{... | collective-permute-start | bytes 1572872 | tf_op jit(solution)/shard_map/ppermute | solution.py:18
  163.4 58.6 %collective-permute-start.5 = (bf16[16,16384]{1,0:T(8,128)(2,1)}, bf16[16,16384]{1,0:T(8,128)(2,1)S(1)}, u32[]{:S(2)}, u32[]{:S(2)}) collective-permute-start(bf16[16,16384]{1,0:T(8,128)(2,1)} %get-tuple-element.19), channel_id=1, source_target_pairs={{0,24},{4,28},{8,16},{12,20},{16,8},{20,12},{24,0},{28,4},{1,25},{... | collective-permute-start | bytes 1572872 | tf_op jit(solution)/shard_map/ppermute | solution.py:18
  165.8 56.1 %collective-permute-start.6 = (bf16[16,16384]{1,0:T(8,128)(2,1)}, bf16[16,16384]{1,0:T(8,128)(2,1)}, u32[]{:S(2)}, u32[]{:S(2)}) collective-permute-start(bf16[16,16384]{1,0:T(8,128)(2,1)} %get-tuple-element.20), channel_id=1, source_target_pairs={{0,28},{4,24},{8,20},{12,16},{16,12},{20,8},{24,4},{28,0},{1,29},{... | collective-permute-start | bytes 1572872 | tf_op jit(solution)/shard_map/ppermute | solution.py:18
  169.1 84.1 %collective-permute-start.3 = (bf16[16,16384]{1,0:T(8,128)(2,1)}, bf16[16,16384]{1,0:T(8,128)(2,1)}, u32[]{:S(2)}, u32[]{:S(2)}) collective-permute-start(bf16[16,16384]{1,0:T(8,128)(2,1)} %shard_map.60), channel_id=1, source_target_pairs={{0,16},{4,20},{8,24},{12,28},{16,0},{20,4},{24,8},{28,12},{1,17},{... | collective-permute-start | bytes 1572872 | tf_op jit(solution)/shard_map/ppermute | solution.py:18
  182.4 74.5 %collective-permute-start.25 = (f32[64,768]{1,0:T(8,128)S(1)}, f32[64,768]{1,0:T(8,128)S(1)}, u32[]{:S(2)}, u32[]{:S(2)}) collective-permute-start(f32[64,768]{1,0:T(8,128)S(1)} %slice.39), channel_id=1, source_target_pairs={{0,2},{1,3},{2,0},{3,1},{4,6},{5,7},{6,4},{7,5},{8,10},{9,11},{10,... | collective-permute-start | bytes 589832 | tf_op jit(solution)/shard_map/ppermute | solution.py:18
  (17 other events, 633.2 us)

commit v8 on v7

--- a/solution.py
+++ b/solution.py
@@ -192,11 +192,12 @@
 
 def run_products(body, codes, arrays, loads, buffers, outs, band, row_count, flops, out_specs=None):
     width = arrays[0].shape[1]
+    held = sum(x.size * x.dtype.itemsize for x in buffers) + SLOTS * row_count * B * width * 4
     return pl.pallas_call(
         functools.partial(body, band, row_count, loads, len(arrays)),
         out_shape=outs,
         in_specs=[pl.BlockSpec(memory_space=pltpu.SMEM)]
-        + [pl.BlockSpec(memory_space=pltpu.HBM)] * len(arrays),
+        + [pl.BlockSpec(memory_space=pl.ANY)] * len(arrays),
         out_specs=out_specs
         or jax.tree.map(lambda _: pl.BlockSpec(memory_space=pltpu.VMEM), outs),
         scratch_shapes=[pltpu.VMEM(x.shape, x.dtype) for x in buffers]
@@ -205,7 +206,7 @@
             pltpu.SMEM((row_count * band + UNROLL,), jnp.int32),
             pltpu.SemaphoreType.DMA((len(loads) + 2,)),
         ],
-        compiler_params=pltpu.CompilerParams(vmem_limit_bytes=60 << 20),
+        compiler_params=pltpu.CompilerParams(vmem_limit_bytes=held + (16 << 20)),
         cost_estimate=pl.CostEstimate(
             flops=flops,
             bytes_accessed=sum(x.size * x.dtype.itemsize for x in arrays),

time: 258 us -> 258 us (level)
  local copies, waits for them, and re-layouts: 12.5 us -> 19.6 us
  Pallas kernels: 47.6 us -> 42.7 us
    unnamed x30 -> x34, local copies, waits for them, and re-layouts: 2.33 us -> 9.44 us
    pallas_call x3, Pallas kernels: 36.3 us -> 31.3 us  [run_products(): pl.pallas_call(functools.partial(body, band, row_count, loads, len(arrays...]
  transfers between devices with their start and end apart: 26 -> 26, of which waited for: 9 -> 9; matrix products, arithmetic and copies ran while one was open for 4% -> 4% of each run, Pallas kernels for 18% -> 17%
where the time goes in v8:
time: 258 us; the launch traced here: 257 us
  waiting for transfers between devices  161 us (62%)
  Pallas kernels  42.7 us (17%)
  starting transfers between devices  30.8 us (12%)
  local copies, waits for them, and re-layouts  19.6 us (8%)
    ppermute x24, waiting for transfers between devices, xor_permute(): return lax.ppermute(value, axis, [(i, i ^ bit) for i in range(count)])  142 us
    pallas_call x3, Pallas kernels, run_products(): pl.pallas_call(functools.partial(body, band, row_count, loads, len(arrays...  31.3 us
    ppermute x24, starting transfers between devices, xor_permute(): return lax.ppermute(value, axis, [(i, i ^ bit) for i in range(count)])  26 us
    ppermute x1, waiting for transfers between devices, galerkin(): moved = lax.ppermute(p_half[1], 'rows', ahead)  18.6 us
    unnamed x34, local copies, waits for them, and re-layouts  9.44 us
    pallas_call x2, Pallas kernels, pack_chunks(): pl.pallas_call(functools.partial(pack_kernel, names, capacity, pieces), o...  7.63 us
  transfers between devices with their start and end apart: 26, of which 9 were waited for; matrix products, arithmetic and copies ran while one was open for 4% of the time, Pallas kernels for 17%

profile of v8, /device:TPU:0, one launch (start us, length us, event | category | flops | bytes accessed | tf_op | source)
XLA Modules:
  0.0 257.3 jit_solution(12471139805046774558)
XLA Ops:
  0.6 2.9 %reshape.43.refs_2_.refs_4_ = bf16[4096,256]{1,0:T(8,128)(2,1)S(1)} reshape(bf16[64,16384]{1,0:T(8,128)(2,1)} %param.6) | data formatting | bytes 4194304 | tf_op jit(solution)/shard_map/reshape | solution.py:224
  3.5 3.0 %collective-permute-start.10 = (bf16[4096,256]{1,0:T(8,128)(2,1)S(1)}, bf16[4096,256]{1,0:T(8,128)(2,1)}, u32[]{:S(2)}, u32[]{:S(2)}) collective-permute-start(bf16[4096,256]{1,0:T(8,128)(2,1)S(1)} %reshape.43.refs_2_.refs_4_), channel_id=1, source_target_pairs={{0,2},{1,3},{2,0},{3,1},{4,6},{5,7},{6,4},{7,5},{8,10},{9,11},{10,... | collective-permute-start | bytes 6291464 | tf_op jit(solution)/shard_map/ppermute | solution.py:18
  6.6 2.6 %fusion.38 = (bf16[32,16384]{1,0:T(8,128)(2,1)}, bf16[32,16384]{1,0:T(8,128)(2,1)S(1)}) fusion(bf16[64,16384]{1,0:T(8,128)(2,1)} %a_hbm.3), kind=kLoop, calls=%fused_computation.101 | loop fusion | bytes 4194304 | tf_op jit(solution)/shard_map/slice | solution.py:226
  9.2 2.3 reshape.44.refs_0_
  15.8 36.6 %collective-permute-done.7 = s32[64,4]{0,1:T(4,128)S(1)} collective-permute-done((s32[64,4]{0,1:T(4,128)S(1)}, s32[64,4]{0,1:T(4,128)S(1)}, u32[]{:S(2)}, u32[]{:S(2)}) %collective-permute-start.7) | collective-permute-done | bytes 1056 | tf_op jit(solution)/shard_map/ppermute | solution.py:18
  57.2 4.7 %collective-permute-start.14 = (bf16[2048,256]{1,0:T(8,128)(2,1)S(1)}, bf16[2048,256]{1,0:T(8,128)(2,1)S(1)}, u32[]{:S(2)}, u32[]{:S(2)}) collective-permute-start(bf16[2048,256]{1,0:T(8,128)(2,1)S(1)} %get-tuple-element.28), channel_id=1, source_target_pairs={{0,4},{4,0},{8,12},{12,8},{16,20},{20,16},{24,28},{28,24},{1,5},{5... | collective-permute-start | bytes 3145736 | tf_op jit(solution)/shard_map/ppermute | solution.py:18
  63.4 18.6 %collective-permute-done.16 = bf16[2048,256]{1,0:T(8,128)(2,1)} collective-permute-done((bf16[2048,256]{1,0:T(8,128)(2,1)S(1)}, bf16[2048,256]{1,0:T(8,128)(2,1)}, u32[]{:S(2)}, u32[]{:S(2)}) %collective-permute-start.16) | collective-permute-done | bytes 1048608 | tf_op jit(solution)/shard_map/ppermute | solution.py:235
  82.0 1.6 collective-permute-start.9
  83.6 2.1 collective-permute-done.14.refs_6_
  86.7 3.5 %collective-permute-start.15 = (bf16[2048,256]{1,0:T(8,128)(2,1)S(1)}, bf16[2048,256]{1,0:T(8,128)(2,1)}, u32[]{:S(2)}, u32[]{:S(2)}) collective-permute-start(bf16[2048,256]{1,0:T(8,128)(2,1)S(1)} %collective-permute-done.13.refs_5_), channel_id=1, source_target_pairs={{0,8},{8,16},{12,4},{16,24},{20,12},{28,20},{1,9},{9,17},{13,5},{1... | collective-permute-start | bytes 3145736 | tf_op jit(solution)/shard_map/ppermute | solution.py:236
  90.3 19.7 %collective-permute-done.9.refs_0_ = bf16[2048,256]{1,0:T(8,128)(2,1)} collective-permute-done((bf16[2048,256]{1,0:T(8,128)(2,1)}, bf16[2048,256]{1,0:T(8,128)(2,1)}, u32[]{:S(2)}, u32[]{:S(2)}) %collective-permute-start.9) | collective-permute-done | bytes 1048608 | tf_op jit(solution)/shard_map/ppermute | solution.py:18
  112.6 4.4 %shard_map.59 = (bf16[16,16384]{1,0:T(8,128)(2,1)}, bf16[16,16384]{1,0:T(8,128)(2,1)}, bf16[16,16384]{1,0:T(8,128)(2,1)}, bf16[16,16384]{1,0:T(8,128)(2,1)}, bf1...) custom-call(s32[1,64]{1,0:T(1,128)} %add_bitcast_fusion.slot_ref, bf16[64,16384]{1,0:T(8,128)(2,1)} %a_hbm.3), custom_call_target="tpu_custom_call" | custom-call | tf_op jit(solution)/shard_map/pallas_call | solution.py:382
  119.0 1.6 copy-done.5
  121.8 13.7 %shard_map.61 = (f32[256,256]{1,0:T(8,128)S(1)}, bf16[4096,256]{1,0:T(8,128)(2,1)S(1)}, bf16[4096,256]{1,0:T(8,128)(2,1)S(1)}) custom-call(s32[512]{0:T(512)S(1)} %pad_add_fusion.1.codes, bf16[2048,256]{1,0:T(8,128)(2,1)} %reshape.44.refs_0_, bf16[2048,256]{1,0:T(8,128)(2,1)} %reshape.42.refs_1_, bf16[4096,256]{1,0:T(8,128)(2,1)S(1)} %reshape.43.refs_2_.refs_4_, ...), custom_call_target="tpu_custom_call" | custom-call | flops 536870912 | bytes 8388608 | tf_op jit(solution)/shard_map/pallas_call | solution.py:196
  138.3 8.4 %shard_map.62.refs_9_ = f32[256,768]{1,0:T(8,128)S(1)} custom-call(s32[513]{0:T(1024)S(1)} %pad_add_fusion.codes, bf16[2048,256]{1,0:T(8,128)(2,1)} %collective-permute-done.18.refs_0_, bf16[4096,256]{1,0:T(8,128)(2,1)} %collective-permute-done.10.refs_1_, bf16[2048,256]{1,0:T(8,128)(2,1)} %collective-permute-done.19.refs_2_, ...), custom_call_target="tpu_custom_call" | custom-call | flops 536870912 | bytes 17039360 | tf_op jit(solution)/shard_map/pallas_call | solution.py:196
  146.7 9.3 %shard_map.63 = (f32[128,768]{1,0:T(8,128)S(1)}, f32[128,768]{1,0:T(8,128)S(1)}) custom-call(s32[513]{0:T(1024)S(1)} %pad_add_fusion.codes, bf16[2048,256]{1,0:T(8,128)(2,1)} %collective-permute-done.9.refs_0_, bf16[4096,256]{1,0:T(8,128)(2,1)} %collective-permute-done.10.refs_1_, bf16[2048,256]{1,0:T(8,128)(2,1)} %collective-permute-done.11.refs_2_, ...), custom_call_target="tpu_custom_call" | custom-call | flops 536870912 | bytes 13369344 | tf_op jit(solution)/shard_map/pallas_call | solution.py:196
  156.1 3.8 %collective-permute-start.2 = (bf16[16,16384]{1,0:T(8,128)(2,1)}, bf16[16,16384]{1,0:T(8,128)(2,1)S(1)}, u32[]{:S(2)}, u32[]{:S(2)}) collective-permute-start(bf16[16,16384]{1,0:T(8,128)(2,1)} %get-tuple-element.17), channel_id=1, source_target_pairs={{0,12},{4,8},{8,4},{12,0},{16,28},{20,24},{24,20},{28,16},{1,13},{... | collective-permute-start | bytes 1572872 | tf_op jit(solution)/shard_map/ppermute | solution.py:18
  160.2 3.2 %shard_map.60 = bf16[16,16384]{1,0:T(8,128)(2,1)} custom-call(s32[1,64]{1,0:T(1,128)} %add_bitcast_fusion.slot_ref, bf16[64,16384]{1,0:T(8,128)(2,1)} %a_hbm.3), custom_call_target="tpu_custom_call" | custom-call | tf_op jit(solution)/shard_map/pallas_call | solution.py:382
  163.4 2.1 collective-permute-start.5
  165.5 3.2 %collective-permute-start.6 = (bf16[16,16384]{1,0:T(8,128)(2,1)}, bf16[16,16384]{1,0:T(8,128)(2,1)S(1)}, u32[]{:S(2)}, u32[]{:S(2)}) collective-permute-start(bf16[16,16384]{1,0:T(8,128)(2,1)} %get-tuple-element.20), channel_id=1, source_target_pairs={{0,28},{4,24},{8,20},{12,16},{16,12},{20,8},{24,4},{28,0},{1,29},{... | collective-permute-start | bytes 1572872 | tf_op jit(solution)/shard_map/ppermute | solution.py:18
  170.5 12.0 %collective-permute-done.2.refs_3_ = bf16[16,16384]{1,0:T(8,128)(2,1)S(1)} collective-permute-done((bf16[16,16384]{1,0:T(8,128)(2,1)}, bf16[16,16384]{1,0:T(8,128)(2,1)S(1)}, u32[]{:S(2)}, u32[]{:S(2)}) %collective-permute-start.2) | collective-permute-done | bytes 524320 | tf_op jit(solution)/shard_map/ppermute | solution.py:18
  183.1 38.6 %collective-permute-done.4.refs_5_ = bf16[16,16384]{1,0:T(8,128)(2,1)S(1)} collective-permute-done((bf16[16,16384]{1,0:T(8,128)(2,1)}, bf16[16,16384]{1,0:T(8,128)(2,1)S(1)}, u32[]{:S(2)}, u32[]{:S(2)}) %collective-permute-start.4) | collective-permute-done | bytes 524320 | tf_op jit(solution)/shard_map/ppermute | solution.py:18
  221.7 31.2 %collective-permute-done.3.refs_4_ = bf16[16,16384]{1,0:T(8,128)(2,1)} collective-permute-done((bf16[16,16384]{1,0:T(8,128)(2,1)}, bf16[16,16384]{1,0:T(8,128)(2,1)}, u32[]{:S(2)}, u32[]{:S(2)}) %collective-permute-start.3) | collective-permute-done | bytes 524320 | tf_op jit(solution)/shard_map/ppermute | solution.py:18
  252.8 3.7 %gather_chunks.1 = bf16[64,16384]{1,0:T(8,128)(2,1)} custom-call(s32[1]{0:T(128)} %bitcast.where, bf16[16,16384]{1,0:T(8,128)(2,1)} %get-tuple-element.14.refs_0_, bf16[16,16384]{1,0:T(8,128)(2,1)} %collective-permute-done.refs_1_, bf16[16,16384]{1,0:T(8,128)(2,1)} %collective-permute-done.1.refs_2_, bf16[16,16384]{1,0:T(8,128)(2,1)} %copy-done.10, ...), custom_call_target="tpu_custom_call" | custom-call | tf_op jit(solution)/shard_map/gather_chunks/pallas_call | solution.py:434
  (92 shorter events, 23.6 us)
Async XLA Ops:
  3.5 80.1 %collective-permute-start.10 = (bf16[4096,256]{1,0:T(8,128)(2,1)S(1)}, bf16[4096,256]{1,0:T(8,128)(2,1)}, u32[]{:S(2)}, u32[]{:S(2)}) collective-permute-start(bf16[4096,256]{1,0:T(8,128)(2,1)S(1)} %reshape.43.refs_2_.refs_4_), channel_id=1, source_target_pairs={{0,2},{1,3},{2,0},{3,1},{4,6},{5,7},{6,4},{7,5},{8,10},{9,11},{10,... | collective-permute-start | bytes 6291464 | tf_op jit(solution)/shard_map/ppermute | solution.py:18
  11.5 44.4 %collective-permute-start.21 = (bf16[2048,256]{1,0:T(8,128)(2,1)}, bf16[2048,256]{1,0:T(8,128)(2,1)}, u32[]{:S(2)}, u32[]{:S(2)}) collective-permute-start(bf16[2048,256]{1,0:T(8,128)(2,1)} %reshape.44.refs_0_), channel_id=1, source_target_pairs={{0,1},{1,0},{2,3},{3,2},{4,5},{5,4},{6,7},{7,6},{8,9},{9,8},{10,11... | collective-permute-start | bytes 3145736 | tf_op jit(solution)/shard_map/ppermute | solution.py:18
  12.9 43.3 %collective-permute-start.22 = (bf16[2048,256]{1,0:T(8,128)(2,1)}, bf16[2048,256]{1,0:T(8,128)(2,1)S(1)}, u32[]{:S(2)}, u32[]{:S(2)}) collective-permute-start(bf16[2048,256]{1,0:T(8,128)(2,1)} %reshape.42.refs_1_), channel_id=1, source_target_pairs={{0,1},{1,0},{2,3},{3,2},{4,5},{5,4},{6,7},{7,6},{8,9},{9,8},{10,11... | collective-permute-start | bytes 3145736 | tf_op jit(solution)/shard_map/ppermute | solution.py:18
  13.5 48.4 %collective-permute-start.13 = (bf16[2048,256]{1,0:T(8,128)(2,1)S(1)}, bf16[2048,256]{1,0:T(8,128)(2,1)S(1)}, u32[]{:S(2)}, u32[]{:S(2)}) collective-permute-start(bf16[2048,256]{1,0:T(8,128)(2,1)S(1)} %get-tuple-element.29), channel_id=1, source_target_pairs={{0,4},{4,0},{8,12},{12,8},{16,20},{20,16},{24,28},{28,24},{1,5},{5... | collective-permute-start | bytes 3145736 | tf_op jit(solution)/shard_map/ppermute | solution.py:18
  15.1 37.2 %collective-permute-start.7 = (s32[64,4]{0,1:T(4,128)S(1)}, s32[64,4]{0,1:T(4,128)S(1)}, u32[]{:S(2)}, u32[]{:S(2)}) collective-permute-start(s32[64,4]{0,1:T(4,128)S(1)} %copy-done.15), channel_id=1, source_target_pairs={{0,2},{1,3},{2,0},{3,1},{4,6},{5,7},{6,4},{7,5},{8,10},{9,11},{10,... | collective-permute-start | bytes 3080 | tf_op jit(solution)/shard_map/ppermute | solution.py:18
  54.6 27.3 %collective-permute-start.16 = (bf16[2048,256]{1,0:T(8,128)(2,1)S(1)}, bf16[2048,256]{1,0:T(8,128)(2,1)}, u32[]{:S(2)}, u32[]{:S(2)}) collective-permute-start(bf16[2048,256]{1,0:T(8,128)(2,1)S(1)} %get-tuple-element.28), channel_id=1, source_target_pairs={{4,12},{8,0},{12,20},{16,8},{20,28},{24,16},{5,13},{9,1},{13,21},{... | collective-permute-start | bytes 3145736 | tf_op jit(solution)/shard_map/ppermute | solution.py:235
  55.9 54.0 %collective-permute-start.23 = (bf16[4096,256]{1,0:T(8,128)(2,1)S(1)}, bf16[4096,256]{1,0:T(8,128)(2,1)S(1)}, u32[]{:S(2)}, u32[]{:S(2)}) collective-permute-start(bf16[4096,256]{1,0:T(8,128)(2,1)S(1)} %reshape.43.refs_2_.refs_4_), channel_id=1, source_target_pairs={{0,1},{1,0},{2,3},{3,2},{4,5},{5,4},{6,7},{7,6},{8,9},{9,8},{10,11... | collective-permute-start | bytes 6291464 | tf_op jit(solution)/shard_map/ppermute | solution.py:18
  57.2 28.5 %collective-permute-start.14 = (bf16[2048,256]{1,0:T(8,128)(2,1)S(1)}, bf16[2048,256]{1,0:T(8,128)(2,1)S(1)}, u32[]{:S(2)}, u32[]{:S(2)}) collective-permute-start(bf16[2048,256]{1,0:T(8,128)(2,1)S(1)} %get-tuple-element.28), channel_id=1, source_target_pairs={{0,4},{4,0},{8,12},{12,8},{16,20},{20,16},{24,28},{28,24},{1,5},{5... | collective-permute-start | bytes 3145736 | tf_op jit(solution)/shard_map/ppermute | solution.py:18
  61.9 28.4 %collective-permute-start.18 = (bf16[2048,256]{1,0:T(8,128)(2,1)}, bf16[2048,256]{1,0:T(8,128)(2,1)}, u32[]{:S(2)}, u32[]{:S(2)}) collective-permute-start(bf16[2048,256]{1,0:T(8,128)(2,1)} %reshape.44.refs_0_), channel_id=1, source_target_pairs={{0,2},{1,3},{2,0},{3,1},{4,6},{5,7},{6,4},{7,5},{8,10},{9,11},{10,... | collective-permute-start | bytes 3145736 | tf_op jit(solution)/shard_map/ppermute | solution.py:18
  82.0 28.0 %collective-permute-start.9 = (bf16[2048,256]{1,0:T(8,128)(2,1)}, bf16[2048,256]{1,0:T(8,128)(2,1)}, u32[]{:S(2)}, u32[]{:S(2)}) collective-permute-start(bf16[2048,256]{1,0:T(8,128)(2,1)} %reshape.42.refs_1_), channel_id=1, source_target_pairs={{0,2},{1,3},{2,0},{3,1},{4,6},{5,7},{6,4},{7,5},{8,10},{9,11},{10,... | collective-permute-start | bytes 3145736 | tf_op jit(solution)/shard_map/ppermute | solution.py:18
  83.6 54.7 %collective-permute-start.12 = (bf16[4096,256]{1,0:T(8,128)(2,1)}, bf16[4096,256]{1,0:T(8,128)(2,1)}, u32[]{:S(2)}, u32[]{:S(2)}) collective-permute-start(bf16[4096,256]{1,0:T(8,128)(2,1)} %collective-permute-done.10.refs_1_), channel_id=1, source_target_pairs={{0,1},{1,0},{2,3},{3,2},{4,5},{5,4},{6,7},{7,6},{8,9},{9,8},{10,11... | collective-permute-start | bytes 6291464 | tf_op jit(solution)/shard_map/ppermute | solution.py:18
  86.7 31.2 %collective-permute-start.15 = (bf16[2048,256]{1,0:T(8,128)(2,1)S(1)}, bf16[2048,256]{1,0:T(8,128)(2,1)}, u32[]{:S(2)}, u32[]{:S(2)}) collective-permute-start(bf16[2048,256]{1,0:T(8,128)(2,1)S(1)} %collective-permute-done.13.refs_5_), channel_id=1, source_target_pairs={{0,8},{8,16},{12,4},{16,24},{20,12},{28,20},{1,9},{9,17},{13,5},{1... | collective-permute-start | bytes 3145736 | tf_op jit(solution)/shard_map/ppermute | solution.py:236
  90.3 28.1 %collective-permute-start.17 = (bf16[2048,256]{1,0:T(8,128)(2,1)}, bf16[2048,256]{1,0:T(8,128)(2,1)}, u32[]{:S(2)}, u32[]{:S(2)}) collective-permute-start(bf16[2048,256]{1,0:T(8,128)(2,1)} %collective-permute-done.16), channel_id=1, source_target_pairs={{0,4},{4,0},{8,12},{12,8},{16,20},{20,16},{24,28},{28,24},{1,5},{5... | collective-permute-start | bytes 3145736 | tf_op jit(solution)/shard_map/ppermute | solution.py:18
  110.0 28.3 %collective-permute-start.19 = (bf16[2048,256]{1,0:T(8,128)(2,1)}, bf16[2048,256]{1,0:T(8,128)(2,1)}, u32[]{:S(2)}, u32[]{:S(2)}) collective-permute-start(bf16[2048,256]{1,0:T(8,128)(2,1)} %collective-permute-done.18.refs_0_), channel_id=1, source_target_pairs={{0,1},{1,0},{2,3},{3,2},{4,5},{5,4},{6,7},{7,6},{8,9},{9,8},{10,11... | collective-permute-start | bytes 3145736 | tf_op jit(solution)/shard_map/ppermute | solution.py:18
  111.4 35.3 %collective-permute-start.11 = (bf16[2048,256]{1,0:T(8,128)(2,1)}, bf16[2048,256]{1,0:T(8,128)(2,1)}, u32[]{:S(2)}, u32[]{:S(2)}) collective-permute-start(bf16[2048,256]{1,0:T(8,128)(2,1)} %collective-permute-done.9.refs_0_), channel_id=1, source_target_pairs={{0,1},{1,0},{2,3},{3,2},{4,5},{5,4},{6,7},{7,6},{8,9},{9,8},{10,11... | collective-permute-start | bytes 3145736 | tf_op jit(solution)/shard_map/ppermute | solution.py:18
  118.0 45.4 %collective-permute-start = (bf16[16,16384]{1,0:T(8,128)(2,1)}, bf16[16,16384]{1,0:T(8,128)(2,1)}, u32[]{:S(2)}, u32[]{:S(2)}) collective-permute-start(bf16[16,16384]{1,0:T(8,128)(2,1)} %get-tuple-element.15), channel_id=1, source_target_pairs={{0,4},{4,0},{8,12},{12,8},{16,20},{20,16},{24,28},{28,24},{1,5},{5... | collective-permute-start | bytes 1572872 | tf_op jit(solution)/shard_map/ppermute | solution.py:18
  118.3 47.2 %collective-permute-start.1 = (bf16[16,16384]{1,0:T(8,128)(2,1)}, bf16[16,16384]{1,0:T(8,128)(2,1)}, u32[]{:S(2)}, u32[]{:S(2)}) collective-permute-start(bf16[16,16384]{1,0:T(8,128)(2,1)} %get-tuple-element.16), channel_id=1, source_target_pairs={{0,8},{4,12},{8,0},{12,4},{16,24},{20,28},{24,16},{28,20},{1,9},{5... | collective-permute-start | bytes 1572872 | tf_op jit(solution)/shard_map/ppermute | solution.py:18
  156.0 12.7 %collective-permute-start.24 = (f32[128,768]{1,0:T(8,128)S(1)}, f32[128,768]{1,0:T(8,128)S(1)}, u32[]{:S(2)}, u32[]{:S(2)}) collective-permute-start(f32[128,768]{1,0:T(8,128)S(1)} %get-tuple-element.25), channel_id=1, source_target_pairs={{0,1},{1,0},{2,3},{3,2},{4,5},{5,4},{6,7},{7,6},{8,9},{9,8},{10,11... | collective-permute-start | bytes 1179656 | tf_op jit(solution)/shard_map/ppermute | solution.py:18
  156.1 26.4 %collective-permute-start.2 = (bf16[16,16384]{1,0:T(8,128)(2,1)}, bf16[16,16384]{1,0:T(8,128)(2,1)S(1)}, u32[]{:S(2)}, u32[]{:S(2)}) collective-permute-start(bf16[16,16384]{1,0:T(8,128)(2,1)} %get-tuple-element.17), channel_id=1, source_target_pairs={{0,12},{4,8},{8,4},{12,0},{16,28},{20,24},{24,20},{28,16},{1,13},{... | collective-permute-start | bytes 1572872 | tf_op jit(solution)/shard_map/ppermute | solution.py:18
  159.9 61.7 %collective-permute-start.4 = (bf16[16,16384]{1,0:T(8,128)(2,1)}, bf16[16,16384]{1,0:T(8,128)(2,1)S(1)}, u32[]{:S(2)}, u32[]{:S(2)}) collective-permute-start(bf16[16,16384]{1,0:T(8,128)(2,1)} %get-tuple-element.18), channel_id=1, source_target_pairs={{0,20},{4,16},{8,28},{12,24},{16,4},{20,0},{24,12},{28,8},{1,21},{... | collective-permute-start | bytes 1572872 | tf_op jit(solution)/shard_map/ppermute | solution.py:18
  163.4 58.2 %collective-permute-start.5 = (bf16[16,16384]{1,0:T(8,128)(2,1)}, bf16[16,16384]{1,0:T(8,128)(2,1)S(1)}, u32[]{:S(2)}, u32[]{:S(2)}) collective-permute-start(bf16[16,16384]{1,0:T(8,128)(2,1)} %get-tuple-element.19), channel_id=1, source_target_pairs={{0,24},{4,28},{8,16},{12,20},{16,8},{20,12},{24,0},{28,4},{1,25},{... | collective-permute-start | bytes 1572872 | tf_op jit(solution)/shard_map/ppermute | solution.py:18
  165.5 56.1 %collective-permute-start.6 = (bf16[16,16384]{1,0:T(8,128)(2,1)}, bf16[16,16384]{1,0:T(8,128)(2,1)S(1)}, u32[]{:S(2)}, u32[]{:S(2)}) collective-permute-start(bf16[16,16384]{1,0:T(8,128)(2,1)} %get-tuple-element.20), channel_id=1, source_target_pairs={{0,28},{4,24},{8,20},{12,16},{16,12},{20,8},{24,4},{28,0},{1,29},{... | collective-permute-start | bytes 1572872 | tf_op jit(solution)/shard_map/ppermute | solution.py:18
  168.7 84.1 %collective-permute-start.3 = (bf16[16,16384]{1,0:T(8,128)(2,1)}, bf16[16,16384]{1,0:T(8,128)(2,1)}, u32[]{:S(2)}, u32[]{:S(2)}) collective-permute-start(bf16[16,16384]{1,0:T(8,128)(2,1)} %shard_map.60), channel_id=1, source_target_pairs={{0,16},{4,20},{8,24},{12,28},{16,0},{20,4},{24,8},{28,12},{1,17},{... | collective-permute-start | bytes 1572872 | tf_op jit(solution)/shard_map/ppermute | solution.py:18
  182.5 74.1 %collective-permute-start.25 = (f32[64,768]{1,0:T(8,128)S(1)}, f32[64,768]{1,0:T(8,128)S(1)}, u32[]{:S(2)}, u32[]{:S(2)}) collective-permute-start(f32[64,768]{1,0:T(8,128)S(1)} %slice.39), channel_id=1, source_target_pairs={{0,2},{1,3},{2,0},{3,1},{4,6},{5,7},{6,4},{7,5},{8,10},{9,11},{10,... | collective-permute-start | bytes 589832 | tf_op jit(solution)/shard_map/ppermute | solution.py:18
  (19 other events, 421.0 us)
